TPU v7x, 256 devices: a whole 4x4x8 slice. The times are simulated.
256 devices in a mesh: robot: 2 (over x_hi), xy: 32 (over y, z), yz: 4 (over x_lo, core).
Axes of the slice: x: 4 (x_hi: 2, x_lo: 2; x = x_hi * 2 + x_lo), y: 4, z: 8, core: 2. Of those that a mesh axis runs over, the one named last changes fastest.
Arguments:
- seed_cost: bfloat16 [4, 64, 512, 512], P('robot', None, 'xy', 'yz'), may hold values from 0 to 9
- occupied: int32 [64, 512, 512], P(None, 'xy', 'yz'), may hold values from 0 to 1, as said below
- unknown: int32 [64, 512, 512], P(None, 'xy', 'yz'), may hold values from 0 to 1, as said below
Outputs:
- signed: float32 [64, 512, 512], P(('robot', 'xy'), 'yz')
Inputs may be any that keep to these rules, and one draw needn't show every extreme that they name: At least one cell is occupied. At least one cell is neither occupied nor unknown.
All inputs are finite; a program needn't handle non-finite values.
Results may differ from a plain program's by a relative error of at most 0.0003.
Values may be sent and summed in bfloat16 or wider, within the bound.
No kernel may reach another device: no remote copies, remote signals or barrier semaphores. Data moves between devices by JAX's collectives and lax.ppermute only.
A program may use at most 64 MiB of HBM per device.

v0:
```python
import jax
import jax.numpy as jnp
from jax import lax
from jax.sharding import PartitionSpec as P

penalty = 1048576.0
voxel_size = 0.2


def lower_envelope(values, along):
    extent = values.shape[along]
    block_size = min(extent, 128)
    places = jnp.arange(extent, dtype=jnp.float32)
    pieces = []
    for offset in range(0, extent, block_size):
        target = places[offset : offset + block_size]
        table = (places[:, None] - target[None, :]) ** 2
        layout = [1] * (values.ndim + 1)
        layout[along] = extent
        layout[along + 1] = block_size
        summed = jnp.expand_dims(values, along + 1) + table.reshape(layout)
        pieces.append(jnp.min(summed, axis=along))
    return jnp.concatenate(pieces, axis=along)


def seed_fields(lowest_cost, occupied, unknown):
    merged_cost = lowest_cost.astype(jnp.float32)
    outside = jnp.where(occupied == 1, merged_cost, merged_cost + penalty)
    inside = jnp.where((occupied == 1) | (unknown == 1), merged_cost + penalty, merged_cost)
    return jnp.stack([outside, inside])


def along_rows(blocks):
    return lower_envelope(blocks, 2)


def along_columns(blocks):
    return lower_envelope(blocks, 3)


def body(seed_cost, occupied, unknown):
    local_lowest = jnp.min(seed_cost, axis=0)
    merged = lax.pmin(local_lowest, "robot")
    fields = lower_envelope(seed_fields(merged, occupied, unknown), 1)
    half_depth = fields.shape[1] // lax.axis_size("robot")
    own_half = lax.dynamic_slice_in_dim(fields, lax.axis_index("robot") * half_depth, half_depth, 1)
    crossed = along_rows(lax.all_to_all(own_half, "xy", split_axis=1, concat_axis=2, tiled=True))
    settled = along_columns(lax.all_to_all(crossed, "yz", split_axis=2, concat_axis=3, tiled=True))
    return voxel_size * (jnp.sqrt(settled[0]) - jnp.sqrt(settled[1]))


def solution(mesh):
    in_specs = (P("robot", None, "xy", "yz"), P(None, "xy", "yz"), P(None, "xy", "yz"))
    out_specs = P(("robot", "xy"), "yz", None)
    return jax.shard_map(body, mesh=mesh, in_specs=in_specs, out_specs=out_specs, check_vma=False)
```

profile of v0, /device:TPU:1, one launch (start us, length us, event | category | flops | bytes accessed | tf_op | source)
XLA Modules:
  0.0 222.3 jit_solution(912114050549137717)
XLA Ops:
  6.5 0.0 copy-start.1
  6.5 0.0 all-reduce.2.cloned.1.call-start
  6.5 1.9 reduce_min.106
  8.5 0.0 all-reduce.2.cloned.1.call-update
  8.5 41.2 %all-reduce.2.cloned.1.call-done = bf16[64,16,128]{2,1,0:T(8,128)(2,1)} async-done(((bf16[64,16,128]{2,1,0:T(8,128)(2,1)}), bf16[64,16,128]{2,1,0:T(8,128)(2,1)}) %all-reduce.2.cloned.1.call-update) | async-done | bytes 262160 | tf_op jit(solution)/shard_map/pmin | solution.py:43
  49.7 0.0 copy-done.1
  49.7 1.1 fusion
  50.9 0.0 copy-done.2
  50.9 0.0 copy-done
  50.9 0.1 fusion.1
  51.0 0.1 pad_maximum_fusion
  51.1 6.0 %add_reduce_fusion.8 = f32[2,64,16,128]{3,2,1,0:T(8,128)S(1)} fusion(f32[64,64]{1,0:T(8,128)S(1)} %subtract_multiply_fusion.4, f32[2,64,16,128]{3,2,1,0:T(8,128)S(1)} %pad_maximum_fusion), kind=kLoop, calls=%fused_computation.8 | loop fusion | flops 33292288 | bytes 2113536 | tf_op jit(solution)/shard_map/reduce_min | solution.py:22
  57.2 0.8 copy.14
  58.1 9.6 %all-to-all-start = ((f32[2,32,16,128]{3,2,0,1:T(8,128)}), f32[2,32,16,128]{3,2,0,1:T(8,128)S(1)}, u32[]{:S(2)}, u32[]{:S(2)}) async-start(f32[2,32,16,128]{3,2,0,1:T(8,128)} %copy.14), calls=%async_computation | async-start | bytes 1048576 | tf_op jit(solution)/shard_map/all_to_all | solution.py:47
  67.7 0.1 subtract_multiply_fusion
  67.8 0.1 subtract_multiply_fusion.2
  67.9 13.7 %all-to-all-done = f32[2,32,16,128]{3,2,0,1:T(8,128)S(1)} async-done(((f32[2,32,16,128]{3,2,0,1:T(8,128)}), f32[2,32,16,128]{3,2,0,1:T(8,128)S(1)}, u32[]{:S(2)}, u32[]{:S(2)}) %all-to-all-start) | async-done | bytes 524320 | tf_op jit(solution)/shard_map/all_to_all | solution.py:47
  81.7 39.4 %add_reduce_fusion.7 = (f32[2,128,128]{2,1,0:T(8,128)S(1)}, f32[2,128,128]{2,1,0:T(8,128)S(1)}, f32[2,128,128]{2,1,0:T(8,128)S(1)}, f32[2,128,128]{2,1,0:T(8,128)S(1)}) fusion(f32[512,128]{1,0:T(8,128)S(1)} %get-tuple-element.18, f32[2,512,128]{2,1,0:T(8,128)S(1)} %bitcast.21, f32[512,128]{1,0:T(8,128)S(1)} %get-tuple-element.17, ...), kind=kLoop, calls=%fused_computation.7 | loop fusion | flops 134086656 | bytes 2097152 | tf_op jit(solution)/shard_map/reduce_min | solution.py:22
  121.1 0.4 copy.16
  121.6 14.2 %all_to_all.24 = f32[2,1,512,128]{3,0,1,2:T(2,128)S(1)} all-to-all(f32[2,1,512,128]{3,0,1,2:T(2,128)S(1)} %copy.16), channel_id=1, replica_groups=mesh['robot'=2,'xy'=32,'yz'=4] {'yz'}, dimensions={2} | all-to-all | bytes 1048576 | tf_op jit(solution)/shard_map/all_to_all | solution.py:48
  135.8 0.2 copy.18
  136.0 0.2 copy.19
  136.2 78.4 %add_reduce_fusion.3 = (f32[2,128,128]{2,1,0:T(8,128)S(1)}, f32[2,128,128]{2,1,0:T(8,128)S(1)}, f32[2,128,128]{2,1,0:T(8,128)S(1)}, f32[2,128,128]{2,1,0:T(8,128)S(1)}) fusion(f32[512,128]{1,0:T(8,128)S(1)} %get-tuple-element.18, f32[2,128,512]{2,1,0:T(8,128)S(1)} %copy.19, f32[512,128]{1,0:T(8,128)S(1)} %get-tuple-element.17, ...), kind=kLoop, calls=%fused_computation.3 | loop fusion | flops 134086656 | bytes 2097152 | tf_op jit(solution)/shard_map/reduce_min | solution.py:22
  214.6 0.8 fusion.4
  (16 shorter events, 0.3 us)
Async XLA Ops:
  6.5 43.2 %copy-start.1 = (s32[64,16,128]{2,1,0:T(8,128)S(1)}, s32[64,16,128]{2,1,0:T(8,128)}, u32[]{:S(2)}) copy-start(s32[64,16,128]{2,1,0:T(8,128)} %param.4) | copy-start | bytes 1572868
  6.5 43.2 %all-reduce.2.cloned.1.call-start = ((), (), s32[]{:S(2)}) async-start(), calls=%async_computation.2 | async-start | bytes 524288 | tf_op jit(solution)/shard_map/pmin | solution.py:43
  8.5 42.4 %copy-start.2 = (s32[64,16,128]{2,1,0:T(8,128)S(1)}, s32[64,16,128]{2,1,0:T(8,128)}, u32[]{:S(2)}) copy-start(s32[64,16,128]{2,1,0:T(8,128)} %param.5) | copy-start | bytes 1572868
  49.7 1.2 copy-start
  58.1 23.6 %all-to-all-start = ((f32[2,32,16,128]{3,2,0,1:T(8,128)}), f32[2,32,16,128]{3,2,0,1:T(8,128)S(1)}, u32[]{:S(2)}, u32[]{:S(2)}) async-start(f32[2,32,16,128]{3,2,0,1:T(8,128)} %copy.14), calls=%async_computation | async-start | bytes 1048576 | tf_op jit(solution)/shard_map/all_to_all | solution.py:47
Sparse Core Ops, SparseCore 0:
  9.9 39.7 all-reduce.1
where the time goes:
time: 223 us; the launch traced here: 222 us
  other arithmetic  128 us (57%)
  waiting for transfers between devices  54.9 us (25%)
  blocking collectives  14.2 us (6%)
  between operations  13.6 us (6%)
  starting transfers between devices  9.57 us (4%)
    reduce_min x3, other arithmetic, lower_envelope(): pieces.append(jnp.min(summed, axis=along))  124 us
    pmin x1, waiting for transfers between devices, body(): merged = lax.pmin(local_lowest, 'robot')  41.2 us
    all_to_all x1, blocking collectives, body(): lax.all_to_all(crossed, 'yz', split_axis=2, concat_axis=3, tiled=True)  14.2 us
    all_to_all x1, waiting for transfers between devices, body(): lax.all_to_all(own_half, 'xy', split_axis=1, concat_axis=2, tiled=True)  13.7 us
    all_to_all x1, starting transfers between devices, body(): lax.all_to_all(own_half, 'xy', split_axis=1, concat_axis=2, tiled=True)  9.57 us
  transfers between devices with their start and end apart: 2, of which 2 were waited for; matrix products, arithmetic and copies ran while one was open for 0% of the time, Pallas kernels for 0%

commit v1 on v0

v1 whole, which is shorter than its diff:
```python
import jax
import jax.numpy as jnp
from jax import lax
from jax.experimental import pallas as pl
from jax.experimental.pallas import tpu as pltpu
from jax.sharding import PartitionSpec as P

penalty = 1048576.0
voxel_size = 0.2

LANES = 128
ROWS = 8
LINE = 512
BLOCK = 32
BLOCKS = LINE // BLOCK
GROUPS = BLOCK // ROWS
FIELDS = 2
MIDDLE = 64


def depth_kernel(half_ref, mine_ref, other_ref, occupied_ref, unknown_ref, out_ref, field_ref):
    half = half_ref[0]
    depth = mine_ref.shape[0]
    own = out_ref.shape[0]

    def seed(place, _):
        source = place + half * (depth - 1 - 2 * place)
        merged = jnp.minimum(mine_ref[source], other_ref[source]).astype(jnp.float32)
        taken = occupied_ref[source] == 1
        hidden = taken | (unknown_ref[source] == 1)
        raised = merged + penalty
        field_ref[0, place] = jnp.where(taken, merged, raised)
        field_ref[1, place] = jnp.where(hidden, raised, merged)
        return 0

    lax.fori_loop(0, depth, seed, 0, unroll=4)
    groups = field_ref.shape[2] // ROWS

    def sweep(piece, _):
        field = piece // groups
        rows = pl.ds(pl.multiple_of((piece - field * groups) * ROWS, ROWS), ROWS)
        best = [None] * own
        for source in range(depth):
            value = field_ref[field, source, rows, :]
            for target in range(own):
                candidate = value + float((target - source) ** 2)
                best[target] = candidate if best[target] is None else jnp.minimum(best[target], candidate)
        for target in range(own):
            out_ref[target + half * (own - 1 - 2 * target), field, rows, :] = best[target]
        return 0

    lax.fori_loop(0, FIELDS * groups, sweep, 0)


def fill_table(table_ref):
    sublane = lax.broadcasted_iota(jnp.int32, (ROWS, LANES), 0).astype(jnp.float32)

    def step(k, _):
        base = sublane + (ROWS * (k - MIDDLE)).astype(jnp.float32)
        for p in range(ROWS):
            apart = base - float(p)
            table_ref[p, k] = apart * apart
        return 0

    lax.fori_loop(0, 2 * MIDDLE, step, 0, unroll=4)


def find_blocks(load, found_ref):
    sublane = lax.broadcasted_iota(jnp.int32, (ROWS, LANES), 0).astype(jnp.float32)
    for field in range(FIELDS):
        low = []
        for block in range(BLOCKS):
            least = load(field, block * BLOCK)
            for group in range(1, GROUPS):
                least = jnp.minimum(least, load(field, block * BLOCK + group * ROWS))
            low.append(jnp.broadcast_to(jnp.min(least, axis=0, keepdims=True), (ROWS, LANES)))
        for first in range(0, BLOCKS, ROWS):
            bound = None
            floor = []
            for block in range(BLOCKS):
                away = jnp.abs(sublane + float(first - block)) * float(BLOCK)
                far = away + float(BLOCK - 1)
                near = jnp.maximum(away - float(BLOCK - 1), 0.0)
                upper = low[block] + far * far
                bound = upper if bound is None else jnp.minimum(bound, upper)
                floor.append(low[block] + near * near)
            count = jnp.zeros((ROWS, 1), jnp.int32)
            words = [count, count]
            for block in range(BLOCKS):
                keep = jnp.min(floor[block] - bound, axis=1, keepdims=True) < 0.0
                code = lax.shift_left(jnp.full((ROWS, 1), block, jnp.int32), (count & 7) * 4)
                words[0] = words[0] | jnp.where(keep & (count < 8), code, 0)
                words[1] = words[1] | jnp.where(keep & (count >= 8), code, 0)
                count = count + jnp.where(keep, 1, 0)
            place = field * BLOCKS + first
            for which, value in enumerate((count, *words)):
                found_ref[which, place : place + ROWS, :] = jnp.broadcast_to(value, (ROWS, LANES))


def line_pass(load, load_row, store, table_ref, found_ref, list_ref, sem):
    fill_table(table_ref)
    find_blocks(load, found_ref)
    copy = pltpu.make_async_copy(found_ref, list_ref, sem)
    copy.start()
    copy.wait()

    def target(place, _):
        field = place // BLOCKS
        block = place - field * BLOCKS

        def pair(_, carry):
            low_word, high_word, best = carry
            source = low_word & 15
            low_word = lax.shift_right_logical(low_word, 4) | lax.shift_left(high_word & 15, 28)
            high_word = lax.shift_right_logical(high_word, 4)
            base = (block - source) * GROUPS + MIDDLE
            best = list(best)
            for p in range(ROWS):
                squares = {k: table_ref[p, base + k] for k in range(1 - GROUPS, GROUPS)}
                for q in range(GROUPS):
                    value = jnp.broadcast_to(load_row(field, source, q * ROWS + p), (ROWS, LANES))
                    for group in range(GROUPS):
                        best[group] = jnp.minimum(best[group], value + squares[group - q])
            return low_word, high_word, tuple(best)

        start = jnp.full((ROWS, LANES), 3e38, jnp.float32)
        state = (list_ref[1, place, 0], list_ref[2, place, 0], (start,) * GROUPS)
        best = lax.fori_loop(0, list_ref[0, place, 0], pair, state)[2]
        for group in range(GROUPS):
            store(field, block, group, best[group])
        return 0

    lax.fori_loop(0, FIELDS * BLOCKS, target, 0)


def row_kernel(in_ref, out_ref, table_ref, found_ref, list_ref, sem):
    chunk = in_ref.shape[2]
    per_block = BLOCK // chunk
    per_out = out_ref.shape[2] // BLOCK

    def load(field, at):
        return in_ref[at // chunk, field, pl.ds(at % chunk, ROWS), :]

    def load_row(field, block, at):
        return in_ref[block * per_block + at // chunk, field, pl.ds(at % chunk, 1), :]

    def store(field, block, group, value):
        piece = block // per_out
        at = pl.multiple_of((block - piece * per_out) * BLOCK, BLOCK) + group * ROWS
        out_ref[piece, field, pl.ds(at, ROWS), :] = value

    line_pass(load, load_row, store, table_ref, found_ref, list_ref, sem)


def column_kernel(in_ref, out_ref, line_ref, far_ref, table_ref, found_ref, list_ref, sem):
    pieces = in_ref.shape[0]
    for piece in range(pieces):
        for field in range(FIELDS):
            line_ref[field, piece * LANES : (piece + 1) * LANES, :] = in_ref[piece, field].T

    def load(field, at):
        return line_ref[field, pl.ds(at, ROWS), :]

    def load_row(field, block, at):
        return line_ref[field, pl.ds(pl.multiple_of(block * BLOCK, BLOCK) + at, 1), :]

    def store(field, block, group, value):
        at = pl.multiple_of(block * BLOCK, BLOCK) + group * ROWS
        far_ref[field, pl.ds(at, ROWS), :] = value

    line_pass(load, load_row, store, table_ref, found_ref, list_ref, sem)
    for piece in range(pieces):
        part = pl.ds(piece * LANES, LANES)
        signed = voxel_size * (jnp.sqrt(far_ref[0, part, :]) - jnp.sqrt(far_ref[1, part, :]))
        out_ref[:, part] = signed.T


def line_scratch():
    return [
        pltpu.VMEM((ROWS, 2 * MIDDLE, ROWS, LANES), jnp.float32),
        pltpu.VMEM((3, FIELDS * BLOCKS, LANES), jnp.int32),
        pltpu.SMEM((3, FIELDS * BLOCKS, LANES), jnp.int32),
        pltpu.SemaphoreType.DMA,
    ]


def body(seed_cost, occupied, unknown):
    depth, rows, columns = occupied.shape
    own = depth // lax.axis_size("robot")
    params = pltpu.CompilerParams(vmem_limit_bytes=32 * 2**20)
    vmem = pl.BlockSpec(memory_space=pltpu.VMEM)
    lowest = jnp.min(seed_cost, axis=0)
    other = lax.ppermute(lowest, "robot", [(0, 1), (1, 0)])
    half = lax.axis_index("robot").astype(jnp.int32).reshape(1)
    planes = pl.pallas_call(
        depth_kernel,
        out_shape=jax.ShapeDtypeStruct((own, FIELDS, rows, columns), jnp.float32),
        in_specs=[pl.BlockSpec(memory_space=pltpu.SMEM)] + [vmem] * 4,
        out_specs=vmem,
        scratch_shapes=[pltpu.VMEM((FIELDS, depth, rows, columns), jnp.float32)],
        compiler_params=params,
    )(half, lowest, other, occupied, unknown)
    crossed = lax.all_to_all(planes, "xy", split_axis=0, concat_axis=0, tiled=True)
    parts = lax.axis_size("yz")
    share = LINE // parts
    settled = pl.pallas_call(
        row_kernel,
        out_shape=jax.ShapeDtypeStruct((parts, FIELDS, share, columns), jnp.float32),
        in_specs=[vmem],
        out_specs=vmem,
        scratch_shapes=line_scratch(),
        compiler_params=params,
    )(crossed)
    turned = lax.all_to_all(settled, "yz", split_axis=0, concat_axis=0, tiled=True)
    signed = pl.pallas_call(
        column_kernel,
        out_shape=jax.ShapeDtypeStruct((share, LINE), jnp.float32),
        in_specs=[vmem],
        out_specs=vmem,
        scratch_shapes=[pltpu.VMEM((FIELDS, LINE, share), jnp.float32)] * 2 + line_scratch(),
        compiler_params=params,
    )(turned)
    return signed[None]


def solution(mesh):
    in_specs = (P("robot", None, "xy", "yz"), P(None, "xy", "yz"), P(None, "xy", "yz"))
    out_specs = P(("robot", "xy"), "yz", None)
    return jax.shard_map(body, mesh=mesh, in_specs=in_specs, out_specs=out_specs, check_vma=False)
```

time: 223 us -> 69.8 us (0.31)
  other arithmetic: 128 us -> 1.19 us
  waiting for transfers between devices: 54.9 us -> 4.99 us
  blocking collectives: 14.2 us -> 40.9 us
  Pallas kernels: 0 us -> 18 us
  between operations: 13.6 us -> 0.02 us
  starting transfers between devices: 9.57 us -> 3.65 us
    reduce_min x4 -> x1, other arithmetic: 126 us -> 1.19 us  [body(): lowest = jnp.min(seed_cost, axis=0)]
    pmin x1 -> x0, waiting for transfers between devices: 41.2 us -> none  [body(): merged = lax.pmin(local_lowest, 'robot')]
    all_to_all x1 -> x2, blocking collectives: 14.2 us -> 40.9 us  [the longest x1 24.9 us: body(): lax.all_to_all(planes, 'xy', split_axis=0, concat_axis=0, tiled=True)]
    pallas_call x0 -> x3, Pallas kernels: none -> 18 us  [the longest x1 8.31 us: body(): pl.pallas_call(row_kernel, out_shape=jax.ShapeDtypeStruct((parts, FIELDS,...]
    all_to_all x1 -> x0, waiting for transfers between devices: 13.7 us -> none  [body(): lax.all_to_all(own_half, 'xy', split_axis=1, concat_axis=2, tiled=True)]
    all_to_all x1 -> x0, starting transfers between devices: 9.57 us -> none  [body(): lax.all_to_all(own_half, 'xy', split_axis=1, concat_axis=2, tiled=True)]
    ppermute x0 -> x1, waiting for transfers between devices: none -> 4.99 us  [body(): other = lax.ppermute(lowest, 'robot', [(0, 1), (1, 0)])]
    ppermute x0 -> x1, starting transfers between devices: none -> 3.65 us  [body(): other = lax.ppermute(lowest, 'robot', [(0, 1), (1, 0)])]
  transfers between devices with their start and end apart: 2 -> 1, of which waited for: 2 -> 1; matrix products, arithmetic and copies ran while one was open for 0% -> 0% of each run, Pallas kernels for 0% -> 0%
where the time goes in v1:
time: 69.8 us
  blocking collectives  40.9 us (59%)
  Pallas kernels  18 us (26%)
  waiting for transfers between devices  4.99 us (7%)
  starting transfers between devices  3.65 us (5%)
  other arithmetic  1.19 us (2%)
  local copies, waits for them, and re-layouts  1.05 us (2%)
    all_to_all x1, blocking collectives, body(): lax.all_to_all(planes, 'xy', split_axis=0, concat_axis=0, tiled=True)  24.9 us
    all_to_all x1, blocking collectives, body(): lax.all_to_all(settled, 'yz', split_axis=0, concat_axis=0, tiled=True)  16 us
    pallas_call x1, Pallas kernels, body(): pl.pallas_call(row_kernel, out_shape=jax.ShapeDtypeStruct((parts, FIELDS,...  8.31 us
    pallas_call x1, Pallas kernels, body(): pl.pallas_call(column_kernel, out_shape=jax.ShapeDtypeStruct((share, LINE...  7.3 us
    ppermute x1, waiting for transfers between devices, body(): other = lax.ppermute(lowest, 'robot', [(0, 1), (1, 0)])  4.99 us
    ppermute x1, starting transfers between devices, body(): other = lax.ppermute(lowest, 'robot', [(0, 1), (1, 0)])  3.65 us
    pallas_call x1, Pallas kernels, body(): pl.pallas_call(depth_kernel, out_shape=jax.ShapeDtypeStruct((own, FIELDS,...  2.37 us
  transfers between devices with their start and end apart: 1, of which 1 were waited for; matrix products, arithmetic and copies ran while one was open for 0% of the time, Pallas kernels for 0%

profile of v1, /device:TPU:1, one launch (start us, length us, event | category | flops | bytes accessed | tf_op | source)
XLA Modules:
  0.0 69.8 jit_solution(11775198105418701013)
XLA Ops:
  0.0 0.0 copy-start
  0.0 1.2 %reduce_min.9.mine_ref = bf16[64,16,128]{2,1,0:T(8,128)(2,1)S(1)} reduce(bf16[2,64,16,128]{3,2,1,0:T(8,128)(2,1)} %param.3, bf16[]{:T(256)} %constant.7.clone.1), dimensions={0}, to_apply=%region_0.0 | reduce | flops 131072 | bytes 786434 | tf_op jit(solution)/shard_map/reduce_min | solution.py:192
  1.2 3.6 %collective-permute-start = (bf16[64,16,128]{2,1,0:T(8,128)(2,1)S(1)}, bf16[64,16,128]{2,1,0:T(8,128)(2,1)S(1)}, u32[]{:S(2)}, u32[]{:S(2)}) collective-permute-start(bf16[64,16,128]{2,1,0:T(8,128)(2,1)S(1)} %reduce_min.9.mine_ref), channel_id=1, source_target_pairs={{0,128},{128,0},{1,129},{129,1},{2,130},{130,2},{3,131},{131,3},{4... | collective-permute-start | bytes 786440 | tf_op jit(solution)/shard_map/ppermute | solution.py:193
  4.8 5.0 %collective-permute-done.other_ref = bf16[64,16,128]{2,1,0:T(8,128)(2,1)S(1)} collective-permute-done((bf16[64,16,128]{2,1,0:T(8,128)(2,1)S(1)}, bf16[64,16,128]{2,1,0:T(8,128)(2,1)S(1)}, u32[]{:S(2)}, u32[]{:S(2)}) %collective-permute-start) | collective-permute-done | bytes 262176 | tf_op jit(solution)/shard_map/ppermute | solution.py:193
  9.8 0.0 copy-done
  9.8 0.0 copy-start.1
  9.8 1.0 %copy-done.1 = s32[64,16,128]{2,1,0:T(8,128)S(1)} copy-done((s32[64,16,128]{2,1,0:T(8,128)S(1)}, s32[64,16,128]{2,1,0:T(8,128)}, u32[]{:S(2)}) %copy-start.1) | copy-done | bytes 524312
  10.9 2.4 %shard_map.37 = f32[32,2,16,128]{3,2,1,0:T(8,128)S(1)} custom-call(s32[1]{0:T(128)} %bitcast.half_ref, bf16[64,16,128]{2,1,0:T(8,128)(2,1)S(1)} %reduce_min.9.mine_ref, bf16[64,16,128]{2,1,0:T(8,128)(2,1)S(1)} %collective-permute-done.other_ref, s32[64,16,128]{2,1,0:T(8,128)S(1)} %copy-done, s32[64,16,128]{2,1,0:T(8,128)S(1)} %copy-done.1), custom_call_target="tpu_custom_call" | custom-call | tf_op jit(solution)/shard_map/pallas_call | solution.py:195
  13.2 24.9 %all_to_all.10.in_ref = f32[32,2,16,128]{3,2,1,0:T(8,128)S(1)} all-to-all(f32[32,2,16,128]{3,2,1,0:T(8,128)S(1)} %shard_map.37), channel_id=1, replica_groups=mesh['robot'=2,'xy'=32,'yz'=4] {'xy'}, dimensions={0} | all-to-all | bytes 1048576 | tf_op jit(solution)/shard_map/all_to_all | solution.py:203
  38.2 8.3 %shard_map.38 = f32[4,2,128,128]{3,2,1,0:T(8,128)S(1)} custom-call(f32[32,2,16,128]{3,2,1,0:T(8,128)S(1)} %all_to_all.10.in_ref), custom_call_target="tpu_custom_call" | custom-call | tf_op jit(solution)/shard_map/pallas_call | solution.py:206
  46.5 16.0 %all_to_all.11.in_ref = f32[4,2,128,128]{3,2,1,0:T(8,128)S(1)} all-to-all(f32[4,2,128,128]{3,2,1,0:T(8,128)S(1)} %shard_map.38), channel_id=1, replica_groups=mesh['robot'=2,'xy'=32,'yz'=4] {'yz'}, dimensions={0} | all-to-all | bytes 1048576 | tf_op jit(solution)/shard_map/all_to_all | solution.py:214
  62.5 7.3 %shard_map.39 = f32[128,512]{1,0:T(8,128)} custom-call(f32[4,2,128,128]{3,2,1,0:T(8,128)S(1)} %all_to_all.11.in_ref), custom_call_target="tpu_custom_call" | custom-call | tf_op jit(solution)/shard_map/pallas_call | solution.py:215
Async XLA Ops:
  0.0 9.8 %copy-start = (s32[64,16,128]{2,1,0:T(8,128)S(1)}, s32[64,16,128]{2,1,0:T(8,128)}, u32[]{:S(2)}) copy-start(s32[64,16,128]{2,1,0:T(8,128)} %occupied_ref.1) | copy-start | bytes 1572868
  1.2 8.6 %collective-permute-start = (bf16[64,16,128]{2,1,0:T(8,128)(2,1)S(1)}, bf16[64,16,128]{2,1,0:T(8,128)(2,1)S(1)}, u32[]{:S(2)}, u32[]{:S(2)}) collective-permute-start(bf16[64,16,128]{2,1,0:T(8,128)(2,1)S(1)} %reduce_min.9.mine_ref), channel_id=1, source_target_pairs={{0,128},{128,0},{1,129},{129,1},{2,130},{130,2},{3,131},{131,3},{4... | collective-permute-start | bytes 786440 | tf_op jit(solution)/shard_map/ppermute | solution.py:193
  9.8 1.0 %copy-start.1 = (s32[64,16,128]{2,1,0:T(8,128)S(1)}, s32[64,16,128]{2,1,0:T(8,128)}, u32[]{:S(2)}) copy-start(s32[64,16,128]{2,1,0:T(8,128)} %unknown_ref.1) | copy-start | bytes 1572868

commit v2 on v0

v2 whole, which is shorter than its diff:
```python
import functools

import jax
import jax.numpy as jnp
from jax import lax
from jax.experimental import pallas as pl
from jax.experimental.pallas import tpu as pltpu
from jax.sharding import PartitionSpec as P

penalty = 1048576.0
voxel_size = 0.2

LANES = 128
ROWS = 8
LINE = 512
BLOCK = 32
BLOCKS = LINE // BLOCK
GROUPS = BLOCK // ROWS
FIELDS = 2
MIDDLE = 64

STEPS = 65520.0 / 13.8629653
HALF_RANGE = 32768


def encode(value):
    code = (jnp.log(1.0 + value) * STEPS + 0.5).astype(jnp.int32)
    return (code - HALF_RANGE).astype(jnp.int16)


def decode(code):
    scaled = (code.astype(jnp.int32) + HALF_RANGE).astype(jnp.float32) * (1.0 / STEPS)
    return jnp.maximum(jnp.exp(scaled) - 1.0, 0.0)


def prepare_kernel(occupied_ref, unknown_ref, raise_ref):
    def masks(place, _):
        taken = occupied_ref[place] == 1
        hidden = taken | (unknown_ref[place] == 1)
        raise_ref[0, place] = jnp.where(taken, 0.0, penalty)
        raise_ref[1, place] = jnp.where(hidden, penalty, 0.0)
        return 0

    lax.fori_loop(0, occupied_ref.shape[0], masks, 0, unroll=4)


def depth_kernel(half_ref, mine_ref, other_ref, raise_ref, out_ref, field_ref, best_ref):
    half = half_ref[0]
    depth = mine_ref.shape[0]
    own = out_ref.shape[0]

    def seed(place, _):
        source = place + half * (depth - 1 - 2 * place)
        merged = jnp.minimum(mine_ref[source], other_ref[source]).astype(jnp.float32)
        for field in range(FIELDS):
            field_ref[field, place] = merged + raise_ref[field, source]
        return 0

    lax.fori_loop(0, depth, seed, 0, unroll=4)
    groups = field_ref.shape[2] // ROWS

    def sweep(piece, _):
        field = piece // groups
        rows = pl.ds(pl.multiple_of((piece - field * groups) * ROWS, ROWS), ROWS)
        best = [None] * own
        for source in range(depth):
            value = field_ref[field, source, rows, :]
            for target in range(own):
                candidate = value + float((target - source) ** 2)
                best[target] = candidate if best[target] is None else jnp.minimum(best[target], candidate)
        for target in range(own):
            best_ref[field, target, rows, :] = best[target]
        return 0

    lax.fori_loop(0, FIELDS * groups, sweep, 0)

    def send(target, _):
        place = target + half * (own - 1 - 2 * target)
        for field in range(FIELDS):
            out_ref[place, field] = encode(best_ref[field, target])
        return 0

    lax.fori_loop(0, own, send, 0, unroll=4)


def fill_table(table_ref):
    sublane = lax.broadcasted_iota(jnp.int32, (ROWS, LANES), 0).astype(jnp.float32)

    def squares(k, _):
        base = sublane + (ROWS * (k - MIDDLE)).astype(jnp.float32)
        for p in range(ROWS):
            apart = base - float(p)
            table_ref[p, k] = apart * apart
        return 0

    lax.fori_loop(0, 2 * MIDDLE, squares, 0, unroll=4)


def find_blocks(line_ref, kept_ref):
    sublane = lax.broadcasted_iota(jnp.int32, (ROWS, LANES), 0).astype(jnp.float32)
    low = []
    for block in range(BLOCKS):
        least = line_ref[block * BLOCK : block * BLOCK + ROWS, :]
        for group in range(1, GROUPS):
            at = block * BLOCK + group * ROWS
            least = jnp.minimum(least, line_ref[at : at + ROWS, :])
        low.append(jnp.broadcast_to(jnp.min(least, axis=0, keepdims=True), (ROWS, LANES)))
    for first in range(0, BLOCKS, ROWS):
        bound = None
        floor = []
        for block in range(BLOCKS):
            away = jnp.abs(sublane + float(first - block)) * float(BLOCK)
            far = away + float(BLOCK - 1)
            near = jnp.maximum(away - float(BLOCK - 1), 0.0)
            upper = low[block] + far * far
            bound = upper if bound is None else jnp.minimum(bound, upper)
            floor.append(low[block] + near * near)
        kept = jnp.zeros((ROWS, 1), jnp.int32)
        for block in range(BLOCKS):
            keep = jnp.min(floor[block] - bound, axis=1, keepdims=True) < 0.0
            kept = kept | jnp.where(keep, 1 << block, 0)
        for row in range(ROWS):
            kept_ref[first + row] = kept[row, 0]


def line_pass(line_ref, far_ref, table_ref, kept_ref):
    find_blocks(line_ref, kept_ref)

    def target(block, _):
        def left(carry):
            return carry[0] != 0

        def pair(carry):
            kept, best = carry
            source = 31 - lax.clz(kept)
            kept = kept ^ lax.shift_left(jnp.int32(1), source)
            base = (block - source) * GROUPS + MIDDLE
            row = pl.multiple_of(source * BLOCK, BLOCK)
            best = list(best)
            for p in range(ROWS):
                squares = {k: table_ref[p, base + k] for k in range(1 - GROUPS, GROUPS)}
                for q in range(GROUPS):
                    value = jnp.broadcast_to(line_ref[pl.ds(row + q * ROWS + p, 1), :], (ROWS, LANES))
                    for group in range(GROUPS):
                        best[group] = jnp.minimum(best[group], value + squares[group - q])
            return kept, tuple(best)

        start = jnp.full((ROWS, LANES), 3e38, jnp.float32)
        best = lax.while_loop(left, pair, (kept_ref[block], (start,) * GROUPS))[1]
        at = pl.multiple_of(block * BLOCK, BLOCK)
        for group in range(GROUPS):
            far_ref[pl.ds(at + group * ROWS, ROWS), :] = best[group]
        return 0

    lax.fori_loop(0, BLOCKS, target, 0)


def row_kernel(field, me_ref, in_ref, *rest):
    (table_ref, own_ref, *send_refs), (line_ref, far_ref, kept_ref) = rest[:-3], rest[-3:]
    if field == 0:
        fill_table(table_ref)
    chunk = in_ref.shape[2]
    for piece in range(in_ref.shape[0]):
        line_ref[piece * chunk : (piece + 1) * chunk, :] = decode(in_ref[piece, field])
    line_pass(line_ref, far_ref, table_ref, kept_ref)
    for step in range(len(send_refs) + 1):
        part = pl.ds(pl.multiple_of((me_ref[0] ^ step) * LANES, LANES), LANES)
        value = far_ref[part, :].T
        if step:
            send_refs[step - 1][...] = encode(value)
        else:
            own_ref[...] = value


def gather_lines(me_ref, own_ref, got_refs, line_ref):
    for step in range(len(got_refs) + 1):
        part = pl.ds(pl.multiple_of((me_ref[0] ^ step) * LANES, LANES), LANES)
        line_ref[part, :] = decode(got_refs[step - 1][...]) if step else own_ref[...]


def column_kernel(me_ref, table_ref, own_ref, *rest):
    got_refs, (far_ref, line_ref, kept_ref) = rest[:-3], rest[-3:]
    gather_lines(me_ref, own_ref, got_refs, line_ref)
    line_pass(line_ref, far_ref, table_ref, kept_ref)


def last_kernel(me_ref, table_ref, outside_ref, own_ref, *rest):
    got_refs, (out_ref, line_ref, far_ref, kept_ref) = rest[:-4], rest[-4:]
    gather_lines(me_ref, own_ref, got_refs, line_ref)
    line_pass(line_ref, far_ref, table_ref, kept_ref)
    for piece in range(LINE // LANES):
        part = pl.ds(piece * LANES, LANES)
        signed = voxel_size * (jnp.sqrt(outside_ref[part, :]) - jnp.sqrt(far_ref[part, :]))
        out_ref[:, part] = signed.T


def body(seed_cost, occupied, unknown):
    depth, rows, columns = occupied.shape
    own = depth // lax.axis_size("robot")
    vmem = pl.BlockSpec(memory_space=pltpu.VMEM)
    smem = pl.BlockSpec(memory_space=pltpu.SMEM)
    f32 = jnp.float32

    def call(kernel, out_shape, scratch, *args, scalar=False, work=4e6):
        in_specs = [smem if scalar and n == 0 else vmem for n in range(len(args))]
        return pl.pallas_call(
            kernel,
            out_shape=out_shape,
            in_specs=in_specs,
            out_specs=jax.tree.map(lambda _: vmem, out_shape),
            scratch_shapes=scratch,
            compiler_params=pltpu.CompilerParams(vmem_limit_bytes=16 * 2**20),
            cost_estimate=pl.CostEstimate(flops=int(work), bytes_accessed=2**20, transcendentals=0),
        )(*args)

    lowest = jnp.min(seed_cost, axis=0)
    other = lax.ppermute(lowest, "robot", [(0, 1), (1, 0)])
    raised = call(
        prepare_kernel, jax.ShapeDtypeStruct((FIELDS, depth, rows, columns), f32), [], occupied, unknown
    )
    half = lax.axis_index("robot").astype(jnp.int32).reshape(1)
    planes = call(
        depth_kernel,
        jax.ShapeDtypeStruct((own, FIELDS, rows, columns), jnp.int16),
        [pltpu.VMEM((FIELDS, depth, rows, columns), f32), pltpu.VMEM((FIELDS, own, rows, columns), f32)],
        half,
        lowest,
        other,
        raised,
        scalar=True,
    )
    crossed = lax.all_to_all(planes, "xy", split_axis=0, concat_axis=0, tiled=True)

    parts = lax.axis_size("yz")
    share = LINE // parts
    me = lax.axis_index("yz").astype(jnp.int32).reshape(1)
    line = pltpu.VMEM((LINE, LANES), f32)
    kept = pltpu.SMEM((BLOCKS,), jnp.int32)
    shapes = (jax.ShapeDtypeStruct((columns, share), f32),)
    shapes += (jax.ShapeDtypeStruct((columns, share), jnp.int16),) * (parts - 1)
    squares = jax.ShapeDtypeStruct((ROWS, 2 * MIDDLE, ROWS, LANES), f32)
    scratch = [line, line, kept]
    row_calls = [functools.partial(row_kernel, field) for field in range(FIELDS)]
    table, *first = call(row_calls[0], (squares, *shapes), scratch, me, crossed, scalar=True)
    second = call(row_calls[1], shapes, scratch, me, crossed, table, scalar=True)
    settled = []
    for made in (first, second):
        got = [
            lax.ppermute(made[step], "yz", [(i, i ^ step) for i in range(parts)]) for step in range(1, parts)
        ]
        settled.append((made[0], *got))
    outside = call(
        column_kernel, jax.ShapeDtypeStruct((LINE, share), f32), [line, kept], me, table, *settled[0], scalar=True
    )
    signed = call(
        last_kernel,
        jax.ShapeDtypeStruct((share, LINE), f32),
        [line, line, kept],
        me,
        table,
        outside,
        *settled[1],
        scalar=True,
    )
    return signed[None]


def solution(mesh):
    in_specs = (P("robot", None, "xy", "yz"), P(None, "xy", "yz"), P(None, "xy", "yz"))
    out_specs = P(("robot", "xy"), "yz", None)
    return jax.shard_map(body, mesh=mesh, in_specs=in_specs, out_specs=out_specs, check_vma=False)
```

time: 223 us -> 57.4 us (0.26)
  other arithmetic: 128 us -> 1.13 us
  waiting for transfers between devices: 54.9 us -> 13.3 us
  starting transfers between devices: 9.57 us -> 25.4 us
  Pallas kernels: 0 us -> 15.7 us
  blocking collectives: 14.2 us -> 0 us
  between operations: 13.6 us -> 0.07 us
    reduce_min x4 -> x1, other arithmetic: 126 us -> 1.13 us  [body(): lowest = jnp.min(seed_cost, axis=0)]
    pmin x1 -> x0, waiting for transfers between devices: 41.2 us -> none  [body(): merged = lax.pmin(local_lowest, 'robot')]
    pallas_call x0 -> x6, Pallas kernels: none -> 15.7 us  [call(): pl.pallas_call(kernel, out_shape=out_shape, in_specs=in_specs, out_specs=...]
    all_to_all x1 -> x0, blocking collectives: 14.2 us -> none  [body(): lax.all_to_all(crossed, 'yz', split_axis=2, concat_axis=3, tiled=True)]
    ppermute x0 -> x7, starting transfers between devices: none -> 13.2 us  [the longest x6 9.59 us: body(): lax.ppermute(made[step], 'yz', [(i, i ^ step) for i in range(parts)])]
    all_to_all x1, waiting for transfers between devices: 13.7 us -> 9.65 us  [body(): lax.all_to_all(planes, 'xy', split_axis=0, concat_axis=0, tiled=True)]
    ppermute x0 -> x7, waiting for transfers between devices: none -> 3.63 us  [the longest x1 2.75 us: body(): other = lax.ppermute(lowest, 'robot', [(0, 1), (1, 0)])]
    all_to_all x1, starting transfers between devices: 9.57 us -> 12.2 us  [body(): lax.all_to_all(planes, 'xy', split_axis=0, concat_axis=0, tiled=True)]
  transfers between devices with their start and end apart: 2 -> 8, of which waited for: 2 -> 3; matrix products, arithmetic and copies ran while one was open for 0% -> 0% of each run, Pallas kernels for 0% -> 9%
where the time goes in v2:
time: 57.4 us; the launch traced here: 57.7 us
  starting transfers between devices  25.4 us (44%)
  Pallas kernels  15.7 us (27%)
  waiting for transfers between devices  13.3 us (23%)
  local copies, waits for them, and re-layouts  2.08 us (4%)
  other arithmetic  1.13 us (2%)
    pallas_call x6, Pallas kernels, call(): pl.pallas_call(kernel, out_shape=out_shape, in_specs=in_specs, out_specs=...  15.7 us
    all_to_all x1, starting transfers between devices, body(): lax.all_to_all(planes, 'xy', split_axis=0, concat_axis=0, tiled=True)  12.2 us
    all_to_all x1, waiting for transfers between devices, body(): lax.all_to_all(planes, 'xy', split_axis=0, concat_axis=0, tiled=True)  9.65 us
    ppermute x6, starting transfers between devices, body(): lax.ppermute(made[step], 'yz', [(i, i ^ step) for i in range(parts)])  9.59 us
    ppermute x1, starting transfers between devices, body(): other = lax.ppermute(lowest, 'robot', [(0, 1), (1, 0)])  3.65 us
    ppermute x1, waiting for transfers between devices, body(): other = lax.ppermute(lowest, 'robot', [(0, 1), (1, 0)])  2.75 us
    unnamed x4, local copies, waits for them, and re-layouts  2.08 us
  transfers between devices with their start and end apart: 8, of which 3 were waited for; matrix products, arithmetic and copies ran while one was open for 0% of the time, Pallas kernels for 9%

profile of v2, /device:TPU:1, one launch (start us, length us, event | category | flops | bytes accessed | tf_op | source)
XLA Modules:
  0.0 57.7 jit_solution(2567605283778653675)
XLA Ops:
  0.0 1.1 %reduce_min.9.mine_ref = bf16[64,16,128]{2,1,0:T(8,128)(2,1)S(1)} reduce(bf16[2,64,16,128]{3,2,1,0:T(8,128)(2,1)} %param.3, bf16[]{:T(256)} %constant.11.clone.1), dimensions={0}, to_apply=%region_0.0 | reduce | flops 131072 | bytes 786434 | tf_op jit(solution)/shard_map/reduce_min | solution.py:216
  1.1 3.6 %collective-permute-start = (bf16[64,16,128]{2,1,0:T(8,128)(2,1)S(1)}, bf16[64,16,128]{2,1,0:T(8,128)(2,1)S(1)}, u32[]{:S(2)}, u32[]{:S(2)}) collective-permute-start(bf16[64,16,128]{2,1,0:T(8,128)(2,1)S(1)} %reduce_min.9.mine_ref), channel_id=1, source_target_pairs={{0,128},{128,0},{1,129},{129,1},{2,130},{130,2},{3,131},{131,3},{4... | collective-permute-start | bytes 786440 | tf_op jit(solution)/shard_map/ppermute | solution.py:217
  4.8 1.0 %copy-done = s32[64,16,128]{2,1,0:T(8,128)S(1)} copy-done((s32[64,16,128]{2,1,0:T(8,128)S(1)}, s32[64,16,128]{2,1,0:T(8,128)}, u32[]{:S(2)}) %copy-start) | copy-done | bytes 524312
  5.8 1.0 %copy-done.1 = s32[64,16,128]{2,1,0:T(8,128)S(1)} copy-done((s32[64,16,128]{2,1,0:T(8,128)S(1)}, s32[64,16,128]{2,1,0:T(8,128)}, u32[]{:S(2)}) %copy-start.1) | copy-done | bytes 524312
  6.9 0.1 shard_map.37.raise_ref
  7.0 2.8 %collective-permute-done.other_ref = bf16[64,16,128]{2,1,0:T(8,128)(2,1)S(1)} collective-permute-done((bf16[64,16,128]{2,1,0:T(8,128)(2,1)S(1)}, bf16[64,16,128]{2,1,0:T(8,128)(2,1)S(1)}, u32[]{:S(2)}, u32[]{:S(2)}) %collective-permute-start) | collective-permute-done | bytes 262176 | tf_op jit(solution)/shard_map/ppermute | solution.py:217
  9.8 3.5 %shard_map.38 = s16[32,2,16,128]{3,2,1,0:T(8,128)(2,1)} custom-call(s32[1]{0:T(128)} %bitcast.1.half_ref, bf16[64,16,128]{2,1,0:T(8,128)(2,1)S(1)} %reduce_min.9.mine_ref, bf16[64,16,128]{2,1,0:T(8,128)(2,1)S(1)} %collective-permute-done.other_ref, f32[2,64,16,128]{3,2,1,0:T(8,128)S(1)} %shard_map.37.raise_ref), custom_call_target="tpu_custom_call" | custom-call | flops 4000000 | bytes 1048576 | tf_op jit(solution)/shard_map/pallas_call | solution.py:206
  13.3 12.2 %all-to-all-start = ((s16[32,2,16,128]{3,2,1,0:T(8,128)(2,1)}), s16[32,2,16,128]{3,2,1,0:T(8,128)(2,1)S(1)}, u32[]{:S(2)}, u32[]{:S(2)}) async-start(s16[32,2,16,128]{3,2,1,0:T(8,128)(2,1)} %shard_map.38), calls=%async_computation | async-start | bytes 524288 | tf_op jit(solution)/shard_map/all_to_all | solution.py:232
  25.5 9.7 %all-to-all-done.in_ref = s16[32,2,16,128]{3,2,1,0:T(8,128)(2,1)S(1)} async-done(((s16[32,2,16,128]{3,2,1,0:T(8,128)(2,1)}), s16[32,2,16,128]{3,2,1,0:T(8,128)(2,1)S(1)}, u32[]{:S(2)}, u32[]{:S(2)}) %all-to-all-start) | async-done | bytes 262176 | tf_op jit(solution)/shard_map/all_to_all | solution.py:232
  35.1 3.6 %shard_map.39 = (f32[8,128,8,128]{3,2,1,0:T(8,128)S(1)}, f32[128,128]{1,0:T(8,128)S(1)}, s16[128,128]{1,0:T(8,128)(2,1)S(1)}, s16[128,128]{1,0:T(8,128)(2,1)S(1)}, s16[128,128]{1,0:T(8,128)(2,1)S(1)}) custom-call(s32[1]{0:T(128)} %bitcast.me_ref, s16[32,2,16,128]{3,2,1,0:T(8,128)(2,1)S(1)} %all-to-all-done.in_ref), custom_call_target="tpu_custom_call" | custom-call | flops 4000000 | bytes 1048576 | tf_op jit(solution)/shard_map/pallas_call | solution.py:206
  38.7 4.8 %collective-permute-start.1 = (s16[128,128]{1,0:T(8,128)(2,1)S(1)}, s16[128,128]{1,0:T(8,128)(2,1)S(1)}, u32[]{:S(2)}, u32[]{:S(2)}) collective-permute-start(s16[128,128]{1,0:T(8,128)(2,1)S(1)} %get-tuple-element.16), channel_id=1, source_target_pairs={{0,1},{1,0},{2,3},{3,2},{4,5},{5,4},{6,7},{7,6},{8,9},{9,8},{10,11... | collective-permute-start | bytes 98312 | tf_op jit(solution)/shard_map/ppermute | solution.py:249
  43.6 2.4 %collective-permute-start.2 = (s16[128,128]{1,0:T(8,128)(2,1)S(1)}, s16[128,128]{1,0:T(8,128)(2,1)S(1)}, u32[]{:S(2)}, u32[]{:S(2)}) collective-permute-start(s16[128,128]{1,0:T(8,128)(2,1)S(1)} %get-tuple-element.17), channel_id=1, source_target_pairs={{0,2},{1,3},{2,0},{3,1},{4,6},{5,7},{6,4},{7,5},{8,10},{9,11},{10,... | collective-permute-start | bytes 98312 | tf_op jit(solution)/shard_map/ppermute | solution.py:249
  46.0 0.1 collective-permute-start.3
  46.1 2.7 %shard_map.41 = (f32[128,128]{1,0:T(8,128)S(1)}, s16[128,128]{1,0:T(8,128)(2,1)S(1)}, s16[128,128]{1,0:T(8,128)(2,1)S(1)}, s16[128,128]{1,0:T(8,128)(2,1)S(1)}) custom-call(s32[1]{0:T(128)} %bitcast.me_ref, s16[32,2,16,128]{3,2,1,0:T(8,128)(2,1)S(1)} %all-to-all-done.in_ref, f32[8,128,8,128]{3,2,1,0:T(8,128)S(1)} %get-tuple-element.14.table_ref.rest_0_), custom_call_target="tpu_custom_call" | custom-call | flops 4000000 | bytes 1048576 | tf_op jit(solution)/shard_map/pallas_call | solution.py:206
  48.8 0.2 collective-permute-start.4
  49.0 1.6 %collective-permute-start.5 = (s16[128,128]{1,0:T(8,128)(2,1)S(1)}, s16[128,128]{1,0:T(8,128)(2,1)S(1)}, u32[]{:S(2)}, u32[]{:S(2)}) collective-permute-start(s16[128,128]{1,0:T(8,128)(2,1)S(1)} %get-tuple-element.21), channel_id=1, source_target_pairs={{0,2},{1,3},{2,0},{3,1},{4,6},{5,7},{6,4},{7,5},{8,10},{9,11},{10,... | collective-permute-start | bytes 98312 | tf_op jit(solution)/shard_map/ppermute | solution.py:249
  50.6 0.0 collective-permute-done.1.rest_0_
  50.6 0.5 collective-permute-start.6
  51.0 0.0 collective-permute-done.2.rest_1_
  51.0 0.0 collective-permute-done.3.rest_2_
  51.0 2.6 %shard_map.40.outside_ref = f32[512,128]{1,0:T(8,128)S(1)} custom-call(s32[1]{0:T(128)} %bitcast.me_ref, f32[8,128,8,128]{3,2,1,0:T(8,128)S(1)} %get-tuple-element.14.table_ref.rest_0_, f32[128,128]{1,0:T(8,128)S(1)} %get-tuple-element.15.own_ref, s16[128,128]{1,0:T(8,128)(2,1)S(1)} %collective-permute-done.1.rest_0_, ...), custom_call_target="tpu_custom_call" | custom-call | flops 4000000 | bytes 1048576 | tf_op jit(solution)/shard_map/pallas_call | solution.py:206
  53.6 0.0 collective-permute-done.4.rest_0_
  53.7 0.9 %collective-permute-done.6.rest_2_ = s16[128,128]{1,0:T(8,128)(2,1)S(1)} collective-permute-done((s16[128,128]{1,0:T(8,128)(2,1)S(1)}, s16[128,128]{1,0:T(8,128)(2,1)S(1)}, u32[]{:S(2)}, u32[]{:S(2)}) %collective-permute-start.6) | collective-permute-done | bytes 32800 | tf_op jit(solution)/shard_map/ppermute | solution.py:249
  54.5 3.2 %shard_map.42 = f32[128,512]{1,0:T(8,128)} custom-call(s32[1]{0:T(128)} %bitcast.me_ref, f32[8,128,8,128]{3,2,1,0:T(8,128)S(1)} %get-tuple-element.14.table_ref.rest_0_, f32[512,128]{1,0:T(8,128)S(1)} %shard_map.40.outside_ref, f32[128,128]{1,0:T(8,128)S(1)} %get-tuple-element.19.own_ref, s16[128,128]{1,0:T(8,128)(2,1)S(1)} %collective-permute-done.4.rest_0_, ...), custom_call_target="tpu_custom_call" | custom-call | flops 4000000 | bytes 1048576 | tf_op jit(solution)/shard_map/pallas_call | solution.py:206
  (3 shorter events, 0.0 us)
Async XLA Ops:
  1.1 8.6 %collective-permute-start = (bf16[64,16,128]{2,1,0:T(8,128)(2,1)S(1)}, bf16[64,16,128]{2,1,0:T(8,128)(2,1)S(1)}, u32[]{:S(2)}, u32[]{:S(2)}) collective-permute-start(bf16[64,16,128]{2,1,0:T(8,128)(2,1)S(1)} %reduce_min.9.mine_ref), channel_id=1, source_target_pairs={{0,128},{128,0},{1,129},{129,1},{2,130},{130,2},{3,131},{131,3},{4... | collective-permute-start | bytes 786440 | tf_op jit(solution)/shard_map/ppermute | solution.py:217
  4.8 1.0 %copy-start = (s32[64,16,128]{2,1,0:T(8,128)S(1)}, s32[64,16,128]{2,1,0:T(8,128)}, u32[]{:S(2)}) copy-start(s32[64,16,128]{2,1,0:T(8,128)} %occupied_ref.1) | copy-start | bytes 1572868
  5.8 1.0 %copy-start.1 = (s32[64,16,128]{2,1,0:T(8,128)S(1)}, s32[64,16,128]{2,1,0:T(8,128)}, u32[]{:S(2)}) copy-start(s32[64,16,128]{2,1,0:T(8,128)} %unknown_ref.1) | copy-start | bytes 1572868
  13.3 21.8 %all-to-all-start = ((s16[32,2,16,128]{3,2,1,0:T(8,128)(2,1)}), s16[32,2,16,128]{3,2,1,0:T(8,128)(2,1)S(1)}, u32[]{:S(2)}, u32[]{:S(2)}) async-start(s16[32,2,16,128]{3,2,1,0:T(8,128)(2,1)} %shard_map.38), calls=%async_computation | async-start | bytes 524288 | tf_op jit(solution)/shard_map/all_to_all | solution.py:232
  38.7 11.8 %collective-permute-start.1 = (s16[128,128]{1,0:T(8,128)(2,1)S(1)}, s16[128,128]{1,0:T(8,128)(2,1)S(1)}, u32[]{:S(2)}, u32[]{:S(2)}) collective-permute-start(s16[128,128]{1,0:T(8,128)(2,1)S(1)} %get-tuple-element.16), channel_id=1, source_target_pairs={{0,1},{1,0},{2,3},{3,2},{4,5},{5,4},{6,7},{7,6},{8,9},{9,8},{10,11... | collective-permute-start | bytes 98312 | tf_op jit(solution)/shard_map/ppermute | solution.py:249
  43.6 7.5 %collective-permute-start.2 = (s16[128,128]{1,0:T(8,128)(2,1)S(1)}, s16[128,128]{1,0:T(8,128)(2,1)S(1)}, u32[]{:S(2)}, u32[]{:S(2)}) collective-permute-start(s16[128,128]{1,0:T(8,128)(2,1)S(1)} %get-tuple-element.17), channel_id=1, source_target_pairs={{0,2},{1,3},{2,0},{3,1},{4,6},{5,7},{6,4},{7,5},{8,10},{9,11},{10,... | collective-permute-start | bytes 98312 | tf_op jit(solution)/shard_map/ppermute | solution.py:249
  46.0 5.0 %collective-permute-start.3 = (s16[128,128]{1,0:T(8,128)(2,1)S(1)}, s16[128,128]{1,0:T(8,128)(2,1)S(1)}, u32[]{:S(2)}, u32[]{:S(2)}) collective-permute-start(s16[128,128]{1,0:T(8,128)(2,1)S(1)} %get-tuple-element.18), channel_id=1, source_target_pairs={{0,3},{1,2},{2,1},{3,0},{4,7},{5,6},{6,5},{7,4},{8,11},{9,10},{10,... | collective-permute-start | bytes 98312 | tf_op jit(solution)/shard_map/ppermute | solution.py:249
  48.8 4.9 %collective-permute-start.4 = (s16[128,128]{1,0:T(8,128)(2,1)S(1)}, s16[128,128]{1,0:T(8,128)(2,1)S(1)}, u32[]{:S(2)}, u32[]{:S(2)}) collective-permute-start(s16[128,128]{1,0:T(8,128)(2,1)S(1)} %get-tuple-element.20), channel_id=1, source_target_pairs={{0,1},{1,0},{2,3},{3,2},{4,5},{5,4},{6,7},{7,6},{8,9},{9,8},{10,11... | collective-permute-start | bytes 98312 | tf_op jit(solution)/shard_map/ppermute | solution.py:249
  49.0 4.7 %collective-permute-start.5 = (s16[128,128]{1,0:T(8,128)(2,1)S(1)}, s16[128,128]{1,0:T(8,128)(2,1)S(1)}, u32[]{:S(2)}, u32[]{:S(2)}) collective-permute-start(s16[128,128]{1,0:T(8,128)(2,1)S(1)} %get-tuple-element.21), channel_id=1, source_target_pairs={{0,2},{1,3},{2,0},{3,1},{4,6},{5,7},{6,4},{7,5},{8,10},{9,11},{10,... | collective-permute-start | bytes 98312 | tf_op jit(solution)/shard_map/ppermute | solution.py:249
  50.6 4.0 %collective-permute-start.6 = (s16[128,128]{1,0:T(8,128)(2,1)S(1)}, s16[128,128]{1,0:T(8,128)(2,1)S(1)}, u32[]{:S(2)}, u32[]{:S(2)}) collective-permute-start(s16[128,128]{1,0:T(8,128)(2,1)S(1)} %get-tuple-element.22), channel_id=1, source_target_pairs={{0,3},{1,2},{2,1},{3,0},{4,7},{5,6},{6,5},{7,4},{8,11},{9,10},{10,... | collective-permute-start | bytes 98312 | tf_op jit(solution)/shard_map/ppermute | solution.py:249

commit v3 on v2

--- a/solution.py
+++ b/solution.py
@@ -17,7 +17,6 @@
 BLOCKS = LINE // BLOCK
 GROUPS = BLOCK // ROWS
 FIELDS = 2
-MIDDLE = 64
 
 STEPS = 65520.0 / 13.8629653
 HALF_RANGE = 32768
@@ -44,8 +43,8 @@
     lax.fori_loop(0, occupied_ref.shape[0], masks, 0, unroll=4)
 
 
-def depth_kernel(half_ref, mine_ref, other_ref, raise_ref, out_ref, field_ref, best_ref):
-    half = half_ref[0]
+def depth_kernel(place_ref, mine_ref, other_ref, raise_ref, out_ref, field_ref, best_ref):
+    half = place_ref[0]
     depth = mine_ref.shape[0]
     own = out_ref.shape[0]
 
@@ -83,19 +82,6 @@
     lax.fori_loop(0, own, send, 0, unroll=4)
 
 
-def fill_table(table_ref):
-    sublane = lax.broadcasted_iota(jnp.int32, (ROWS, LANES), 0).astype(jnp.float32)
-
-    def squares(k, _):
-        base = sublane + (ROWS * (k - MIDDLE)).astype(jnp.float32)
-        for p in range(ROWS):
-            apart = base - float(p)
-            table_ref[p, k] = apart * apart
-        return 0
-
-    lax.fori_loop(0, 2 * MIDDLE, squares, 0, unroll=4)
-
-
 def find_blocks(line_ref, kept_ref):
     sublane = lax.broadcasted_iota(jnp.int32, (ROWS, LANES), 0).astype(jnp.float32)
     low = []
@@ -106,14 +92,13 @@
             least = jnp.minimum(least, line_ref[at : at + ROWS, :])
         low.append(jnp.broadcast_to(jnp.min(least, axis=0, keepdims=True), (ROWS, LANES)))
     for first in range(0, BLOCKS, ROWS):
-        bound = None
+        bound = jnp.full((ROWS, LANES), penalty, jnp.float32)
         floor = []
         for block in range(BLOCKS):
             away = jnp.abs(sublane + float(first - block)) * float(BLOCK)
             far = away + float(BLOCK - 1)
             near = jnp.maximum(away - float(BLOCK - 1), 0.0)
-            upper = low[block] + far * far
-            bound = upper if bound is None else jnp.minimum(bound, upper)
+            bound = jnp.minimum(bound, low[block] + far * far)
             floor.append(low[block] + near * near)
         kept = jnp.zeros((ROWS, 1), jnp.int32)
         for block in range(BLOCKS):
@@ -124,30 +109,35 @@
 
 
 def line_pass(line_ref, far_ref, table_ref, kept_ref):
+    sublane = lax.broadcasted_iota(jnp.int32, (ROWS, LANES), 0).astype(jnp.float32)
+    for at in range(0, 2 * LINE, ROWS):
+        apart = sublane + float(at - LINE)
+        table_ref[at : at + ROWS, :] = apart * apart
     find_blocks(line_ref, kept_ref)
 
     def target(block, _):
+        at = pl.multiple_of(block * BLOCK, BLOCK)
+
         def left(carry):
             return carry[0] != 0
 
         def pair(carry):
-            kept, best = carry
-            source = 31 - lax.clz(kept)
+            kept, source, best = carry
+            base = pl.multiple_of((block - source) * BLOCK + LINE, BLOCK)
+            row = pl.multiple_of(source * BLOCK, BLOCK)
             kept = kept ^ lax.shift_left(jnp.int32(1), source)
-            base = (block - source) * GROUPS + MIDDLE
-            row = pl.multiple_of(source * BLOCK, BLOCK)
             best = list(best)
             for p in range(ROWS):
-                squares = {k: table_ref[p, base + k] for k in range(1 - GROUPS, GROUPS)}
+                squares = {k: table_ref[pl.ds(base + (k * ROWS - p), ROWS), :] for k in range(1 - GROUPS, GROUPS)}
                 for q in range(GROUPS):
                     value = jnp.broadcast_to(line_ref[pl.ds(row + q * ROWS + p, 1), :], (ROWS, LANES))
                     for group in range(GROUPS):
                         best[group] = jnp.minimum(best[group], value + squares[group - q])
-            return kept, tuple(best)
-
-        start = jnp.full((ROWS, LANES), 3e38, jnp.float32)
-        best = lax.while_loop(left, pair, (kept_ref[block], (start,) * GROUPS))[1]
-        at = pl.multiple_of(block * BLOCK, BLOCK)
+            return kept, 31 - lax.clz(kept), tuple(best)
+
+        kept = kept_ref[block]
+        start = tuple(line_ref[pl.ds(at + group * ROWS, ROWS), :] for group in range(GROUPS))
+        best = lax.while_loop(left, pair, (kept, 31 - lax.clz(kept), start))[2]
         for group in range(GROUPS):
             far_ref[pl.ds(at + group * ROWS, ROWS), :] = best[group]
         return 0
@@ -155,16 +145,14 @@
     lax.fori_loop(0, BLOCKS, target, 0)
 
 
-def row_kernel(field, me_ref, in_ref, *rest):
-    (table_ref, own_ref, *send_refs), (line_ref, far_ref, kept_ref) = rest[:-3], rest[-3:]
-    if field == 0:
-        fill_table(table_ref)
+def row_kernel(field, place_ref, in_ref, own_ref, *rest):
+    send_refs, (line_ref, far_ref, table_ref, kept_ref) = rest[:-4], rest[-4:]
     chunk = in_ref.shape[2]
     for piece in range(in_ref.shape[0]):
         line_ref[piece * chunk : (piece + 1) * chunk, :] = decode(in_ref[piece, field])
     line_pass(line_ref, far_ref, table_ref, kept_ref)
     for step in range(len(send_refs) + 1):
-        part = pl.ds(pl.multiple_of((me_ref[0] ^ step) * LANES, LANES), LANES)
+        part = pl.ds(pl.multiple_of((place_ref[1] ^ step) * LANES, LANES), LANES)
         value = far_ref[part, :].T
         if step:
             send_refs[step - 1][...] = encode(value)
@@ -172,21 +160,21 @@
             own_ref[...] = value
 
 
-def gather_lines(me_ref, own_ref, got_refs, line_ref):
+def gather_lines(place_ref, own_ref, got_refs, line_ref):
     for step in range(len(got_refs) + 1):
-        part = pl.ds(pl.multiple_of((me_ref[0] ^ step) * LANES, LANES), LANES)
+        part = pl.ds(pl.multiple_of((place_ref[1] ^ step) * LANES, LANES), LANES)
         line_ref[part, :] = decode(got_refs[step - 1][...]) if step else own_ref[...]
 
 
-def column_kernel(me_ref, table_ref, own_ref, *rest):
-    got_refs, (far_ref, line_ref, kept_ref) = rest[:-3], rest[-3:]
-    gather_lines(me_ref, own_ref, got_refs, line_ref)
+def column_kernel(place_ref, own_ref, *rest):
+    got_refs, (far_ref, line_ref, table_ref, kept_ref) = rest[:-4], rest[-4:]
+    gather_lines(place_ref, own_ref, got_refs, line_ref)
     line_pass(line_ref, far_ref, table_ref, kept_ref)
 
 
-def last_kernel(me_ref, table_ref, outside_ref, own_ref, *rest):
-    got_refs, (out_ref, line_ref, far_ref, kept_ref) = rest[:-4], rest[-4:]
-    gather_lines(me_ref, own_ref, got_refs, line_ref)
+def last_kernel(place_ref, outside_ref, own_ref, *rest):
+    got_refs, (out_ref, line_ref, far_ref, table_ref, kept_ref) = rest[:-5], rest[-5:]
+    gather_lines(place_ref, own_ref, got_refs, line_ref)
     line_pass(line_ref, far_ref, table_ref, kept_ref)
     for piece in range(LINE // LANES):
         part = pl.ds(piece * LANES, LANES)
@@ -213,17 +201,17 @@
             cost_estimate=pl.CostEstimate(flops=int(work), bytes_accessed=2**20, transcendentals=0),
         )(*args)
 
+    place = jnp.stack([lax.axis_index("robot"), lax.axis_index("yz")]).astype(jnp.int32)
     lowest = jnp.min(seed_cost, axis=0)
     other = lax.ppermute(lowest, "robot", [(0, 1), (1, 0)])
     raised = call(
         prepare_kernel, jax.ShapeDtypeStruct((FIELDS, depth, rows, columns), f32), [], occupied, unknown
     )
-    half = lax.axis_index("robot").astype(jnp.int32).reshape(1)
     planes = call(
         depth_kernel,
         jax.ShapeDtypeStruct((own, FIELDS, rows, columns), jnp.int16),
         [pltpu.VMEM((FIELDS, depth, rows, columns), f32), pltpu.VMEM((FIELDS, own, rows, columns), f32)],
-        half,
+        place,
         lowest,
         other,
         raised,
@@ -233,34 +221,29 @@
 
     parts = lax.axis_size("yz")
     share = LINE // parts
-    me = lax.axis_index("yz").astype(jnp.int32).reshape(1)
-    line = pltpu.VMEM((LINE, LANES), f32)
-    kept = pltpu.SMEM((BLOCKS,), jnp.int32)
+    scratch = [
+        pltpu.VMEM((LINE, LANES), f32),
+        pltpu.VMEM((LINE, LANES), f32),
+        pltpu.VMEM((2 * LINE, LANES), f32),
+        pltpu.SMEM((BLOCKS,), jnp.int32),
+    ]
     shapes = (jax.ShapeDtypeStruct((columns, share), f32),)
     shapes += (jax.ShapeDtypeStruct((columns, share), jnp.int16),) * (parts - 1)
-    squares = jax.ShapeDtypeStruct((ROWS, 2 * MIDDLE, ROWS, LANES), f32)
-    scratch = [line, line, kept]
-    row_calls = [functools.partial(row_kernel, field) for field in range(FIELDS)]
-    table, *first = call(row_calls[0], (squares, *shapes), scratch, me, crossed, scalar=True)
-    second = call(row_calls[1], shapes, scratch, me, crossed, table, scalar=True)
     settled = []
-    for made in (first, second):
+    for field in range(FIELDS):
+        own_part, *others = call(
+            functools.partial(row_kernel, field), shapes, scratch, place, crossed, scalar=True
+        )
         got = [
-            lax.ppermute(made[step], "yz", [(i, i ^ step) for i in range(parts)]) for step in range(1, parts)
+            lax.ppermute(part, "yz", [(i, i ^ step) for i in range(parts)])
+            for step, part in enumerate(others, 1)
         ]
-        settled.append((made[0], *got))
+        settled.append((own_part, *got))
     outside = call(
-        column_kernel, jax.ShapeDtypeStruct((LINE, share), f32), [line, kept], me, table, *settled[0], scalar=True
+        column_kernel, jax.ShapeDtypeStruct((LINE, share), f32), scratch[1:], place, *settled[0], scalar=True
     )
     signed = call(
-        last_kernel,
-        jax.ShapeDtypeStruct((share, LINE), f32),
-        [line, line, kept],
-        me,
-        table,
-        outside,
-        *settled[1],
-        scalar=True,
+        last_kernel, jax.ShapeDtypeStruct((share, LINE), f32), scratch, place, outside, *settled[1], scalar=True
     )
     return signed[None]
 

time: 57.4 us -> 55.1 us (0.960)
  blocking collectives: 0 us -> 21.6 us
  starting transfers between devices: 25.4 us -> 9.23 us
  waiting for transfers between devices: 13.3 us -> 4.64 us
  Pallas kernels: 15.7 us -> 17 us
  local copies, waits for them, and re-layouts: 2.08 us -> 1.05 us
    all_to_all x0 -> x1, blocking collectives: none -> 21.6 us  [body(): lax.all_to_all(planes, 'xy', split_axis=0, concat_axis=0, tiled=True)]
    all_to_all x1 -> x0, starting transfers between devices: 12.2 us -> none  [body(): lax.all_to_all(planes, 'xy', split_axis=0, concat_axis=0, tiled=True)]
    all_to_all x1 -> x0, waiting for transfers between devices: 9.65 us -> none  [body(): lax.all_to_all(planes, 'xy', split_axis=0, concat_axis=0, tiled=True)]
    ppermute x6, starting transfers between devices: 9.59 us -> 5.58 us  [body(): lax.ppermute(part, 'yz', [(i, i ^ step) for i in range(parts)])]
    pallas_call x6, Pallas kernels: 15.7 us -> 17 us  [call(): pl.pallas_call(kernel, out_shape=out_shape, in_specs=in_specs, out_specs=...]
    unnamed x4, local copies, waits for them, and re-layouts: 2.08 us -> 1.05 us
    ppermute x1, waiting for transfers between devices: 2.75 us -> 3.71 us  [body(): other = lax.ppermute(lowest, 'robot', [(0, 1), (1, 0)])]
  transfers between devices with their start and end apart: 8 -> 7, of which waited for: 3 -> 2; matrix products, arithmetic and copies ran while one was open for 0% -> 0% of each run, Pallas kernels for 9% -> 11%
where the time goes in v3:
time: 55.1 us; the launch traced here: 54.9 us
  blocking collectives  21.6 us (39%)
  Pallas kernels  17 us (31%)
  starting transfers between devices  9.23 us (17%)
  waiting for transfers between devices  4.64 us (8%)
  other arithmetic  1.26 us (2%)
  local copies, waits for them, and re-layouts  1.05 us (2%)
    all_to_all x1, blocking collectives, body(): lax.all_to_all(planes, 'xy', split_axis=0, concat_axis=0, tiled=True)  21.6 us
    pallas_call x6, Pallas kernels, call(): pl.pallas_call(kernel, out_shape=out_shape, in_specs=in_specs, out_specs=...  17 us
    ppermute x6, starting transfers between devices, body(): lax.ppermute(part, 'yz', [(i, i ^ step) for i in range(parts)])  5.58 us
    ppermute x1, waiting for transfers between devices, body(): other = lax.ppermute(lowest, 'robot', [(0, 1), (1, 0)])  3.71 us
    ppermute x1, starting transfers between devices, body(): other = lax.ppermute(lowest, 'robot', [(0, 1), (1, 0)])  3.65 us
    reduce_min x1, other arithmetic, body(): lowest = jnp.min(seed_cost, axis=0)  1.19 us
  transfers between devices with their start and end apart: 7, of which 2 were waited for; matrix products, arithmetic and copies ran while one was open for 0% of the time, Pallas kernels for 11%

profile of v3, /device:TPU:1, one launch (start us, length us, event | category | flops | bytes accessed | tf_op | source)
XLA Modules:
  0.0 54.9 jit_solution(18317612024188492971)
XLA Ops:
  0.0 1.2 %reduce_min.9.mine_ref = bf16[64,16,128]{2,1,0:T(8,128)(2,1)S(1)} reduce(bf16[2,64,16,128]{3,2,1,0:T(8,128)(2,1)} %param.3, bf16[]{:T(256)} %constant.11.clone.1), dimensions={0}, to_apply=%region_0.0 | reduce | flops 131072 | bytes 786434 | tf_op jit(solution)/shard_map/reduce_min | solution.py:205
  1.2 3.6 %collective-permute-start = (bf16[64,16,128]{2,1,0:T(8,128)(2,1)S(1)}, bf16[64,16,128]{2,1,0:T(8,128)(2,1)S(1)}, u32[]{:S(2)}, u32[]{:S(2)}) collective-permute-start(bf16[64,16,128]{2,1,0:T(8,128)(2,1)S(1)} %reduce_min.9.mine_ref), channel_id=1, source_target_pairs={{0,128},{128,0},{1,129},{129,1},{2,130},{130,2},{3,131},{131,3},{4... | collective-permute-start | bytes 786440 | tf_op jit(solution)/shard_map/ppermute | solution.py:206
  4.8 1.0 %copy-done.1 = s32[64,16,128]{2,1,0:T(8,128)S(1)} copy-done((s32[64,16,128]{2,1,0:T(8,128)S(1)}, s32[64,16,128]{2,1,0:T(8,128)}, u32[]{:S(2)}) %copy-start.1) | copy-done | bytes 524312
  5.9 0.1 shard_map.37.raise_ref
  6.0 0.1 pad_add_fusion.place_ref
  6.1 3.7 %collective-permute-done.other_ref = bf16[64,16,128]{2,1,0:T(8,128)(2,1)S(1)} collective-permute-done((bf16[64,16,128]{2,1,0:T(8,128)(2,1)S(1)}, bf16[64,16,128]{2,1,0:T(8,128)(2,1)S(1)}, u32[]{:S(2)}, u32[]{:S(2)}) %collective-permute-start) | collective-permute-done | bytes 262176 | tf_op jit(solution)/shard_map/ppermute | solution.py:206
  9.8 3.4 %shard_map.38 = s16[32,2,16,128]{3,2,1,0:T(8,128)(2,1)S(1)} custom-call(s32[2]{0:T(128)S(1)} %pad_add_fusion.place_ref, bf16[64,16,128]{2,1,0:T(8,128)(2,1)S(1)} %reduce_min.9.mine_ref, bf16[64,16,128]{2,1,0:T(8,128)(2,1)S(1)} %collective-permute-done.other_ref, f32[2,64,16,128]{3,2,1,0:T(8,128)S(1)} %shard_map.37.raise_ref), custom_call_target="tpu_custom_call" | custom-call | flops 4000000 | bytes 1048576 | tf_op jit(solution)/shard_map/pallas_call | solution.py:194
  13.2 21.6 %all_to_all.5.in_ref = s16[32,2,16,128]{3,2,1,0:T(8,128)(2,1)S(1)} all-to-all(s16[32,2,16,128]{3,2,1,0:T(8,128)(2,1)S(1)} %shard_map.38), channel_id=1, replica_groups=mesh['robot'=2,'xy'=32,'yz'=4] {'xy'}, dimensions={0} | all-to-all | bytes 524288 | tf_op jit(solution)/shard_map/all_to_all | solution.py:220
  34.8 3.9 %shard_map.39 = (f32[128,128]{1,0:T(8,128)S(1)}, s16[128,128]{1,0:T(8,128)(2,1)S(1)}, s16[128,128]{1,0:T(8,128)(2,1)S(1)}, s16[128,128]{1,0:T(8,128)(2,1)S(1)}) custom-call(s32[2]{0:T(128)S(1)} %pad_add_fusion.place_ref, s16[32,2,16,128]{3,2,1,0:T(8,128)(2,1)S(1)} %all_to_all.5.in_ref), custom_call_target="tpu_custom_call" | custom-call | flops 4000000 | bytes 1048576 | tf_op jit(solution)/shard_map/pallas_call | solution.py:194
  38.7 1.6 %collective-permute-start.1 = (s16[128,128]{1,0:T(8,128)(2,1)S(1)}, s16[128,128]{1,0:T(8,128)(2,1)S(1)}, u32[]{:S(2)}, u32[]{:S(2)}) collective-permute-start(s16[128,128]{1,0:T(8,128)(2,1)S(1)} %get-tuple-element.14), channel_id=1, source_target_pairs={{0,1},{1,0},{2,3},{3,2},{4,5},{5,4},{6,7},{7,6},{8,9},{9,8},{10,11... | collective-permute-start | bytes 98312 | tf_op jit(solution)/shard_map/ppermute | solution.py:238
  40.3 1.6 %collective-permute-start.2 = (s16[128,128]{1,0:T(8,128)(2,1)S(1)}, s16[128,128]{1,0:T(8,128)(2,1)S(1)}, u32[]{:S(2)}, u32[]{:S(2)}) collective-permute-start(s16[128,128]{1,0:T(8,128)(2,1)S(1)} %get-tuple-element.15), channel_id=1, source_target_pairs={{0,2},{1,3},{2,0},{3,1},{4,6},{5,7},{6,4},{7,5},{8,10},{9,11},{10,... | collective-permute-start | bytes 98312 | tf_op jit(solution)/shard_map/ppermute | solution.py:238
  42.0 0.1 collective-permute-start.3
  42.1 3.1 %shard_map.41 = (f32[128,128]{1,0:T(8,128)S(1)}, s16[128,128]{1,0:T(8,128)(2,1)S(1)}, s16[128,128]{1,0:T(8,128)(2,1)S(1)}, s16[128,128]{1,0:T(8,128)(2,1)S(1)}) custom-call(s32[2]{0:T(128)S(1)} %pad_add_fusion.place_ref, s16[32,2,16,128]{3,2,1,0:T(8,128)(2,1)S(1)} %all_to_all.5.in_ref), custom_call_target="tpu_custom_call" | custom-call | flops 4000000 | bytes 1048576 | tf_op jit(solution)/shard_map/pallas_call | solution.py:194
  45.2 0.3 collective-permute-start.4
  45.6 1.5 %collective-permute-start.5 = (s16[128,128]{1,0:T(8,128)(2,1)S(1)}, s16[128,128]{1,0:T(8,128)(2,1)S(1)}, u32[]{:S(2)}, u32[]{:S(2)}) collective-permute-start(s16[128,128]{1,0:T(8,128)(2,1)S(1)} %get-tuple-element.19), channel_id=1, source_target_pairs={{0,2},{1,3},{2,0},{3,1},{4,6},{5,7},{6,4},{7,5},{8,10},{9,11},{10,... | collective-permute-start | bytes 98312 | tf_op jit(solution)/shard_map/ppermute | solution.py:238
  47.1 0.0 collective-permute-done.1.rest_0_
  47.1 0.4 collective-permute-start.6
  47.4 0.0 collective-permute-done.2.rest_1_
  47.5 0.0 collective-permute-done.3.rest_2_
  47.5 2.7 %shard_map.40.outside_ref = f32[512,128]{1,0:T(8,128)S(1)} custom-call(s32[2]{0:T(128)S(1)} %pad_add_fusion.place_ref, f32[128,128]{1,0:T(8,128)S(1)} %get-tuple-element.13.own_ref, s16[128,128]{1,0:T(8,128)(2,1)S(1)} %collective-permute-done.1.rest_0_, s16[128,128]{1,0:T(8,128)(2,1)S(1)} %collective-permute-done.2.rest_1_, ...), custom_call_target="tpu_custom_call" | custom-call | flops 4000000 | bytes 1048576 | tf_op jit(solution)/shard_map/pallas_call | solution.py:194
  50.1 0.0 collective-permute-done.4.rest_0_
  50.1 0.0 collective-permute-done.5.rest_1_
  50.1 0.9 %collective-permute-done.6.rest_2_ = s16[128,128]{1,0:T(8,128)(2,1)S(1)} collective-permute-done((s16[128,128]{1,0:T(8,128)(2,1)S(1)}, s16[128,128]{1,0:T(8,128)(2,1)S(1)}, u32[]{:S(2)}, u32[]{:S(2)}) %collective-permute-start.6) | collective-permute-done | bytes 32800 | tf_op jit(solution)/shard_map/ppermute | solution.py:238
  51.1 3.8 %shard_map.42 = f32[128,512]{1,0:T(8,128)} custom-call(s32[2]{0:T(128)S(1)} %pad_add_fusion.place_ref, f32[512,128]{1,0:T(8,128)S(1)} %shard_map.40.outside_ref, f32[128,128]{1,0:T(8,128)S(1)} %get-tuple-element.17.own_ref, s16[128,128]{1,0:T(8,128)(2,1)S(1)} %collective-permute-done.4.rest_0_, s16[128,128]{1,0:T(8,128)(2,1)S(1)} %collective-permute-done.5.rest_1_, ...), custom_call_target="tpu_custom_call" | custom-call | flops 4000000 | bytes 1048576 | tf_op jit(solution)/shard_map/pallas_call | solution.py:194
  (3 shorter events, 0.0 us)
Async XLA Ops:
  0.0 4.8 %copy-start = (s32[64,16,128]{2,1,0:T(8,128)S(1)}, s32[64,16,128]{2,1,0:T(8,128)}, u32[]{:S(2)}) copy-start(s32[64,16,128]{2,1,0:T(8,128)} %occupied_ref.1) | copy-start | bytes 1572868
  1.2 8.6 %collective-permute-start = (bf16[64,16,128]{2,1,0:T(8,128)(2,1)S(1)}, bf16[64,16,128]{2,1,0:T(8,128)(2,1)S(1)}, u32[]{:S(2)}, u32[]{:S(2)}) collective-permute-start(bf16[64,16,128]{2,1,0:T(8,128)(2,1)S(1)} %reduce_min.9.mine_ref), channel_id=1, source_target_pairs={{0,128},{128,0},{1,129},{129,1},{2,130},{130,2},{3,131},{131,3},{4... | collective-permute-start | bytes 786440 | tf_op jit(solution)/shard_map/ppermute | solution.py:206
  4.8 1.0 %copy-start.1 = (s32[64,16,128]{2,1,0:T(8,128)S(1)}, s32[64,16,128]{2,1,0:T(8,128)}, u32[]{:S(2)}) copy-start(s32[64,16,128]{2,1,0:T(8,128)} %unknown_ref.1) | copy-start | bytes 1572868
  38.7 8.4 %collective-permute-start.1 = (s16[128,128]{1,0:T(8,128)(2,1)S(1)}, s16[128,128]{1,0:T(8,128)(2,1)S(1)}, u32[]{:S(2)}, u32[]{:S(2)}) collective-permute-start(s16[128,128]{1,0:T(8,128)(2,1)S(1)} %get-tuple-element.14), channel_id=1, source_target_pairs={{0,1},{1,0},{2,3},{3,2},{4,5},{5,4},{6,7},{7,6},{8,9},{9,8},{10,11... | collective-permute-start | bytes 98312 | tf_op jit(solution)/shard_map/ppermute | solution.py:238
  40.3 7.1 %collective-permute-start.2 = (s16[128,128]{1,0:T(8,128)(2,1)S(1)}, s16[128,128]{1,0:T(8,128)(2,1)S(1)}, u32[]{:S(2)}, u32[]{:S(2)}) collective-permute-start(s16[128,128]{1,0:T(8,128)(2,1)S(1)} %get-tuple-element.15), channel_id=1, source_target_pairs={{0,2},{1,3},{2,0},{3,1},{4,6},{5,7},{6,4},{7,5},{8,10},{9,11},{10,... | collective-permute-start | bytes 98312 | tf_op jit(solution)/shard_map/ppermute | solution.py:238
  42.0 5.5 %collective-permute-start.3 = (s16[128,128]{1,0:T(8,128)(2,1)S(1)}, s16[128,128]{1,0:T(8,128)(2,1)S(1)}, u32[]{:S(2)}, u32[]{:S(2)}) collective-permute-start(s16[128,128]{1,0:T(8,128)(2,1)S(1)} %get-tuple-element.16), channel_id=1, source_target_pairs={{0,3},{1,2},{2,1},{3,0},{4,7},{5,6},{6,5},{7,4},{8,11},{9,10},{10,... | collective-permute-start | bytes 98312 | tf_op jit(solution)/shard_map/ppermute | solution.py:238
  45.2 4.9 %collective-permute-start.4 = (s16[128,128]{1,0:T(8,128)(2,1)S(1)}, s16[128,128]{1,0:T(8,128)(2,1)S(1)}, u32[]{:S(2)}, u32[]{:S(2)}) collective-permute-start(s16[128,128]{1,0:T(8,128)(2,1)S(1)} %get-tuple-element.18), channel_id=1, source_target_pairs={{0,1},{1,0},{2,3},{3,2},{4,5},{5,4},{6,7},{7,6},{8,9},{9,8},{10,11... | collective-permute-start | bytes 98312 | tf_op jit(solution)/shard_map/ppermute | solution.py:238
  45.6 4.6 %collective-permute-start.5 = (s16[128,128]{1,0:T(8,128)(2,1)S(1)}, s16[128,128]{1,0:T(8,128)(2,1)S(1)}, u32[]{:S(2)}, u32[]{:S(2)}) collective-permute-start(s16[128,128]{1,0:T(8,128)(2,1)S(1)} %get-tuple-element.19), channel_id=1, source_target_pairs={{0,2},{1,3},{2,0},{3,1},{4,6},{5,7},{6,4},{7,5},{8,10},{9,11},{10,... | collective-permute-start | bytes 98312 | tf_op jit(solution)/shard_map/ppermute | solution.py:238
  47.1 4.0 %collective-permute-start.6 = (s16[128,128]{1,0:T(8,128)(2,1)S(1)}, s16[128,128]{1,0:T(8,128)(2,1)S(1)}, u32[]{:S(2)}, u32[]{:S(2)}) collective-permute-start(s16[128,128]{1,0:T(8,128)(2,1)S(1)} %get-tuple-element.20), channel_id=1, source_target_pairs={{0,3},{1,2},{2,1},{3,0},{4,7},{5,6},{6,5},{7,4},{8,11},{9,10},{10,... | collective-permute-start | bytes 98312 | tf_op jit(solution)/shard_map/ppermute | solution.py:238

commit v4 on v3

--- a/solution.py
+++ b/solution.py
@@ -16,6 +16,7 @@
 BLOCK = 32
 BLOCKS = LINE // BLOCK
 GROUPS = BLOCK // ROWS
+PAD = ROWS
 FIELDS = 2
 
 STEPS = 65520.0 / 13.8629653
@@ -82,22 +83,25 @@
     lax.fori_loop(0, own, send, 0, unroll=4)
 
 
-def find_blocks(line_ref, kept_ref):
+def find_blocks(line_ref, kept_ref, least_gap=0.0, reached_ref=None):
     sublane = lax.broadcasted_iota(jnp.int32, (ROWS, LANES), 0).astype(jnp.float32)
     low = []
     for block in range(BLOCKS):
-        least = line_ref[block * BLOCK : block * BLOCK + ROWS, :]
+        at = PAD + block * BLOCK
+        least = line_ref[at : at + ROWS, :]
         for group in range(1, GROUPS):
-            at = block * BLOCK + group * ROWS
-            least = jnp.minimum(least, line_ref[at : at + ROWS, :])
+            least = jnp.minimum(least, line_ref[at + group * ROWS : at + (group + 1) * ROWS, :])
         low.append(jnp.broadcast_to(jnp.min(least, axis=0, keepdims=True), (ROWS, LANES)))
+    some = jnp.int32(0)
     for first in range(0, BLOCKS, ROWS):
         bound = jnp.full((ROWS, LANES), penalty, jnp.float32)
+        if reached_ref is not None:
+            bound = jnp.minimum(bound, reached_ref[first : first + ROWS, :])
         floor = []
         for block in range(BLOCKS):
             away = jnp.abs(sublane + float(first - block)) * float(BLOCK)
             far = away + float(BLOCK - 1)
-            near = jnp.maximum(away - float(BLOCK - 1), 0.0)
+            near = jnp.maximum(away - float(BLOCK - 1), least_gap)
             bound = jnp.minimum(bound, low[block] + far * far)
             floor.append(low[block] + near * near)
         kept = jnp.zeros((ROWS, 1), jnp.int32)
@@ -105,52 +109,105 @@
             keep = jnp.min(floor[block] - bound, axis=1, keepdims=True) < 0.0
             kept = kept | jnp.where(keep, 1 << block, 0)
         for row in range(ROWS):
-            kept_ref[first + row] = kept[row, 0]
-
-
-def line_pass(line_ref, far_ref, table_ref, kept_ref):
+            word = kept[row, 0]
+            kept_ref[first + row] = word
+            some = some | jnp.where(word != 0, jnp.int32(1 << (first + row)), 0)
+    return some
+
+
+def lower_block(line_ref, far_ref, table_ref, kept_ref, block, start):
+    def left(carry):
+        return carry[0] != 0
+
+    def pair(carry):
+        kept, source, best = carry
+        base = pl.multiple_of((block - source) * BLOCK + LINE, BLOCK)
+        row = pl.multiple_of(source * BLOCK, BLOCK) + PAD
+        kept = kept ^ lax.shift_left(jnp.int32(1), source)
+        best = list(best)
+        for p in range(ROWS):
+            squares = {k: table_ref[pl.ds(base + (k * ROWS - p), ROWS), :] for k in range(1 - GROUPS, GROUPS)}
+            for q in range(GROUPS):
+                value = jnp.broadcast_to(line_ref[pl.ds(row + q * ROWS + p, 1), :], (ROWS, LANES))
+                for group in range(GROUPS):
+                    best[group] = jnp.minimum(best[group], value + squares[group - q])
+        return kept, 31 - lax.clz(kept), tuple(best)
+
+    kept = kept_ref[block]
+    best = lax.while_loop(left, pair, (kept, 31 - lax.clz(kept), start))[2]
+    at = pl.multiple_of(block * BLOCK, BLOCK)
+    for group in range(GROUPS):
+        far_ref[pl.ds(at + group * ROWS, ROWS), :] = best[group]
+
+
+def fill_table(table_ref):
     sublane = lax.broadcasted_iota(jnp.int32, (ROWS, LANES), 0).astype(jnp.float32)
     for at in range(0, 2 * LINE, ROWS):
         apart = sublane + float(at - LINE)
         table_ref[at : at + ROWS, :] = apart * apart
+
+
+def sparse_pass(line_ref, far_ref, table_ref, kept_ref, _):
+    fill_table(table_ref)
     find_blocks(line_ref, kept_ref)
 
     def target(block, _):
+        at = pl.multiple_of(block * BLOCK, BLOCK) + PAD
+        start = tuple(line_ref[pl.ds(at + group * ROWS, ROWS), :] for group in range(GROUPS))
+        lower_block(line_ref, far_ref, table_ref, kept_ref, block, start)
+        return 0
+
+    lax.fori_loop(0, BLOCKS, target, 0)
+
+
+def dense_pass(line_ref, far_ref, table_ref, kept_ref, reached_ref):
+    fill_table(table_ref)
+    margin = jnp.full((PAD, LANES), 3e38, jnp.float32)
+    line_ref[:PAD, :] = margin
+    line_ref[PAD + LINE :, :] = margin
+
+    def band(block, _):
         at = pl.multiple_of(block * BLOCK, BLOCK)
-
-        def left(carry):
-            return carry[0] != 0
-
-        def pair(carry):
-            kept, source, best = carry
-            base = pl.multiple_of((block - source) * BLOCK + LINE, BLOCK)
-            row = pl.multiple_of(source * BLOCK, BLOCK)
-            kept = kept ^ lax.shift_left(jnp.int32(1), source)
-            best = list(best)
-            for p in range(ROWS):
-                squares = {k: table_ref[pl.ds(base + (k * ROWS - p), ROWS), :] for k in range(1 - GROUPS, GROUPS)}
-                for q in range(GROUPS):
-                    value = jnp.broadcast_to(line_ref[pl.ds(row + q * ROWS + p, 1), :], (ROWS, LANES))
-                    for group in range(GROUPS):
-                        best[group] = jnp.minimum(best[group], value + squares[group - q])
-            return kept, 31 - lax.clz(kept), tuple(best)
-
-        kept = kept_ref[block]
-        start = tuple(line_ref[pl.ds(at + group * ROWS, ROWS), :] for group in range(GROUPS))
-        best = lax.while_loop(left, pair, (kept, 31 - lax.clz(kept), start))[2]
+        best = [None] * GROUPS
+        for p in range(ROWS):
+            first = LINE - p
+            squares = {k: table_ref[first + k * ROWS : first + (k + 1) * ROWS, :] for k in (-1, 0, 1)}
+            for q in range(-1, GROUPS + 1):
+                value = jnp.broadcast_to(line_ref[pl.ds(at + (PAD + q * ROWS + p), 1), :], (ROWS, LANES))
+                for group in range(max(q - 1, 0), min(q + 2, GROUPS)):
+                    candidate = value + squares[group - q]
+                    best[group] = candidate if best[group] is None else jnp.minimum(best[group], candidate)
+        most = best[0]
         for group in range(GROUPS):
             far_ref[pl.ds(at + group * ROWS, ROWS), :] = best[group]
-        return 0
-
-    lax.fori_loop(0, BLOCKS, target, 0)
+            most = jnp.maximum(most, best[group])
+        reached_ref[pl.ds(block, 1), :] = jnp.max(most, axis=0, keepdims=True)
+        return 0
+
+    lax.fori_loop(0, BLOCKS, band, 0, unroll=2)
+
+    def left(some):
+        return some != 0
+
+    def target(some):
+        block = 31 - lax.clz(some)
+        at = pl.multiple_of(block * BLOCK, BLOCK)
+        start = tuple(far_ref[pl.ds(at + group * ROWS, ROWS), :] for group in range(GROUPS))
+        lower_block(line_ref, far_ref, table_ref, kept_ref, block, start)
+        return some ^ lax.shift_left(jnp.int32(1), block)
+
+    lax.while_loop(left, target, find_blocks(line_ref, kept_ref, float(ROWS + 1), reached_ref))
+
+
+PASSES = (sparse_pass, dense_pass)
 
 
 def row_kernel(field, place_ref, in_ref, own_ref, *rest):
-    send_refs, (line_ref, far_ref, table_ref, kept_ref) = rest[:-4], rest[-4:]
+    send_refs, (line_ref, far_ref, *scratch) = rest[:-5], rest[-5:]
     chunk = in_ref.shape[2]
     for piece in range(in_ref.shape[0]):
-        line_ref[piece * chunk : (piece + 1) * chunk, :] = decode(in_ref[piece, field])
-    line_pass(line_ref, far_ref, table_ref, kept_ref)
+        line_ref[PAD + piece * chunk : PAD + (piece + 1) * chunk, :] = decode(in_ref[piece, field])
+    PASSES[field](line_ref, far_ref, *scratch)
     for step in range(len(send_refs) + 1):
         part = pl.ds(pl.multiple_of((place_ref[1] ^ step) * LANES, LANES), LANES)
         value = far_ref[part, :].T
@@ -162,20 +219,20 @@
 
 def gather_lines(place_ref, own_ref, got_refs, line_ref):
     for step in range(len(got_refs) + 1):
-        part = pl.ds(pl.multiple_of((place_ref[1] ^ step) * LANES, LANES), LANES)
+        part = pl.ds(pl.multiple_of((place_ref[1] ^ step) * LANES, LANES) + PAD, LANES)
         line_ref[part, :] = decode(got_refs[step - 1][...]) if step else own_ref[...]
 
 
 def column_kernel(place_ref, own_ref, *rest):
-    got_refs, (far_ref, line_ref, table_ref, kept_ref) = rest[:-4], rest[-4:]
+    got_refs, (far_ref, line_ref, *scratch) = rest[:-5], rest[-5:]
     gather_lines(place_ref, own_ref, got_refs, line_ref)
-    line_pass(line_ref, far_ref, table_ref, kept_ref)
+    PASSES[0](line_ref, far_ref, *scratch)
 
 
 def last_kernel(place_ref, outside_ref, own_ref, *rest):
-    got_refs, (out_ref, line_ref, far_ref, table_ref, kept_ref) = rest[:-5], rest[-5:]
+    got_refs, (out_ref, line_ref, far_ref, *scratch) = rest[:-6], rest[-6:]
     gather_lines(place_ref, own_ref, got_refs, line_ref)
-    line_pass(line_ref, far_ref, table_ref, kept_ref)
+    PASSES[1](line_ref, far_ref, *scratch)
     for piece in range(LINE // LANES):
         part = pl.ds(piece * LANES, LANES)
         signed = voxel_size * (jnp.sqrt(outside_ref[part, :]) - jnp.sqrt(far_ref[part, :]))
@@ -221,18 +278,19 @@
 
     parts = lax.axis_size("yz")
     share = LINE // parts
+    line = pltpu.VMEM((LINE + 2 * PAD, LANES), f32)
     scratch = [
-        pltpu.VMEM((LINE, LANES), f32),
-        pltpu.VMEM((LINE, LANES), f32),
         pltpu.VMEM((2 * LINE, LANES), f32),
         pltpu.SMEM((BLOCKS,), jnp.int32),
+        pltpu.VMEM((BLOCKS, LANES), f32),
     ]
+    lines = [line, pltpu.VMEM((LINE, LANES), f32), *scratch]
     shapes = (jax.ShapeDtypeStruct((columns, share), f32),)
     shapes += (jax.ShapeDtypeStruct((columns, share), jnp.int16),) * (parts - 1)
     settled = []
     for field in range(FIELDS):
         own_part, *others = call(
-            functools.partial(row_kernel, field), shapes, scratch, place, crossed, scalar=True
+            functools.partial(row_kernel, field), shapes, lines, place, crossed, scalar=True
         )
         got = [
             lax.ppermute(part, "yz", [(i, i ^ step) for i in range(parts)])
@@ -240,10 +298,10 @@
         ]
         settled.append((own_part, *got))
     outside = call(
-        column_kernel, jax.ShapeDtypeStruct((LINE, share), f32), scratch[1:], place, *settled[0], scalar=True
+        column_kernel, jax.ShapeDtypeStruct((LINE, share), f32), [line, *scratch], place, *settled[0], scalar=True
     )
     signed = call(
-        last_kernel, jax.ShapeDtypeStruct((share, LINE), f32), scratch, place, outside, *settled[1], scalar=True
+        last_kernel, jax.ShapeDtypeStruct((share, LINE), f32), lines, place, outside, *settled[1], scalar=True
     )
     return signed[None]
 

time: 55.1 us -> 55.7 us (1.011)
  starting transfers between devices: 9.23 us -> 13 us
  Pallas kernels: 17 us -> 14.5 us
  waiting for transfers between devices: 4.64 us -> 3.73 us
    ppermute x6, starting transfers between devices: 5.58 us -> 9.31 us  [body(): lax.ppermute(part, 'yz', [(i, i ^ step) for i in range(parts)])]
    pallas_call x6, Pallas kernels: 17 us -> 14.5 us  [call(): pl.pallas_call(kernel, out_shape=out_shape, in_specs=in_specs, out_specs=...]
    ppermute x6, waiting for transfers between devices: 0.93 us -> 0.02 us  [body(): lax.ppermute(part, 'yz', [(i, i ^ step) for i in range(parts)])]
  transfers between devices with their start and end apart: 7 -> 7, of which waited for: 2 -> 1; matrix products, arithmetic and copies ran while one was open for 0% -> 0% of each run, Pallas kernels for 11% -> 10%
where the time goes in v4:
time: 55.7 us; the launch traced here: 55.2 us
  blocking collectives  21.6 us (39%)
  Pallas kernels  14.5 us (26%)
  starting transfers between devices  13 us (23%)
  waiting for transfers between devices  3.73 us (7%)
  other arithmetic  1.26 us (2%)
  local copies, waits for them, and re-layouts  1.05 us (2%)
    all_to_all x1, blocking collectives, body(): lax.all_to_all(planes, 'xy', split_axis=0, concat_axis=0, tiled=True)  21.6 us
    pallas_call x6, Pallas kernels, call(): pl.pallas_call(kernel, out_shape=out_shape, in_specs=in_specs, out_specs=...  14.5 us
    ppermute x6, starting transfers between devices, body(): lax.ppermute(part, 'yz', [(i, i ^ step) for i in range(parts)])  9.31 us
    ppermute x1, waiting for transfers between devices, body(): other = lax.ppermute(lowest, 'robot', [(0, 1), (1, 0)])  3.71 us
    ppermute x1, starting transfers between devices, body(): other = lax.ppermute(lowest, 'robot', [(0, 1), (1, 0)])  3.65 us
    reduce_min x1, other arithmetic, body(): lowest = jnp.min(seed_cost, axis=0)  1.19 us
  transfers between devices with their start and end apart: 7, of which 1 were waited for; matrix products, arithmetic and copies ran while one was open for 0% of the time, Pallas kernels for 10%

profile of v4, /device:TPU:1, one launch (start us, length us, event | category | flops | bytes accessed | tf_op | source)
XLA Modules:
  0.0 55.2 jit_solution(13228599001639875604)
XLA Ops:
  0.0 1.2 %reduce_min.9.mine_ref = bf16[64,16,128]{2,1,0:T(8,128)(2,1)S(1)} reduce(bf16[2,64,16,128]{3,2,1,0:T(8,128)(2,1)} %param.3, bf16[]{:T(256)} %constant.11.clone.1), dimensions={0}, to_apply=%region_0.0 | reduce | flops 131072 | bytes 786434 | tf_op jit(solution)/shard_map/reduce_min | solution.py:262
  1.2 3.6 %collective-permute-start = (bf16[64,16,128]{2,1,0:T(8,128)(2,1)S(1)}, bf16[64,16,128]{2,1,0:T(8,128)(2,1)S(1)}, u32[]{:S(2)}, u32[]{:S(2)}) collective-permute-start(bf16[64,16,128]{2,1,0:T(8,128)(2,1)S(1)} %reduce_min.9.mine_ref), channel_id=1, source_target_pairs={{0,128},{128,0},{1,129},{129,1},{2,130},{130,2},{3,131},{131,3},{4... | collective-permute-start | bytes 786440 | tf_op jit(solution)/shard_map/ppermute | solution.py:263
  4.8 1.0 %copy-done.1 = s32[64,16,128]{2,1,0:T(8,128)S(1)} copy-done((s32[64,16,128]{2,1,0:T(8,128)S(1)}, s32[64,16,128]{2,1,0:T(8,128)}, u32[]{:S(2)}) %copy-start.1) | copy-done | bytes 524312
  5.9 0.1 shard_map.37.raise_ref
  6.0 0.1 pad_add_fusion.place_ref
  6.1 3.7 %collective-permute-done.other_ref = bf16[64,16,128]{2,1,0:T(8,128)(2,1)S(1)} collective-permute-done((bf16[64,16,128]{2,1,0:T(8,128)(2,1)S(1)}, bf16[64,16,128]{2,1,0:T(8,128)(2,1)S(1)}, u32[]{:S(2)}, u32[]{:S(2)}) %collective-permute-start) | collective-permute-done | bytes 262176 | tf_op jit(solution)/shard_map/ppermute | solution.py:263
  9.8 3.4 %shard_map.38 = s16[32,2,16,128]{3,2,1,0:T(8,128)(2,1)S(1)} custom-call(s32[2]{0:T(128)S(1)} %pad_add_fusion.place_ref, bf16[64,16,128]{2,1,0:T(8,128)(2,1)S(1)} %reduce_min.9.mine_ref, bf16[64,16,128]{2,1,0:T(8,128)(2,1)S(1)} %collective-permute-done.other_ref, f32[2,64,16,128]{3,2,1,0:T(8,128)S(1)} %shard_map.37.raise_ref), custom_call_target="tpu_custom_call" | custom-call | flops 4000000 | bytes 1048576 | tf_op jit(solution)/shard_map/pallas_call | solution.py:251
  13.2 21.6 %all_to_all.5.in_ref = s16[32,2,16,128]{3,2,1,0:T(8,128)(2,1)S(1)} all-to-all(s16[32,2,16,128]{3,2,1,0:T(8,128)(2,1)S(1)} %shard_map.38), channel_id=1, replica_groups=mesh['robot'=2,'xy'=32,'yz'=4] {'xy'}, dimensions={0} | all-to-all | bytes 524288 | tf_op jit(solution)/shard_map/all_to_all | solution.py:277
  34.8 3.2 %shard_map.39 = (f32[128,128]{1,0:T(8,128)S(1)}, s16[128,128]{1,0:T(8,128)(2,1)S(1)}, s16[128,128]{1,0:T(8,128)(2,1)S(1)}, s16[128,128]{1,0:T(8,128)(2,1)S(1)}) custom-call(s32[2]{0:T(128)S(1)} %pad_add_fusion.place_ref, s16[32,2,16,128]{3,2,1,0:T(8,128)(2,1)S(1)} %all_to_all.5.in_ref), custom_call_target="tpu_custom_call" | custom-call | flops 4000000 | bytes 1048576 | tf_op jit(solution)/shard_map/pallas_call | solution.py:251
  38.0 4.8 %collective-permute-start.1 = (s16[128,128]{1,0:T(8,128)(2,1)S(1)}, s16[128,128]{1,0:T(8,128)(2,1)S(1)}, u32[]{:S(2)}, u32[]{:S(2)}) collective-permute-start(s16[128,128]{1,0:T(8,128)(2,1)S(1)} %get-tuple-element.14), channel_id=1, source_target_pairs={{0,1},{1,0},{2,3},{3,2},{4,5},{5,4},{6,7},{7,6},{8,9},{9,8},{10,11... | collective-permute-start | bytes 98312 | tf_op jit(solution)/shard_map/ppermute | solution.py:296
  42.9 0.0 collective-permute-start.2
  42.9 1.7 %collective-permute-start.3 = (s16[128,128]{1,0:T(8,128)(2,1)S(1)}, s16[128,128]{1,0:T(8,128)(2,1)S(1)}, u32[]{:S(2)}, u32[]{:S(2)}) collective-permute-start(s16[128,128]{1,0:T(8,128)(2,1)S(1)} %get-tuple-element.16), channel_id=1, source_target_pairs={{0,3},{1,2},{2,1},{3,0},{4,7},{5,6},{6,5},{7,4},{8,11},{9,10},{10,... | collective-permute-start | bytes 98312 | tf_op jit(solution)/shard_map/ppermute | solution.py:296
  44.6 2.0 %shard_map.41 = (f32[128,128]{1,0:T(8,128)S(1)}, s16[128,128]{1,0:T(8,128)(2,1)S(1)}, s16[128,128]{1,0:T(8,128)(2,1)S(1)}, s16[128,128]{1,0:T(8,128)(2,1)S(1)}) custom-call(s32[2]{0:T(128)S(1)} %pad_add_fusion.place_ref, s16[32,2,16,128]{3,2,1,0:T(8,128)(2,1)S(1)} %all_to_all.5.in_ref), custom_call_target="tpu_custom_call" | custom-call | flops 4000000 | bytes 1048576 | tf_op jit(solution)/shard_map/pallas_call | solution.py:251
  46.6 1.0 %collective-permute-start.4 = (s16[128,128]{1,0:T(8,128)(2,1)S(1)}, s16[128,128]{1,0:T(8,128)(2,1)S(1)}, u32[]{:S(2)}, u32[]{:S(2)}) collective-permute-start(s16[128,128]{1,0:T(8,128)(2,1)S(1)} %get-tuple-element.18), channel_id=1, source_target_pairs={{0,1},{1,0},{2,3},{3,2},{4,5},{5,4},{6,7},{7,6},{8,9},{9,8},{10,11... | collective-permute-start | bytes 98312 | tf_op jit(solution)/shard_map/ppermute | solution.py:296
  47.6 0.0 collective-permute-start.5
  47.6 0.0 collective-permute-done.1.rest_0_
  47.6 1.7 %collective-permute-start.6 = (s16[128,128]{1,0:T(8,128)(2,1)S(1)}, s16[128,128]{1,0:T(8,128)(2,1)S(1)}, u32[]{:S(2)}, u32[]{:S(2)}) collective-permute-start(s16[128,128]{1,0:T(8,128)(2,1)S(1)} %get-tuple-element.20), channel_id=1, source_target_pairs={{0,3},{1,2},{2,1},{3,0},{4,7},{5,6},{6,5},{7,4},{8,11},{9,10},{10,... | collective-permute-start | bytes 98312 | tf_op jit(solution)/shard_map/ppermute | solution.py:296
  49.4 0.0 collective-permute-done.2.rest_1_
  49.4 0.0 collective-permute-done.3.rest_2_
  49.4 3.2 %shard_map.40.outside_ref = f32[512,128]{1,0:T(8,128)S(1)} custom-call(s32[2]{0:T(128)S(1)} %pad_add_fusion.place_ref, f32[128,128]{1,0:T(8,128)S(1)} %get-tuple-element.13.own_ref, s16[128,128]{1,0:T(8,128)(2,1)S(1)} %collective-permute-done.1.rest_0_, s16[128,128]{1,0:T(8,128)(2,1)S(1)} %collective-permute-done.2.rest_1_, ...), custom_call_target="tpu_custom_call" | custom-call | flops 4000000 | bytes 1048576 | tf_op jit(solution)/shard_map/pallas_call | solution.py:251
  52.6 0.0 collective-permute-done.4.rest_0_
  52.6 0.0 collective-permute-done.5.rest_1_
  52.6 0.0 collective-permute-done.6.rest_2_
  52.6 2.5 %shard_map.42 = f32[128,512]{1,0:T(8,128)} custom-call(s32[2]{0:T(128)S(1)} %pad_add_fusion.place_ref, f32[512,128]{1,0:T(8,128)S(1)} %shard_map.40.outside_ref, f32[128,128]{1,0:T(8,128)S(1)} %get-tuple-element.17.own_ref, s16[128,128]{1,0:T(8,128)(2,1)S(1)} %collective-permute-done.4.rest_0_, s16[128,128]{1,0:T(8,128)(2,1)S(1)} %collective-permute-done.5.rest_1_, ...), custom_call_target="tpu_custom_call" | custom-call | flops 4000000 | bytes 1048576 | tf_op jit(solution)/shard_map/pallas_call | solution.py:251
  (3 shorter events, 0.0 us)
Async XLA Ops:
  0.0 4.8 %copy-start = (s32[64,16,128]{2,1,0:T(8,128)S(1)}, s32[64,16,128]{2,1,0:T(8,128)}, u32[]{:S(2)}) copy-start(s32[64,16,128]{2,1,0:T(8,128)} %occupied_ref.1) | copy-start | bytes 1572868
  1.2 8.6 %collective-permute-start = (bf16[64,16,128]{2,1,0:T(8,128)(2,1)S(1)}, bf16[64,16,128]{2,1,0:T(8,128)(2,1)S(1)}, u32[]{:S(2)}, u32[]{:S(2)}) collective-permute-start(bf16[64,16,128]{2,1,0:T(8,128)(2,1)S(1)} %reduce_min.9.mine_ref), channel_id=1, source_target_pairs={{0,128},{128,0},{1,129},{129,1},{2,130},{130,2},{3,131},{131,3},{4... | collective-permute-start | bytes 786440 | tf_op jit(solution)/shard_map/ppermute | solution.py:263
  4.8 1.0 %copy-start.1 = (s32[64,16,128]{2,1,0:T(8,128)S(1)}, s32[64,16,128]{2,1,0:T(8,128)}, u32[]{:S(2)}) copy-start(s32[64,16,128]{2,1,0:T(8,128)} %unknown_ref.1) | copy-start | bytes 1572868
  38.0 9.6 %collective-permute-start.1 = (s16[128,128]{1,0:T(8,128)(2,1)S(1)}, s16[128,128]{1,0:T(8,128)(2,1)S(1)}, u32[]{:S(2)}, u32[]{:S(2)}) collective-permute-start(s16[128,128]{1,0:T(8,128)(2,1)S(1)} %get-tuple-element.14), channel_id=1, source_target_pairs={{0,1},{1,0},{2,3},{3,2},{4,5},{5,4},{6,7},{7,6},{8,9},{9,8},{10,11... | collective-permute-start | bytes 98312 | tf_op jit(solution)/shard_map/ppermute | solution.py:296
  42.9 6.5 %collective-permute-start.2 = (s16[128,128]{1,0:T(8,128)(2,1)S(1)}, s16[128,128]{1,0:T(8,128)(2,1)S(1)}, u32[]{:S(2)}, u32[]{:S(2)}) collective-permute-start(s16[128,128]{1,0:T(8,128)(2,1)S(1)} %get-tuple-element.15), channel_id=1, source_target_pairs={{0,2},{1,3},{2,0},{3,1},{4,6},{5,7},{6,4},{7,5},{8,10},{9,11},{10,... | collective-permute-start | bytes 98312 | tf_op jit(solution)/shard_map/ppermute | solution.py:296
  42.9 6.5 %collective-permute-start.3 = (s16[128,128]{1,0:T(8,128)(2,1)S(1)}, s16[128,128]{1,0:T(8,128)(2,1)S(1)}, u32[]{:S(2)}, u32[]{:S(2)}) collective-permute-start(s16[128,128]{1,0:T(8,128)(2,1)S(1)} %get-tuple-element.16), channel_id=1, source_target_pairs={{0,3},{1,2},{2,1},{3,0},{4,7},{5,6},{6,5},{7,4},{8,11},{9,10},{10,... | collective-permute-start | bytes 98312 | tf_op jit(solution)/shard_map/ppermute | solution.py:296
  46.6 6.0 %collective-permute-start.4 = (s16[128,128]{1,0:T(8,128)(2,1)S(1)}, s16[128,128]{1,0:T(8,128)(2,1)S(1)}, u32[]{:S(2)}, u32[]{:S(2)}) collective-permute-start(s16[128,128]{1,0:T(8,128)(2,1)S(1)} %get-tuple-element.18), channel_id=1, source_target_pairs={{0,1},{1,0},{2,3},{3,2},{4,5},{5,4},{6,7},{7,6},{8,9},{9,8},{10,11... | collective-permute-start | bytes 98312 | tf_op jit(solution)/shard_map/ppermute | solution.py:296
  47.6 5.0 %collective-permute-start.5 = (s16[128,128]{1,0:T(8,128)(2,1)S(1)}, s16[128,128]{1,0:T(8,128)(2,1)S(1)}, u32[]{:S(2)}, u32[]{:S(2)}) collective-permute-start(s16[128,128]{1,0:T(8,128)(2,1)S(1)} %get-tuple-element.19), channel_id=1, source_target_pairs={{0,2},{1,3},{2,0},{3,1},{4,6},{5,7},{6,4},{7,5},{8,10},{9,11},{10,... | collective-permute-start | bytes 98312 | tf_op jit(solution)/shard_map/ppermute | solution.py:296
  47.6 5.0 %collective-permute-start.6 = (s16[128,128]{1,0:T(8,128)(2,1)S(1)}, s16[128,128]{1,0:T(8,128)(2,1)S(1)}, u32[]{:S(2)}, u32[]{:S(2)}) collective-permute-start(s16[128,128]{1,0:T(8,128)(2,1)S(1)} %get-tuple-element.20), channel_id=1, source_target_pairs={{0,3},{1,2},{2,1},{3,0},{4,7},{5,6},{6,5},{7,4},{8,11},{9,10},{10,... | collective-permute-start | bytes 98312 | tf_op jit(solution)/shard_map/ppermute | solution.py:296

commit v5 on v4

--- a/solution.py
+++ b/solution.py
@@ -1,5 +1,3 @@
-import functools
-
 import jax
 import jax.numpy as jnp
 from jax import lax
@@ -83,14 +81,18 @@
     lax.fori_loop(0, own, send, 0, unroll=4)
 
 
-def find_blocks(line_ref, kept_ref, least_gap=0.0, reached_ref=None):
+def bit(place):
+    return jnp.int32((1 << place) - (1 << 32 if place == 31 else 0))
+
+
+def find_blocks(line_ref, kept_ref, size, least_gap=0.0, reached_ref=None):
     sublane = lax.broadcasted_iota(jnp.int32, (ROWS, LANES), 0).astype(jnp.float32)
+    sources = range(0, LINE, size)
     low = []
-    for block in range(BLOCKS):
-        at = PAD + block * BLOCK
-        least = line_ref[at : at + ROWS, :]
-        for group in range(1, GROUPS):
-            least = jnp.minimum(least, line_ref[at + group * ROWS : at + (group + 1) * ROWS, :])
+    for source in sources:
+        least = line_ref[PAD + source : PAD + source + ROWS, :]
+        for at in range(PAD + source + ROWS, PAD + source + size, ROWS):
+            least = jnp.minimum(least, line_ref[at : at + ROWS, :])
         low.append(jnp.broadcast_to(jnp.min(least, axis=0, keepdims=True), (ROWS, LANES)))
     some = jnp.int32(0)
     for first in range(0, BLOCKS, ROWS):
@@ -98,36 +100,38 @@
         if reached_ref is not None:
             bound = jnp.minimum(bound, reached_ref[first : first + ROWS, :])
         floor = []
-        for block in range(BLOCKS):
-            away = jnp.abs(sublane + float(first - block)) * float(BLOCK)
-            far = away + float(BLOCK - 1)
-            near = jnp.maximum(away - float(BLOCK - 1), least_gap)
-            bound = jnp.minimum(bound, low[block] + far * far)
-            floor.append(low[block] + near * near)
+        for source, least in zip(sources, low):
+            after = sublane * float(BLOCK) + float(first * BLOCK - source)
+            far = jnp.maximum(after + float(BLOCK - 1), float(size - 1) - after)
+            near = jnp.maximum(jnp.maximum(after - float(size - 1), -after - float(BLOCK - 1)), least_gap)
+            bound = jnp.minimum(bound, least + far * far)
+            floor.append(least + near * near)
         kept = jnp.zeros((ROWS, 1), jnp.int32)
-        for block in range(BLOCKS):
-            keep = jnp.min(floor[block] - bound, axis=1, keepdims=True) < 0.0
-            kept = kept | jnp.where(keep, 1 << block, 0)
+        for place in range(len(sources)):
+            keep = jnp.min(floor[place] - bound, axis=1, keepdims=True) < 0.0
+            kept = kept | jnp.where(keep, bit(place), 0)
         for row in range(ROWS):
             word = kept[row, 0]
             kept_ref[first + row] = word
-            some = some | jnp.where(word != 0, jnp.int32(1 << (first + row)), 0)
+            some = some | jnp.where(word != 0, bit(first + row), 0)
     return some
 
 
-def lower_block(line_ref, far_ref, table_ref, kept_ref, block, start):
+def lower_block(line_ref, far_ref, table_ref, kept_ref, size, block, start):
+    pieces = size // ROWS
+
     def left(carry):
         return carry[0] != 0
 
     def pair(carry):
         kept, source, best = carry
-        base = pl.multiple_of((block - source) * BLOCK + LINE, BLOCK)
-        row = pl.multiple_of(source * BLOCK, BLOCK) + PAD
+        base = pl.multiple_of(block * BLOCK - source * size + LINE, size)
+        row = pl.multiple_of(source * size, size) + PAD
         kept = kept ^ lax.shift_left(jnp.int32(1), source)
         best = list(best)
         for p in range(ROWS):
-            squares = {k: table_ref[pl.ds(base + (k * ROWS - p), ROWS), :] for k in range(1 - GROUPS, GROUPS)}
-            for q in range(GROUPS):
+            squares = {k: table_ref[pl.ds(base + (k * ROWS - p), ROWS), :] for k in range(1 - pieces, GROUPS)}
+            for q in range(pieces):
                 value = jnp.broadcast_to(line_ref[pl.ds(row + q * ROWS + p, 1), :], (ROWS, LANES))
                 for group in range(GROUPS):
                     best[group] = jnp.minimum(best[group], value + squares[group - q])
@@ -148,20 +152,19 @@
 
 
 def sparse_pass(line_ref, far_ref, table_ref, kept_ref, _):
-    fill_table(table_ref)
-    find_blocks(line_ref, kept_ref)
+    size = BLOCK // 2
+    find_blocks(line_ref, kept_ref, size)
 
     def target(block, _):
         at = pl.multiple_of(block * BLOCK, BLOCK) + PAD
         start = tuple(line_ref[pl.ds(at + group * ROWS, ROWS), :] for group in range(GROUPS))
-        lower_block(line_ref, far_ref, table_ref, kept_ref, block, start)
+        lower_block(line_ref, far_ref, table_ref, kept_ref, size, block, start)
         return 0
 
     lax.fori_loop(0, BLOCKS, target, 0)
 
 
 def dense_pass(line_ref, far_ref, table_ref, kept_ref, reached_ref):
-    fill_table(table_ref)
     margin = jnp.full((PAD, LANES), 3e38, jnp.float32)
     line_ref[:PAD, :] = margin
     line_ref[PAD + LINE :, :] = margin
@@ -193,49 +196,43 @@
         block = 31 - lax.clz(some)
         at = pl.multiple_of(block * BLOCK, BLOCK)
         start = tuple(far_ref[pl.ds(at + group * ROWS, ROWS), :] for group in range(GROUPS))
-        lower_block(line_ref, far_ref, table_ref, kept_ref, block, start)
+        lower_block(line_ref, far_ref, table_ref, kept_ref, BLOCK, block, start)
         return some ^ lax.shift_left(jnp.int32(1), block)
 
-    lax.while_loop(left, target, find_blocks(line_ref, kept_ref, float(ROWS + 1), reached_ref))
+    lax.while_loop(left, target, find_blocks(line_ref, kept_ref, BLOCK, float(ROWS + 1), reached_ref))
 
 
 PASSES = (sparse_pass, dense_pass)
 
 
-def row_kernel(field, place_ref, in_ref, own_ref, *rest):
-    send_refs, (line_ref, far_ref, *scratch) = rest[:-5], rest[-5:]
+def row_kernel(place_ref, in_ref, own_ref, *rest):
+    send_refs, (line_ref, far_ref, table_ref, *scratch) = rest[:-5], rest[-5:]
     chunk = in_ref.shape[2]
-    for piece in range(in_ref.shape[0]):
-        line_ref[PAD + piece * chunk : PAD + (piece + 1) * chunk, :] = decode(in_ref[piece, field])
-    PASSES[field](line_ref, far_ref, *scratch)
-    for step in range(len(send_refs) + 1):
-        part = pl.ds(pl.multiple_of((place_ref[1] ^ step) * LANES, LANES), LANES)
-        value = far_ref[part, :].T
-        if step:
-            send_refs[step - 1][...] = encode(value)
-        else:
-            own_ref[...] = value
-
-
-def gather_lines(place_ref, own_ref, got_refs, line_ref):
-    for step in range(len(got_refs) + 1):
-        part = pl.ds(pl.multiple_of((place_ref[1] ^ step) * LANES, LANES) + PAD, LANES)
-        line_ref[part, :] = decode(got_refs[step - 1][...]) if step else own_ref[...]
+    fill_table(table_ref)
+    for field in range(FIELDS):
+        for piece in range(in_ref.shape[0]):
+            line_ref[PAD + piece * chunk : PAD + (piece + 1) * chunk, :] = decode(in_ref[piece, field])
+        PASSES[field](line_ref, far_ref, table_ref, *scratch)
+        for step in range(len(send_refs) + 1):
+            part = pl.ds(pl.multiple_of((place_ref[1] ^ step) * LANES, LANES), LANES)
+            value = far_ref[part, :].T
+            if step:
+                send_refs[step - 1][field] = encode(value)
+            else:
+                own_ref[field] = value
 
 
 def column_kernel(place_ref, own_ref, *rest):
-    got_refs, (far_ref, line_ref, *scratch) = rest[:-5], rest[-5:]
-    gather_lines(place_ref, own_ref, got_refs, line_ref)
-    PASSES[0](line_ref, far_ref, *scratch)
-
-
-def last_kernel(place_ref, outside_ref, own_ref, *rest):
-    got_refs, (out_ref, line_ref, far_ref, *scratch) = rest[:-6], rest[-6:]
-    gather_lines(place_ref, own_ref, got_refs, line_ref)
-    PASSES[1](line_ref, far_ref, *scratch)
+    got_refs, (out_ref, line_ref, outside_ref, inside_ref, table_ref, *scratch) = rest[:-7], rest[-7:]
+    fill_table(table_ref)
+    for field, far_ref in enumerate((outside_ref, inside_ref)):
+        for step in range(len(got_refs) + 1):
+            part = pl.ds(pl.multiple_of((place_ref[1] ^ step) * LANES, LANES) + PAD, LANES)
+            line_ref[part, :] = decode(got_refs[step - 1][field]) if step else own_ref[field]
+        PASSES[field](line_ref, far_ref, table_ref, *scratch)
     for piece in range(LINE // LANES):
         part = pl.ds(piece * LANES, LANES)
-        signed = voxel_size * (jnp.sqrt(outside_ref[part, :]) - jnp.sqrt(far_ref[part, :]))
+        signed = voxel_size * (jnp.sqrt(outside_ref[part, :]) - jnp.sqrt(inside_ref[part, :]))
         out_ref[:, part] = signed.T
 
 
@@ -279,29 +276,26 @@
     parts = lax.axis_size("yz")
     share = LINE // parts
     line = pltpu.VMEM((LINE + 2 * PAD, LANES), f32)
+    far = pltpu.VMEM((LINE, LANES), f32)
     scratch = [
         pltpu.VMEM((2 * LINE, LANES), f32),
         pltpu.SMEM((BLOCKS,), jnp.int32),
         pltpu.VMEM((BLOCKS, LANES), f32),
     ]
-    lines = [line, pltpu.VMEM((LINE, LANES), f32), *scratch]
-    shapes = (jax.ShapeDtypeStruct((columns, share), f32),)
-    shapes += (jax.ShapeDtypeStruct((columns, share), jnp.int16),) * (parts - 1)
-    settled = []
-    for field in range(FIELDS):
-        own_part, *others = call(
-            functools.partial(row_kernel, field), shapes, lines, place, crossed, scalar=True
-        )
-        got = [
-            lax.ppermute(part, "yz", [(i, i ^ step) for i in range(parts)])
-            for step, part in enumerate(others, 1)
-        ]
-        settled.append((own_part, *got))
-    outside = call(
-        column_kernel, jax.ShapeDtypeStruct((LINE, share), f32), [line, *scratch], place, *settled[0], scalar=True
-    )
+    shapes = (jax.ShapeDtypeStruct((FIELDS, columns, share), f32),)
+    shapes += (jax.ShapeDtypeStruct((FIELDS, columns, share), jnp.int16),) * (parts - 1)
+    own_part, *others = call(row_kernel, shapes, [line, far, *scratch], place, crossed, scalar=True)
+    got = [
+        lax.ppermute(part, "yz", [(i, i ^ step) for i in range(parts)]) for step, part in enumerate(others, 1)
+    ]
     signed = call(
-        last_kernel, jax.ShapeDtypeStruct((share, LINE), f32), lines, place, outside, *settled[1], scalar=True
+        column_kernel,
+        jax.ShapeDtypeStruct((share, LINE), f32),
+        [line, far, far, *scratch],
+        place,
+        own_part,
+        *got,
+        scalar=True,
     )
     return signed[None]
 

time: 55.7 us -> 53.3 us (0.957)
  starting transfers between devices: 13 us -> 8.98 us
  waiting for transfers between devices: 3.73 us -> 7.2 us
  Pallas kernels: 14.5 us -> 12.9 us
    ppermute x6 -> x3, starting transfers between devices: 9.31 us -> 5.33 us  [body(): lax.ppermute(part, 'yz', [(i, i ^ step) for i in range(parts)])]
    ppermute x6 -> x3, waiting for transfers between devices: 0.02 us -> 3.49 us  [body(): lax.ppermute(part, 'yz', [(i, i ^ step) for i in range(parts)])]
    pallas_call x6 -> x4, Pallas kernels: 14.5 us -> 12.9 us  [call(): pl.pallas_call(kernel, out_shape=out_shape, in_specs=in_specs, out_specs=...]
  transfers between devices with their start and end apart: 7 -> 4, of which waited for: 1 -> 3; matrix products, arithmetic and copies ran while one was open for 0% -> 0% of each run, Pallas kernels for 10% -> 0%
where the time goes in v5:
time: 53.3 us; the launch traced here: 53.1 us
  blocking collectives  21.6 us (41%)
  Pallas kernels  12.9 us (24%)
  starting transfers between devices  8.98 us (17%)
  waiting for transfers between devices  7.2 us (14%)
  other arithmetic  1.26 us (2%)
  local copies, waits for them, and re-layouts  1.05 us (2%)
    all_to_all x1, blocking collectives, body(): lax.all_to_all(planes, 'xy', split_axis=0, concat_axis=0, tiled=True)  21.6 us
    pallas_call x4, Pallas kernels, call(): pl.pallas_call(kernel, out_shape=out_shape, in_specs=in_specs, out_specs=...  12.9 us
    ppermute x3, starting transfers between devices, body(): lax.ppermute(part, 'yz', [(i, i ^ step) for i in range(parts)])  5.33 us
    ppermute x1, waiting for transfers between devices, body(): other = lax.ppermute(lowest, 'robot', [(0, 1), (1, 0)])  3.71 us
    ppermute x1, starting transfers between devices, body(): other = lax.ppermute(lowest, 'robot', [(0, 1), (1, 0)])  3.65 us
    ppermute x3, waiting for transfers between devices, body(): lax.ppermute(part, 'yz', [(i, i ^ step) for i in range(parts)])  3.49 us
    reduce_min x1, other arithmetic, body(): lowest = jnp.min(seed_cost, axis=0)  1.19 us
  transfers between devices with their start and end apart: 4, of which 3 were waited for; matrix products, arithmetic and copies ran while one was open for 0% of the time, Pallas kernels for 0%

profile of v5, /device:TPU:1, one launch (start us, length us, event | category | flops | bytes accessed | tf_op | source)
XLA Modules:
  0.0 53.1 jit_solution(15256433447192029361)
XLA Ops:
  0.0 0.0 copy-start
  0.0 1.2 %reduce_min.9.mine_ref = bf16[64,16,128]{2,1,0:T(8,128)(2,1)S(1)} reduce(bf16[2,64,16,128]{3,2,1,0:T(8,128)(2,1)} %param.3, bf16[]{:T(256)} %constant.11.clone.1), dimensions={0}, to_apply=%region_0.0 | reduce | flops 131072 | bytes 786434 | tf_op jit(solution)/shard_map/reduce_min | solution.py:259
  1.2 3.6 %collective-permute-start = (bf16[64,16,128]{2,1,0:T(8,128)(2,1)S(1)}, bf16[64,16,128]{2,1,0:T(8,128)(2,1)S(1)}, u32[]{:S(2)}, u32[]{:S(2)}) collective-permute-start(bf16[64,16,128]{2,1,0:T(8,128)(2,1)S(1)} %reduce_min.9.mine_ref), channel_id=1, source_target_pairs={{0,128},{128,0},{1,129},{129,1},{2,130},{130,2},{3,131},{131,3},{4... | collective-permute-start | bytes 786440 | tf_op jit(solution)/shard_map/ppermute | solution.py:260
  4.8 0.0 copy-done
  4.8 0.0 copy-start.1
  4.8 1.0 %copy-done.1 = s32[64,16,128]{2,1,0:T(8,128)S(1)} copy-done((s32[64,16,128]{2,1,0:T(8,128)S(1)}, s32[64,16,128]{2,1,0:T(8,128)}, u32[]{:S(2)}) %copy-start.1) | copy-done | bytes 524312
  5.9 0.1 shard_map.37.raise_ref
  6.0 0.1 pad_add_fusion.place_ref
  6.1 3.7 %collective-permute-done.other_ref = bf16[64,16,128]{2,1,0:T(8,128)(2,1)S(1)} collective-permute-done((bf16[64,16,128]{2,1,0:T(8,128)(2,1)S(1)}, bf16[64,16,128]{2,1,0:T(8,128)(2,1)S(1)}, u32[]{:S(2)}, u32[]{:S(2)}) %collective-permute-start) | collective-permute-done | bytes 262176 | tf_op jit(solution)/shard_map/ppermute | solution.py:260
  9.8 3.4 %shard_map.38 = s16[32,2,16,128]{3,2,1,0:T(8,128)(2,1)S(1)} custom-call(s32[2]{0:T(128)S(1)} %pad_add_fusion.place_ref, bf16[64,16,128]{2,1,0:T(8,128)(2,1)S(1)} %reduce_min.9.mine_ref, bf16[64,16,128]{2,1,0:T(8,128)(2,1)S(1)} %collective-permute-done.other_ref, f32[2,64,16,128]{3,2,1,0:T(8,128)S(1)} %shard_map.37.raise_ref), custom_call_target="tpu_custom_call" | custom-call | flops 4000000 | bytes 1048576 | tf_op jit(solution)/shard_map/pallas_call | solution.py:248
  13.2 21.6 %all_to_all.5.in_ref = s16[32,2,16,128]{3,2,1,0:T(8,128)(2,1)S(1)} all-to-all(s16[32,2,16,128]{3,2,1,0:T(8,128)(2,1)S(1)} %shard_map.38), channel_id=1, replica_groups=mesh['robot'=2,'xy'=32,'yz'=4] {'xy'}, dimensions={0} | all-to-all | bytes 524288 | tf_op jit(solution)/shard_map/all_to_all | solution.py:274
  34.8 5.0 %shard_map.39 = (f32[2,128,128]{2,1,0:T(8,128)S(1)}, s16[2,128,128]{2,1,0:T(8,128)(2,1)S(1)}, s16[2,128,128]{2,1,0:T(8,128)(2,1)S(1)}, s16[2,128,128]{2,1,0:T(8,128)(2,1)S(1)}) custom-call(s32[2]{0:T(128)S(1)} %pad_add_fusion.place_ref, s16[32,2,16,128]{3,2,1,0:T(8,128)(2,1)S(1)} %all_to_all.5.in_ref), custom_call_target="tpu_custom_call" | custom-call | flops 4000000 | bytes 1048576 | tf_op jit(solution)/shard_map/pallas_call | solution.py:248
  39.8 3.6 %collective-permute-start.1 = (s16[2,128,128]{2,1,0:T(8,128)(2,1)S(1)}, s16[2,128,128]{2,1,0:T(8,128)(2,1)S(1)}, u32[]{:S(2)}, u32[]{:S(2)}) collective-permute-start(s16[2,128,128]{2,1,0:T(8,128)(2,1)S(1)} %get-tuple-element.10), channel_id=1, source_target_pairs={{0,1},{1,0},{2,3},{3,2},{4,5},{5,4},{6,7},{7,6},{8,9},{9,8},{10,11... | collective-permute-start | bytes 196616 | tf_op jit(solution)/shard_map/ppermute | solution.py:289
  43.4 0.0 collective-permute-start.2
  43.4 1.7 %collective-permute-start.3 = (s16[2,128,128]{2,1,0:T(8,128)(2,1)S(1)}, s16[2,128,128]{2,1,0:T(8,128)(2,1)S(1)}, u32[]{:S(2)}, u32[]{:S(2)}) collective-permute-start(s16[2,128,128]{2,1,0:T(8,128)(2,1)S(1)} %get-tuple-element.12), channel_id=1, source_target_pairs={{0,3},{1,2},{2,1},{3,0},{4,7},{5,6},{6,5},{7,4},{8,11},{9,10},{10,... | collective-permute-start | bytes 196616 | tf_op jit(solution)/shard_map/ppermute | solution.py:289
  45.1 0.0 collective-permute-done.1.rest_0_
  45.1 1.8 %collective-permute-done.2.rest_1_ = s16[2,128,128]{2,1,0:T(8,128)(2,1)S(1)} collective-permute-done((s16[2,128,128]{2,1,0:T(8,128)(2,1)S(1)}, s16[2,128,128]{2,1,0:T(8,128)(2,1)S(1)}, u32[]{:S(2)}, u32[]{:S(2)}) %collective-permute-start.2) | collective-permute-done | bytes 65568 | tf_op jit(solution)/shard_map/ppermute | solution.py:289
  46.9 1.7 %collective-permute-done.3.rest_2_ = s16[2,128,128]{2,1,0:T(8,128)(2,1)S(1)} collective-permute-done((s16[2,128,128]{2,1,0:T(8,128)(2,1)S(1)}, s16[2,128,128]{2,1,0:T(8,128)(2,1)S(1)}, u32[]{:S(2)}, u32[]{:S(2)}) %collective-permute-start.3) | collective-permute-done | bytes 65568 | tf_op jit(solution)/shard_map/ppermute | solution.py:289
  48.6 4.5 %shard_map.40 = f32[128,512]{1,0:T(8,128)} custom-call(s32[2]{0:T(128)S(1)} %pad_add_fusion.place_ref, f32[2,128,128]{2,1,0:T(8,128)S(1)} %get-tuple-element.9.own_ref, s16[2,128,128]{2,1,0:T(8,128)(2,1)S(1)} %collective-permute-done.1.rest_0_, s16[2,128,128]{2,1,0:T(8,128)(2,1)S(1)} %collective-permute-done.2.rest_1_, ...), custom_call_target="tpu_custom_call" | custom-call | flops 4000000 | bytes 1048576 | tf_op jit(solution)/shard_map/pallas_call | solution.py:248
Async XLA Ops:
  0.0 4.8 %copy-start = (s32[64,16,128]{2,1,0:T(8,128)S(1)}, s32[64,16,128]{2,1,0:T(8,128)}, u32[]{:S(2)}) copy-start(s32[64,16,128]{2,1,0:T(8,128)} %occupied_ref.1) | copy-start | bytes 1572868
  1.2 8.6 %collective-permute-start = (bf16[64,16,128]{2,1,0:T(8,128)(2,1)S(1)}, bf16[64,16,128]{2,1,0:T(8,128)(2,1)S(1)}, u32[]{:S(2)}, u32[]{:S(2)}) collective-permute-start(bf16[64,16,128]{2,1,0:T(8,128)(2,1)S(1)} %reduce_min.9.mine_ref), channel_id=1, source_target_pairs={{0,128},{128,0},{1,129},{129,1},{2,130},{130,2},{3,131},{131,3},{4... | collective-permute-start | bytes 786440 | tf_op jit(solution)/shard_map/ppermute | solution.py:260
  4.8 1.0 %copy-start.1 = (s32[64,16,128]{2,1,0:T(8,128)S(1)}, s32[64,16,128]{2,1,0:T(8,128)}, u32[]{:S(2)}) copy-start(s32[64,16,128]{2,1,0:T(8,128)} %unknown_ref.1) | copy-start | bytes 1572868
  39.8 5.3 %collective-permute-start.1 = (s16[2,128,128]{2,1,0:T(8,128)(2,1)S(1)}, s16[2,128,128]{2,1,0:T(8,128)(2,1)S(1)}, u32[]{:S(2)}, u32[]{:S(2)}) collective-permute-start(s16[2,128,128]{2,1,0:T(8,128)(2,1)S(1)} %get-tuple-element.10), channel_id=1, source_target_pairs={{0,1},{1,0},{2,3},{3,2},{4,5},{5,4},{6,7},{7,6},{8,9},{9,8},{10,11... | collective-permute-start | bytes 196616 | tf_op jit(solution)/shard_map/ppermute | solution.py:289
  43.4 3.5 %collective-permute-start.2 = (s16[2,128,128]{2,1,0:T(8,128)(2,1)S(1)}, s16[2,128,128]{2,1,0:T(8,128)(2,1)S(1)}, u32[]{:S(2)}, u32[]{:S(2)}) collective-permute-start(s16[2,128,128]{2,1,0:T(8,128)(2,1)S(1)} %get-tuple-element.11), channel_id=1, source_target_pairs={{0,2},{1,3},{2,0},{3,1},{4,6},{5,7},{6,4},{7,5},{8,10},{9,11},{10,... | collective-permute-start | bytes 196616 | tf_op jit(solution)/shard_map/ppermute | solution.py:289
  43.4 5.2 %collective-permute-start.3 = (s16[2,128,128]{2,1,0:T(8,128)(2,1)S(1)}, s16[2,128,128]{2,1,0:T(8,128)(2,1)S(1)}, u32[]{:S(2)}, u32[]{:S(2)}) collective-permute-start(s16[2,128,128]{2,1,0:T(8,128)(2,1)S(1)} %get-tuple-element.12), channel_id=1, source_target_pairs={{0,3},{1,2},{2,1},{3,0},{4,7},{5,6},{6,5},{7,4},{8,11},{9,10},{10,... | collective-permute-start | bytes 196616 | tf_op jit(solution)/shard_map/ppermute | solution.py:289

commit v6 on v4

--- a/solution.py
+++ b/solution.py
@@ -44,8 +44,8 @@
     lax.fori_loop(0, occupied_ref.shape[0], masks, 0, unroll=4)
 
 
-def depth_kernel(place_ref, mine_ref, other_ref, raise_ref, out_ref, field_ref, best_ref):
-    half = place_ref[0]
+def depth_kernel(mine_ref, other_ref, raise_ref, out_ref, field_ref, best_ref):
+    half = lax.axis_index("robot")
     depth = mine_ref.shape[0]
     own = out_ref.shape[0]
 
@@ -83,14 +83,18 @@
     lax.fori_loop(0, own, send, 0, unroll=4)
 
 
-def find_blocks(line_ref, kept_ref, least_gap=0.0, reached_ref=None):
+def bit(place):
+    return jnp.int32((1 << place) - (1 << 32 if place == 31 else 0))
+
+
+def find_blocks(line_ref, kept_ref, size, least_gap=0.0, reached_ref=None):
     sublane = lax.broadcasted_iota(jnp.int32, (ROWS, LANES), 0).astype(jnp.float32)
+    sources = range(0, LINE, size)
     low = []
-    for block in range(BLOCKS):
-        at = PAD + block * BLOCK
-        least = line_ref[at : at + ROWS, :]
-        for group in range(1, GROUPS):
-            least = jnp.minimum(least, line_ref[at + group * ROWS : at + (group + 1) * ROWS, :])
+    for source in sources:
+        least = line_ref[PAD + source : PAD + source + ROWS, :]
+        for at in range(PAD + source + ROWS, PAD + source + size, ROWS):
+            least = jnp.minimum(least, line_ref[at : at + ROWS, :])
         low.append(jnp.broadcast_to(jnp.min(least, axis=0, keepdims=True), (ROWS, LANES)))
     some = jnp.int32(0)
     for first in range(0, BLOCKS, ROWS):
@@ -98,36 +102,38 @@
         if reached_ref is not None:
             bound = jnp.minimum(bound, reached_ref[first : first + ROWS, :])
         floor = []
-        for block in range(BLOCKS):
-            away = jnp.abs(sublane + float(first - block)) * float(BLOCK)
-            far = away + float(BLOCK - 1)
-            near = jnp.maximum(away - float(BLOCK - 1), least_gap)
-            bound = jnp.minimum(bound, low[block] + far * far)
-            floor.append(low[block] + near * near)
+        for source, least in zip(sources, low):
+            after = sublane * float(BLOCK) + float(first * BLOCK - source)
+            far = jnp.maximum(after + float(BLOCK - 1), float(size - 1) - after)
+            near = jnp.maximum(jnp.maximum(after - float(size - 1), -after - float(BLOCK - 1)), least_gap)
+            bound = jnp.minimum(bound, least + far * far)
+            floor.append(least + near * near)
         kept = jnp.zeros((ROWS, 1), jnp.int32)
-        for block in range(BLOCKS):
-            keep = jnp.min(floor[block] - bound, axis=1, keepdims=True) < 0.0
-            kept = kept | jnp.where(keep, 1 << block, 0)
+        for place in range(len(sources)):
+            keep = jnp.min(floor[place] - bound, axis=1, keepdims=True) < 0.0
+            kept = kept | jnp.where(keep, bit(place), 0)
         for row in range(ROWS):
             word = kept[row, 0]
             kept_ref[first + row] = word
-            some = some | jnp.where(word != 0, jnp.int32(1 << (first + row)), 0)
+            some = some | jnp.where(word != 0, bit(first + row), 0)
     return some
 
 
-def lower_block(line_ref, far_ref, table_ref, kept_ref, block, start):
+def lower_block(line_ref, far_ref, table_ref, kept_ref, size, block, start):
+    pieces = size // ROWS
+
     def left(carry):
         return carry[0] != 0
 
     def pair(carry):
         kept, source, best = carry
-        base = pl.multiple_of((block - source) * BLOCK + LINE, BLOCK)
-        row = pl.multiple_of(source * BLOCK, BLOCK) + PAD
+        base = pl.multiple_of(block * BLOCK - source * size + LINE, size)
+        row = pl.multiple_of(source * size, size) + PAD
         kept = kept ^ lax.shift_left(jnp.int32(1), source)
         best = list(best)
         for p in range(ROWS):
-            squares = {k: table_ref[pl.ds(base + (k * ROWS - p), ROWS), :] for k in range(1 - GROUPS, GROUPS)}
-            for q in range(GROUPS):
+            squares = {k: table_ref[pl.ds(base + (k * ROWS - p), ROWS), :] for k in range(1 - pieces, GROUPS)}
+            for q in range(pieces):
                 value = jnp.broadcast_to(line_ref[pl.ds(row + q * ROWS + p, 1), :], (ROWS, LANES))
                 for group in range(GROUPS):
                     best[group] = jnp.minimum(best[group], value + squares[group - q])
@@ -148,13 +154,14 @@
 
 
 def sparse_pass(line_ref, far_ref, table_ref, kept_ref, _):
+    size = BLOCK // 2
     fill_table(table_ref)
-    find_blocks(line_ref, kept_ref)
+    find_blocks(line_ref, kept_ref, size)
 
     def target(block, _):
         at = pl.multiple_of(block * BLOCK, BLOCK) + PAD
         start = tuple(line_ref[pl.ds(at + group * ROWS, ROWS), :] for group in range(GROUPS))
-        lower_block(line_ref, far_ref, table_ref, kept_ref, block, start)
+        lower_block(line_ref, far_ref, table_ref, kept_ref, size, block, start)
         return 0
 
     lax.fori_loop(0, BLOCKS, target, 0)
@@ -193,23 +200,23 @@
         block = 31 - lax.clz(some)
         at = pl.multiple_of(block * BLOCK, BLOCK)
         start = tuple(far_ref[pl.ds(at + group * ROWS, ROWS), :] for group in range(GROUPS))
-        lower_block(line_ref, far_ref, table_ref, kept_ref, block, start)
+        lower_block(line_ref, far_ref, table_ref, kept_ref, BLOCK, block, start)
         return some ^ lax.shift_left(jnp.int32(1), block)
 
-    lax.while_loop(left, target, find_blocks(line_ref, kept_ref, float(ROWS + 1), reached_ref))
+    lax.while_loop(left, target, find_blocks(line_ref, kept_ref, BLOCK, float(ROWS + 1), reached_ref))
 
 
 PASSES = (sparse_pass, dense_pass)
 
 
-def row_kernel(field, place_ref, in_ref, own_ref, *rest):
+def row_kernel(field, in_ref, own_ref, *rest):
     send_refs, (line_ref, far_ref, *scratch) = rest[:-5], rest[-5:]
     chunk = in_ref.shape[2]
     for piece in range(in_ref.shape[0]):
         line_ref[PAD + piece * chunk : PAD + (piece + 1) * chunk, :] = decode(in_ref[piece, field])
     PASSES[field](line_ref, far_ref, *scratch)
     for step in range(len(send_refs) + 1):
-        part = pl.ds(pl.multiple_of((place_ref[1] ^ step) * LANES, LANES), LANES)
+        part = pl.ds(pl.multiple_of((lax.axis_index("yz") ^ step) * LANES, LANES), LANES)
         value = far_ref[part, :].T
         if step:
             send_refs[step - 1][...] = encode(value)
@@ -217,21 +224,21 @@
             own_ref[...] = value
 
 
-def gather_lines(place_ref, own_ref, got_refs, line_ref):
+def gather_lines(own_ref, got_refs, line_ref):
     for step in range(len(got_refs) + 1):
-        part = pl.ds(pl.multiple_of((place_ref[1] ^ step) * LANES, LANES) + PAD, LANES)
+        part = pl.ds(pl.multiple_of((lax.axis_index("yz") ^ step) * LANES, LANES) + PAD, LANES)
         line_ref[part, :] = decode(got_refs[step - 1][...]) if step else own_ref[...]
 
 
-def column_kernel(place_ref, own_ref, *rest):
+def column_kernel(own_ref, *rest):
     got_refs, (far_ref, line_ref, *scratch) = rest[:-5], rest[-5:]
-    gather_lines(place_ref, own_ref, got_refs, line_ref)
+    gather_lines(own_ref, got_refs, line_ref)
     PASSES[0](line_ref, far_ref, *scratch)
 
 
-def last_kernel(place_ref, outside_ref, own_ref, *rest):
+def last_kernel(outside_ref, own_ref, *rest):
     got_refs, (out_ref, line_ref, far_ref, *scratch) = rest[:-6], rest[-6:]
-    gather_lines(place_ref, own_ref, got_refs, line_ref)
+    gather_lines(own_ref, got_refs, line_ref)
     PASSES[1](line_ref, far_ref, *scratch)
     for piece in range(LINE // LANES):
         part = pl.ds(piece * LANES, LANES)
@@ -243,22 +250,19 @@
     depth, rows, columns = occupied.shape
     own = depth // lax.axis_size("robot")
     vmem = pl.BlockSpec(memory_space=pltpu.VMEM)
-    smem = pl.BlockSpec(memory_space=pltpu.SMEM)
     f32 = jnp.float32
 
-    def call(kernel, out_shape, scratch, *args, scalar=False, work=4e6):
-        in_specs = [smem if scalar and n == 0 else vmem for n in range(len(args))]
+    def call(kernel, out_shape, scratch, *args, work=4e6):
         return pl.pallas_call(
             kernel,
             out_shape=out_shape,
-            in_specs=in_specs,
+            in_specs=[vmem] * len(args),
             out_specs=jax.tree.map(lambda _: vmem, out_shape),
             scratch_shapes=scratch,
             compiler_params=pltpu.CompilerParams(vmem_limit_bytes=16 * 2**20),
             cost_estimate=pl.CostEstimate(flops=int(work), bytes_accessed=2**20, transcendentals=0),
         )(*args)
 
-    place = jnp.stack([lax.axis_index("robot"), lax.axis_index("yz")]).astype(jnp.int32)
     lowest = jnp.min(seed_cost, axis=0)
     other = lax.ppermute(lowest, "robot", [(0, 1), (1, 0)])
     raised = call(
@@ -268,11 +272,9 @@
         depth_kernel,
         jax.ShapeDtypeStruct((own, FIELDS, rows, columns), jnp.int16),
         [pltpu.VMEM((FIELDS, depth, rows, columns), f32), pltpu.VMEM((FIELDS, own, rows, columns), f32)],
-        place,
         lowest,
         other,
         raised,
-        scalar=True,
     )
     crossed = lax.all_to_all(planes, "xy", split_axis=0, concat_axis=0, tiled=True)
 
@@ -290,7 +292,7 @@
     settled = []
     for field in range(FIELDS):
         own_part, *others = call(
-            functools.partial(row_kernel, field), shapes, lines, place, crossed, scalar=True
+            functools.partial(row_kernel, field), shapes, lines, crossed
         )
         got = [
             lax.ppermute(part, "yz", [(i, i ^ step) for i in range(parts)])
@@ -298,10 +300,10 @@
         ]
         settled.append((own_part, *got))
     outside = call(
-        column_kernel, jax.ShapeDtypeStruct((LINE, share), f32), [line, *scratch], place, *settled[0], scalar=True
+        column_kernel, jax.ShapeDtypeStruct((LINE, share), f32), [line, *scratch], *settled[0]
     )
     signed = call(
-        last_kernel, jax.ShapeDtypeStruct((share, LINE), f32), lines, place, outside, *settled[1], scalar=True
+        last_kernel, jax.ShapeDtypeStruct((share, LINE), f32), lines, outside, *settled[1]
     )
     return signed[None]
 

time: 55.7 us -> 51.4 us (0.923); the launches traced: 55.2 us -> 52.4 us
  Pallas kernels: 14.5 us -> 12.3 us
  starting transfers between devices: 13 us -> 12.3 us
    pallas_call x6, Pallas kernels: 14.5 us -> 12.3 us  [call(): pl.pallas_call(kernel, out_shape=out_shape, in_specs=[vmem] * len(args),...]
    ppermute x6, starting transfers between devices: 9.31 us -> 8.69 us  [body(): lax.ppermute(part, 'yz', [(i, i ^ step) for i in range(parts)])]
  transfers between devices with their start and end apart: 7 -> 7, of which waited for: 1 -> 1; matrix products, arithmetic and copies ran while one was open for 0% -> 0% of each run, Pallas kernels for 10% -> 8%
where the time goes in v6:
time: 51.4 us; the launch traced here: 52.4 us
  blocking collectives  21.6 us (42%)
  starting transfers between devices  12.3 us (24%)
  Pallas kernels  12.3 us (24%)
  waiting for transfers between devices  3.81 us (7%)
  other arithmetic  1.19 us (2%)
  local copies, waits for them, and re-layouts  1.05 us (2%)
    all_to_all x1, blocking collectives, body(): lax.all_to_all(planes, 'xy', split_axis=0, concat_axis=0, tiled=True)  21.6 us
    pallas_call x6, Pallas kernels, call(): pl.pallas_call(kernel, out_shape=out_shape, in_specs=[vmem] * len(args),...  12.3 us
    ppermute x6, starting transfers between devices, body(): lax.ppermute(part, 'yz', [(i, i ^ step) for i in range(parts)])  8.69 us
    ppermute x1, waiting for transfers between devices, body(): other = lax.ppermute(lowest, 'robot', [(0, 1), (1, 0)])  3.79 us
    ppermute x1, starting transfers between devices, body(): other = lax.ppermute(lowest, 'robot', [(0, 1), (1, 0)])  3.65 us
    reduce_min x1, other arithmetic, body(): lowest = jnp.min(seed_cost, axis=0)  1.19 us
    unnamed x4, local copies, waits for them, and re-layouts  1.05 us
  transfers between devices with their start and end apart: 7, of which 1 were waited for; matrix products, arithmetic and copies ran while one was open for 0% of the time, Pallas kernels for 8%

profile of v6, /device:TPU:1, one launch (start us, length us, event | category | flops | bytes accessed | tf_op | source)
XLA Modules:
  0.0 52.4 jit_solution(16871989939256147556)
XLA Ops:
  0.0 1.2 %reduce_min.9.mine_ref = bf16[64,16,128]{2,1,0:T(8,128)(2,1)S(1)} reduce(bf16[2,64,16,128]{3,2,1,0:T(8,128)(2,1)} %param.3, bf16[]{:T(256)} %constant.0.clone.1), dimensions={0}, to_apply=%region_0.0 | reduce | flops 131072 | bytes 786434 | tf_op jit(solution)/shard_map/reduce_min | solution.py:266
  1.2 3.6 %collective-permute-start = (bf16[64,16,128]{2,1,0:T(8,128)(2,1)S(1)}, bf16[64,16,128]{2,1,0:T(8,128)(2,1)S(1)}, u32[]{:S(2)}, u32[]{:S(2)}) collective-permute-start(bf16[64,16,128]{2,1,0:T(8,128)(2,1)S(1)} %reduce_min.9.mine_ref), channel_id=1, source_target_pairs={{0,128},{128,0},{1,129},{129,1},{2,130},{130,2},{3,131},{131,3},{4... | collective-permute-start | bytes 786440 | tf_op jit(solution)/shard_map/ppermute | solution.py:267
  4.8 0.0 copy-done
  4.8 1.0 %copy-done.1 = s32[64,16,128]{2,1,0:T(8,128)S(1)} copy-done((s32[64,16,128]{2,1,0:T(8,128)S(1)}, s32[64,16,128]{2,1,0:T(8,128)}, u32[]{:S(2)}) %copy-start.1) | copy-done | bytes 524312
  5.9 0.1 shard_map.37.raise_ref
  6.0 3.8 %collective-permute-done.other_ref = bf16[64,16,128]{2,1,0:T(8,128)(2,1)S(1)} collective-permute-done((bf16[64,16,128]{2,1,0:T(8,128)(2,1)S(1)}, bf16[64,16,128]{2,1,0:T(8,128)(2,1)S(1)}, u32[]{:S(2)}, u32[]{:S(2)}) %collective-permute-start) | collective-permute-done | bytes 262176 | tf_op jit(solution)/shard_map/ppermute | solution.py:267
  9.8 2.8 %shard_map.38 = s16[32,2,16,128]{3,2,1,0:T(8,128)(2,1)S(1)} custom-call(bf16[64,16,128]{2,1,0:T(8,128)(2,1)S(1)} %reduce_min.9.mine_ref, bf16[64,16,128]{2,1,0:T(8,128)(2,1)S(1)} %collective-permute-done.other_ref, f32[2,64,16,128]{3,2,1,0:T(8,128)S(1)} %shard_map.37.raise_ref), custom_call_target="tpu_custom_call" | custom-call | flops 4000000 | bytes 1048576 | tf_op jit(solution)/shard_map/pallas_call | solution.py:256
  12.6 21.6 %all_to_all.5.in_ref = s16[32,2,16,128]{3,2,1,0:T(8,128)(2,1)S(1)} all-to-all(s16[32,2,16,128]{3,2,1,0:T(8,128)(2,1)S(1)} %shard_map.38), channel_id=1, replica_groups=mesh['robot'=2,'xy'=32,'yz'=4] {'xy'}, dimensions={0} | all-to-all | bytes 524288 | tf_op jit(solution)/shard_map/all_to_all | solution.py:279
  34.3 2.8 %shard_map.39 = (f32[128,128]{1,0:T(8,128)S(1)}, s16[128,128]{1,0:T(8,128)(2,1)S(1)}, s16[128,128]{1,0:T(8,128)(2,1)S(1)}, s16[128,128]{1,0:T(8,128)(2,1)S(1)}) custom-call(s16[32,2,16,128]{3,2,1,0:T(8,128)(2,1)S(1)} %all_to_all.5.in_ref), custom_call_target="tpu_custom_call" | custom-call | flops 4000000 | bytes 1048576 | tf_op jit(solution)/shard_map/pallas_call | solution.py:256
  37.0 4.7 %collective-permute-start.1 = (s16[128,128]{1,0:T(8,128)(2,1)S(1)}, s16[128,128]{1,0:T(8,128)(2,1)S(1)}, u32[]{:S(2)}, u32[]{:S(2)}) collective-permute-start(s16[128,128]{1,0:T(8,128)(2,1)S(1)} %get-tuple-element.14), channel_id=1, source_target_pairs={{0,1},{1,0},{2,3},{3,2},{4,5},{5,4},{6,7},{7,6},{8,9},{9,8},{10,11... | collective-permute-start | bytes 98312 | tf_op jit(solution)/shard_map/ppermute | solution.py:298
  41.8 0.4 collective-permute-start.2
  42.1 1.4 %collective-permute-start.3 = (s16[128,128]{1,0:T(8,128)(2,1)S(1)}, s16[128,128]{1,0:T(8,128)(2,1)S(1)}, u32[]{:S(2)}, u32[]{:S(2)}) collective-permute-start(s16[128,128]{1,0:T(8,128)(2,1)S(1)} %get-tuple-element.16), channel_id=1, source_target_pairs={{0,3},{1,2},{2,1},{3,0},{4,7},{5,6},{6,5},{7,4},{8,11},{9,10},{10,... | collective-permute-start | bytes 98312 | tf_op jit(solution)/shard_map/ppermute | solution.py:298
  43.5 1.8 %shard_map.41 = (f32[128,128]{1,0:T(8,128)S(1)}, s16[128,128]{1,0:T(8,128)(2,1)S(1)}, s16[128,128]{1,0:T(8,128)(2,1)S(1)}, s16[128,128]{1,0:T(8,128)(2,1)S(1)}) custom-call(s16[32,2,16,128]{3,2,1,0:T(8,128)(2,1)S(1)} %all_to_all.5.in_ref), custom_call_target="tpu_custom_call" | custom-call | flops 4000000 | bytes 1048576 | tf_op jit(solution)/shard_map/pallas_call | solution.py:256
  45.3 0.4 collective-permute-start.4
  45.7 0.3 collective-permute-start.5
  46.0 0.0 collective-permute-done.1.rest_0_
  46.0 1.5 %collective-permute-start.6 = (s16[128,128]{1,0:T(8,128)(2,1)S(1)}, s16[128,128]{1,0:T(8,128)(2,1)S(1)}, u32[]{:S(2)}, u32[]{:S(2)}) collective-permute-start(s16[128,128]{1,0:T(8,128)(2,1)S(1)} %get-tuple-element.20), channel_id=1, source_target_pairs={{0,3},{1,2},{2,1},{3,0},{4,7},{5,6},{6,5},{7,4},{8,11},{9,10},{10,... | collective-permute-start | bytes 98312 | tf_op jit(solution)/shard_map/ppermute | solution.py:298
  47.5 0.0 collective-permute-done.2.rest_1_
  47.5 0.0 collective-permute-done.3.rest_2_
  47.6 2.5 %shard_map.40.outside_ref = f32[512,128]{1,0:T(8,128)S(1)} custom-call(f32[128,128]{1,0:T(8,128)S(1)} %get-tuple-element.13.own_ref, s16[128,128]{1,0:T(8,128)(2,1)S(1)} %collective-permute-done.1.rest_0_, s16[128,128]{1,0:T(8,128)(2,1)S(1)} %collective-permute-done.2.rest_1_, s16[128,128]{1,0:T(8,128)(2,1)S(1)} %collective-permute-done.3.rest_2_), custom_call_target="tpu_custom_call" | custom-call | flops 4000000 | bytes 1048576 | tf_op jit(solution)/shard_map/pallas_call | solution.py:256
  50.0 0.0 collective-permute-done.4.rest_0_
  50.1 0.0 collective-permute-done.5.rest_1_
  50.1 0.0 collective-permute-done.6.rest_2_
  50.1 2.3 %shard_map.42 = f32[128,512]{1,0:T(8,128)} custom-call(f32[512,128]{1,0:T(8,128)S(1)} %shard_map.40.outside_ref, f32[128,128]{1,0:T(8,128)S(1)} %get-tuple-element.17.own_ref, s16[128,128]{1,0:T(8,128)(2,1)S(1)} %collective-permute-done.4.rest_0_, s16[128,128]{1,0:T(8,128)(2,1)S(1)} %collective-permute-done.5.rest_1_, ...), custom_call_target="tpu_custom_call" | custom-call | flops 4000000 | bytes 1048576 | tf_op jit(solution)/shard_map/pallas_call | solution.py:256
  (2 shorter events, 0.0 us)
Async XLA Ops:
  0.0 4.8 %copy-start = (s32[64,16,128]{2,1,0:T(8,128)S(1)}, s32[64,16,128]{2,1,0:T(8,128)}, u32[]{:S(2)}) copy-start(s32[64,16,128]{2,1,0:T(8,128)} %occupied_ref.1) | copy-start | bytes 1572868
  1.2 8.6 %collective-permute-start = (bf16[64,16,128]{2,1,0:T(8,128)(2,1)S(1)}, bf16[64,16,128]{2,1,0:T(8,128)(2,1)S(1)}, u32[]{:S(2)}, u32[]{:S(2)}) collective-permute-start(bf16[64,16,128]{2,1,0:T(8,128)(2,1)S(1)} %reduce_min.9.mine_ref), channel_id=1, source_target_pairs={{0,128},{128,0},{1,129},{129,1},{2,130},{130,2},{3,131},{131,3},{4... | collective-permute-start | bytes 786440 | tf_op jit(solution)/shard_map/ppermute | solution.py:267
  4.8 1.0 %copy-start.1 = (s32[64,16,128]{2,1,0:T(8,128)S(1)}, s32[64,16,128]{2,1,0:T(8,128)}, u32[]{:S(2)}) copy-start(s32[64,16,128]{2,1,0:T(8,128)} %unknown_ref.1) | copy-start | bytes 1572868
  37.0 9.0 %collective-permute-start.1 = (s16[128,128]{1,0:T(8,128)(2,1)S(1)}, s16[128,128]{1,0:T(8,128)(2,1)S(1)}, u32[]{:S(2)}, u32[]{:S(2)}) collective-permute-start(s16[128,128]{1,0:T(8,128)(2,1)S(1)} %get-tuple-element.14), channel_id=1, source_target_pairs={{0,1},{1,0},{2,3},{3,2},{4,5},{5,4},{6,7},{7,6},{8,9},{9,8},{10,11... | collective-permute-start | bytes 98312 | tf_op jit(solution)/shard_map/ppermute | solution.py:298
  41.8 5.8 %collective-permute-start.2 = (s16[128,128]{1,0:T(8,128)(2,1)S(1)}, s16[128,128]{1,0:T(8,128)(2,1)S(1)}, u32[]{:S(2)}, u32[]{:S(2)}) collective-permute-start(s16[128,128]{1,0:T(8,128)(2,1)S(1)} %get-tuple-element.15), channel_id=1, source_target_pairs={{0,2},{1,3},{2,0},{3,1},{4,6},{5,7},{6,4},{7,5},{8,10},{9,11},{10,... | collective-permute-start | bytes 98312 | tf_op jit(solution)/shard_map/ppermute | solution.py:298
  42.1 5.4 %collective-permute-start.3 = (s16[128,128]{1,0:T(8,128)(2,1)S(1)}, s16[128,128]{1,0:T(8,128)(2,1)S(1)}, u32[]{:S(2)}, u32[]{:S(2)}) collective-permute-start(s16[128,128]{1,0:T(8,128)(2,1)S(1)} %get-tuple-element.16), channel_id=1, source_target_pairs={{0,3},{1,2},{2,1},{3,0},{4,7},{5,6},{6,5},{7,4},{8,11},{9,10},{10,... | collective-permute-start | bytes 98312 | tf_op jit(solution)/shard_map/ppermute | solution.py:298
  45.3 4.7 %collective-permute-start.4 = (s16[128,128]{1,0:T(8,128)(2,1)S(1)}, s16[128,128]{1,0:T(8,128)(2,1)S(1)}, u32[]{:S(2)}, u32[]{:S(2)}) collective-permute-start(s16[128,128]{1,0:T(8,128)(2,1)S(1)} %get-tuple-element.18), channel_id=1, source_target_pairs={{0,1},{1,0},{2,3},{3,2},{4,5},{5,4},{6,7},{7,6},{8,9},{9,8},{10,11... | collective-permute-start | bytes 98312 | tf_op jit(solution)/shard_map/ppermute | solution.py:298
  45.7 4.4 %collective-permute-start.5 = (s16[128,128]{1,0:T(8,128)(2,1)S(1)}, s16[128,128]{1,0:T(8,128)(2,1)S(1)}, u32[]{:S(2)}, u32[]{:S(2)}) collective-permute-start(s16[128,128]{1,0:T(8,128)(2,1)S(1)} %get-tuple-element.19), channel_id=1, source_target_pairs={{0,2},{1,3},{2,0},{3,1},{4,6},{5,7},{6,4},{7,5},{8,10},{9,11},{10,... | collective-permute-start | bytes 98312 | tf_op jit(solution)/shard_map/ppermute | solution.py:298
  46.0 4.1 %collective-permute-start.6 = (s16[128,128]{1,0:T(8,128)(2,1)S(1)}, s16[128,128]{1,0:T(8,128)(2,1)S(1)}, u32[]{:S(2)}, u32[]{:S(2)}) collective-permute-start(s16[128,128]{1,0:T(8,128)(2,1)S(1)} %get-tuple-element.20), channel_id=1, source_target_pairs={{0,3},{1,2},{2,1},{3,0},{4,7},{5,6},{6,5},{7,4},{8,11},{9,10},{10,... | collective-permute-start | bytes 98312 | tf_op jit(solution)/shard_map/ppermute | solution.py:298

commit v7 on v6

--- a/solution.py
+++ b/solution.py
@@ -33,6 +33,28 @@
     return jnp.maximum(jnp.exp(scaled) - 1.0, 0.0)
 
 
+def lowest_kernel(cost_ref, out_ref, buffer_ref, least_ref, in_sems, out_sems):
+    parts = in_sems.shape[0]
+    step = out_ref.shape[0] // parts
+    arrive, leave = [], []
+    for part in range(parts):
+        planes = pl.ds(part * step, step)
+        arrive.append(pltpu.make_async_copy(cost_ref.at[:, planes], buffer_ref.at[:, planes], in_sems.at[part]))
+        leave.append(pltpu.make_async_copy(least_ref.at[planes], out_ref.at[planes], out_sems.at[part]))
+    for copy in arrive:
+        copy.start()
+    for part in range(parts):
+        arrive[part].wait()
+        planes = pl.ds(part * step, step)
+        least = buffer_ref[0, planes]
+        for robot in range(1, buffer_ref.shape[0]):
+            least = jnp.minimum(least, buffer_ref[robot, planes])
+        least_ref[planes] = least
+        leave[part].start()
+    for copy in leave:
+        copy.wait()
+
+
 def prepare_kernel(occupied_ref, unknown_ref, raise_ref):
     def masks(place, _):
         taken = occupied_ref[place] == 1
@@ -56,7 +78,7 @@
             field_ref[field, place] = merged + raise_ref[field, source]
         return 0
 
-    lax.fori_loop(0, depth, seed, 0, unroll=4)
+    lax.fori_loop(0, depth, seed, 0, unroll=8)
     groups = field_ref.shape[2] // ROWS
 
     def sweep(piece, _):
@@ -80,7 +102,7 @@
             out_ref[place, field] = encode(best_ref[field, target])
         return 0
 
-    lax.fori_loop(0, own, send, 0, unroll=4)
+    lax.fori_loop(0, own, send, 0, unroll=8)
 
 
 def bit(place):
@@ -155,7 +177,6 @@
 
 def sparse_pass(line_ref, far_ref, table_ref, kept_ref, _):
     size = BLOCK // 2
-    fill_table(table_ref)
     find_blocks(line_ref, kept_ref, size)
 
     def target(block, _):
@@ -167,8 +188,7 @@
     lax.fori_loop(0, BLOCKS, target, 0)
 
 
-def dense_pass(line_ref, far_ref, table_ref, kept_ref, reached_ref):
-    fill_table(table_ref)
+def dense_pass(line_ref, far_ref, table_ref, kept_ref, reached_ref, finish=None):
     margin = jnp.full((PAD, LANES), 3e38, jnp.float32)
     line_ref[:PAD, :] = margin
     line_ref[PAD + LINE :, :] = margin
@@ -203,18 +223,27 @@
         lower_block(line_ref, far_ref, table_ref, kept_ref, BLOCK, block, start)
         return some ^ lax.shift_left(jnp.int32(1), block)
 
-    lax.while_loop(left, target, find_blocks(line_ref, kept_ref, BLOCK, float(ROWS + 1), reached_ref))
+    some = find_blocks(line_ref, kept_ref, BLOCK, float(ROWS + 1), reached_ref)
+    if finish is None:
+        lax.while_loop(left, target, some)
+        return
+    per_part = LANES // BLOCK
+    for part in range(LINE // LANES):
+        lax.while_loop(left, target, some & (((1 << per_part) - 1) << (part * per_part)))
+        finish(part)
 
 
 PASSES = (sparse_pass, dense_pass)
 
 
-def row_kernel(field, in_ref, own_ref, *rest):
-    send_refs, (line_ref, far_ref, *scratch) = rest[:-5], rest[-5:]
+def row_kernel(field, in_ref, table_ref, own_ref, *rest):
+    send_refs, (line_ref, far_ref, *scratch) = rest[:-4], rest[-4:]
     chunk = in_ref.shape[2]
+    if field == 0:
+        fill_table(table_ref)
     for piece in range(in_ref.shape[0]):
         line_ref[PAD + piece * chunk : PAD + (piece + 1) * chunk, :] = decode(in_ref[piece, field])
-    PASSES[field](line_ref, far_ref, *scratch)
+    PASSES[field](line_ref, far_ref, table_ref, *scratch)
     for step in range(len(send_refs) + 1):
         part = pl.ds(pl.multiple_of((lax.axis_index("yz") ^ step) * LANES, LANES), LANES)
         value = far_ref[part, :].T
@@ -230,40 +259,64 @@
         line_ref[part, :] = decode(got_refs[step - 1][...]) if step else own_ref[...]
 
 
-def column_kernel(own_ref, *rest):
-    got_refs, (far_ref, line_ref, *scratch) = rest[:-5], rest[-5:]
+def column_kernel(table_ref, own_ref, *rest):
+    got_refs, (far_ref, line_ref, *scratch) = rest[:-4], rest[-4:]
     gather_lines(own_ref, got_refs, line_ref)
-    PASSES[0](line_ref, far_ref, *scratch)
-
-
-def last_kernel(outside_ref, own_ref, *rest):
-    got_refs, (out_ref, line_ref, far_ref, *scratch) = rest[:-6], rest[-6:]
+    sparse_pass(line_ref, far_ref, table_ref, *scratch)
+
+
+def last_kernel(table_ref, outside_ref, own_ref, *rest):
+    got_refs, (out_ref, line_ref, far_ref, *scratch, part_ref, sems) = rest[:-7], rest[-7:]
     gather_lines(own_ref, got_refs, line_ref)
-    PASSES[1](line_ref, far_ref, *scratch)
-    for piece in range(LINE // LANES):
-        part = pl.ds(piece * LANES, LANES)
-        signed = voxel_size * (jnp.sqrt(outside_ref[part, :]) - jnp.sqrt(far_ref[part, :]))
-        out_ref[:, part] = signed.T
+
+    def copy(part):
+        return pltpu.make_async_copy(
+            part_ref.at[part], out_ref.at[:, pl.ds(part * LANES, LANES)], sems.at[part]
+        )
+
+    def finish(part):
+        rows = pl.ds(part * LANES, LANES)
+        signed = voxel_size * (jnp.sqrt(outside_ref[rows, :]) - jnp.sqrt(far_ref[rows, :]))
+        part_ref[part] = signed.T
+        copy(part).start()
+
+    dense_pass(line_ref, far_ref, table_ref, *scratch, finish=finish)
+    for part in range(LINE // LANES):
+        copy(part).wait()
 
 
 def body(seed_cost, occupied, unknown):
     depth, rows, columns = occupied.shape
     own = depth // lax.axis_size("robot")
     vmem = pl.BlockSpec(memory_space=pltpu.VMEM)
+    hbm = pl.BlockSpec(memory_space=pltpu.HBM)
     f32 = jnp.float32
 
-    def call(kernel, out_shape, scratch, *args, work=4e6):
+    def call(kernel, out_shape, scratch, *args, source=vmem, target=vmem, limit=16 * 2**20):
         return pl.pallas_call(
             kernel,
             out_shape=out_shape,
-            in_specs=[vmem] * len(args),
-            out_specs=jax.tree.map(lambda _: vmem, out_shape),
+            in_specs=[source] * len(args),
+            out_specs=jax.tree.map(lambda _: target, out_shape),
             scratch_shapes=scratch,
-            compiler_params=pltpu.CompilerParams(vmem_limit_bytes=16 * 2**20),
-            cost_estimate=pl.CostEstimate(flops=int(work), bytes_accessed=2**20, transcendentals=0),
+            compiler_params=pltpu.CompilerParams(vmem_limit_bytes=limit),
+            cost_estimate=pl.CostEstimate(flops=4 * 10**6, bytes_accessed=2**20, transcendentals=0),
         )(*args)
 
-    lowest = jnp.min(seed_cost, axis=0)
+    lowest = call(
+        lowest_kernel,
+        jax.ShapeDtypeStruct(seed_cost.shape[1:], seed_cost.dtype),
+        [
+            pltpu.VMEM(seed_cost.shape, seed_cost.dtype),
+            pltpu.VMEM(seed_cost.shape[1:], seed_cost.dtype),
+            pltpu.SemaphoreType.DMA((4,)),
+            pltpu.SemaphoreType.DMA((4,)),
+        ],
+        seed_cost,
+        source=hbm,
+        target=hbm,
+        limit=64 * 2**20 - 400 * 2**10,
+    )
     other = lax.ppermute(lowest, "robot", [(0, 1), (1, 0)])
     raised = call(
         prepare_kernel, jax.ShapeDtypeStruct((FIELDS, depth, rows, columns), f32), [], occupied, unknown
@@ -281,29 +334,30 @@
     parts = lax.axis_size("yz")
     share = LINE // parts
     line = pltpu.VMEM((LINE + 2 * PAD, LANES), f32)
-    scratch = [
-        pltpu.VMEM((2 * LINE, LANES), f32),
-        pltpu.SMEM((BLOCKS,), jnp.int32),
-        pltpu.VMEM((BLOCKS, LANES), f32),
-    ]
+    scratch = [pltpu.SMEM((BLOCKS,), jnp.int32), pltpu.VMEM((BLOCKS, LANES), f32)]
     lines = [line, pltpu.VMEM((LINE, LANES), f32), *scratch]
+    squares = jax.ShapeDtypeStruct((2 * LINE, LANES), f32)
     shapes = (jax.ShapeDtypeStruct((columns, share), f32),)
     shapes += (jax.ShapeDtypeStruct((columns, share), jnp.int16),) * (parts - 1)
+    row_calls = [functools.partial(row_kernel, field) for field in range(FIELDS)]
+    table, *first = call(row_calls[0], (squares, *shapes), lines, crossed)
+    second = call(row_calls[1], shapes, lines, crossed, table)
     settled = []
-    for field in range(FIELDS):
-        own_part, *others = call(
-            functools.partial(row_kernel, field), shapes, lines, crossed
-        )
+    for own_part, *others in (first, second):
         got = [
             lax.ppermute(part, "yz", [(i, i ^ step) for i in range(parts)])
             for step, part in enumerate(others, 1)
         ]
         settled.append((own_part, *got))
-    outside = call(
-        column_kernel, jax.ShapeDtypeStruct((LINE, share), f32), [line, *scratch], *settled[0]
-    )
+    outside = call(column_kernel, jax.ShapeDtypeStruct((LINE, share), f32), [line, *scratch], table, *settled[0])
     signed = call(
-        last_kernel, jax.ShapeDtypeStruct((share, LINE), f32), lines, outside, *settled[1]
+        last_kernel,
+        jax.ShapeDtypeStruct((share, LINE), f32),
+        [*lines, pltpu.VMEM((LINE // LANES, share, LANES), f32), pltpu.SemaphoreType.DMA((LINE // LANES,))],
+        table,
+        outside,
+        *settled[1],
+        target=hbm,
     )
     return signed[None]
 

time: 51.4 us -> 53.2 us (1.035); the launches traced: 52.4 us -> 52.7 us
  Pallas kernels: 12.3 us -> 14.5 us
  starting transfers between devices: 12.3 us -> 10.3 us
  other arithmetic: 1.19 us -> 0 us
  local copies, waits for them, and re-layouts: 1.05 us -> 2.09 us
    pallas_call x6 -> x7, Pallas kernels: 12.3 us -> 14.5 us  [call(): pl.pallas_call(kernel, out_shape=out_shape, in_specs=[source] * len(args)...]
    ppermute x6, starting transfers between devices: 8.69 us -> 6.66 us  [body(): lax.ppermute(part, 'yz', [(i, i ^ step) for i in range(parts)])]
    ppermute x6, waiting for transfers between devices: 0.02 us -> 1.23 us  [body(): lax.ppermute(part, 'yz', [(i, i ^ step) for i in range(parts)])]
    reduce_min x1 -> x0, other arithmetic: 1.19 us -> none  [body(): lowest = jnp.min(seed_cost, axis=0)]
    unnamed x4 -> x6, local copies, waits for them, and re-layouts: 1.05 us -> 2.09 us
    ppermute x1, waiting for transfers between devices: 3.79 us -> 3.07 us  [body(): other = lax.ppermute(lowest, 'robot', [(0, 1), (1, 0)])]
  transfers between devices with their start and end apart: 7 -> 7, of which waited for: 1 -> 2; matrix products, arithmetic and copies ran while one was open for 0% -> 0% of each run, Pallas kernels for 8% -> 8%
where the time goes in v7:
time: 53.2 us; the launch traced here: 52.7 us
  blocking collectives  21.5 us (40%)
  Pallas kernels  14.5 us (27%)
  starting transfers between devices  10.3 us (19%)
  waiting for transfers between devices  4.3 us (8%)
  local copies, waits for them, and re-layouts  2.09 us (4%)
    all_to_all x1, blocking collectives, body(): lax.all_to_all(planes, 'xy', split_axis=0, concat_axis=0, tiled=True)  21.5 us
    pallas_call x7, Pallas kernels, call(): pl.pallas_call(kernel, out_shape=out_shape, in_specs=[source] * len(args)...  14.5 us
    ppermute x6, starting transfers between devices, body(): lax.ppermute(part, 'yz', [(i, i ^ step) for i in range(parts)])  6.66 us
    ppermute x1, starting transfers between devices, body(): other = lax.ppermute(lowest, 'robot', [(0, 1), (1, 0)])  3.65 us
    ppermute x1, waiting for transfers between devices, body(): other = lax.ppermute(lowest, 'robot', [(0, 1), (1, 0)])  3.07 us
    unnamed x6, local copies, waits for them, and re-layouts  2.09 us
    ppermute x6, waiting for transfers between devices, body(): lax.ppermute(part, 'yz', [(i, i ^ step) for i in range(parts)])  1.23 us
  transfers between devices with their start and end apart: 7, of which 2 were waited for; matrix products, arithmetic and copies ran while one was open for 0% of the time, Pallas kernels for 8%

profile of v7, /device:TPU:1, one launch (start us, length us, event | category | flops | bytes accessed | tf_op | source)
XLA Modules:
  0.0 52.7 jit_solution(10239466176095872404)
XLA Ops:
  0.0 1.8 %shard_map.37.mine_ref = bf16[64,16,128]{2,1,0:T(8,128)(2,1)} custom-call(bf16[2,64,16,128]{3,2,1,0:T(8,128)(2,1)} %cost_ref.1), custom_call_target="tpu_custom_call" | custom-call | flops 4000000 | bytes 1048576 | tf_op jit(solution)/shard_map/pallas_call | solution.py:296
  1.8 0.0 copy-start
  1.8 3.6 %collective-permute-start = (bf16[64,16,128]{2,1,0:T(8,128)(2,1)}, bf16[64,16,128]{2,1,0:T(8,128)(2,1)S(1)}, u32[]{:S(2)}, u32[]{:S(2)}) collective-permute-start(bf16[64,16,128]{2,1,0:T(8,128)(2,1)} %shard_map.37.mine_ref), channel_id=1, source_target_pairs={{0,128},{128,0},{1,129},{129,1},{2,130},{130,2},{3,131},{131,3},{4... | collective-permute-start | bytes 786440 | tf_op jit(solution)/shard_map/ppermute | solution.py:320
  5.5 1.0 %copy-done.1 = s32[64,16,128]{2,1,0:T(8,128)S(1)} copy-done((s32[64,16,128]{2,1,0:T(8,128)S(1)}, s32[64,16,128]{2,1,0:T(8,128)}, u32[]{:S(2)}) %copy-start.1) | copy-done | bytes 524312
  6.5 1.0 %copy-done.2 = s32[64,16,128]{2,1,0:T(8,128)S(1)} copy-done((s32[64,16,128]{2,1,0:T(8,128)S(1)}, s32[64,16,128]{2,1,0:T(8,128)}, u32[]{:S(2)}) %copy-start.2) | copy-done | bytes 524312
  7.6 0.1 shard_map.38.raise_ref
  7.7 3.1 %collective-permute-done.other_ref = bf16[64,16,128]{2,1,0:T(8,128)(2,1)S(1)} collective-permute-done((bf16[64,16,128]{2,1,0:T(8,128)(2,1)}, bf16[64,16,128]{2,1,0:T(8,128)(2,1)S(1)}, u32[]{:S(2)}, u32[]{:S(2)}) %collective-permute-start) | collective-permute-done | bytes 262176 | tf_op jit(solution)/shard_map/ppermute | solution.py:320
  10.8 2.7 %shard_map.39 = s16[32,2,16,128]{3,2,1,0:T(8,128)(2,1)S(1)} custom-call(bf16[64,16,128]{2,1,0:T(8,128)(2,1)S(1)} %copy-done, bf16[64,16,128]{2,1,0:T(8,128)(2,1)S(1)} %collective-permute-done.other_ref, f32[2,64,16,128]{3,2,1,0:T(8,128)S(1)} %shard_map.38.raise_ref), custom_call_target="tpu_custom_call" | custom-call | flops 4000000 | bytes 1048576 | tf_op jit(solution)/shard_map/pallas_call | solution.py:296
  13.5 21.5 %all_to_all.5.in_ref = s16[32,2,16,128]{3,2,1,0:T(8,128)(2,1)S(1)} all-to-all(s16[32,2,16,128]{3,2,1,0:T(8,128)(2,1)S(1)} %shard_map.39), channel_id=1, replica_groups=mesh['robot'=2,'xy'=32,'yz'=4] {'xy'}, dimensions={0} | all-to-all | bytes 524288 | tf_op jit(solution)/shard_map/all_to_all | solution.py:332
  35.0 3.8 %shard_map.40 = (f32[1024,128]{1,0:T(8,128)S(1)}, f32[128,128]{1,0:T(8,128)S(1)}, s16[128,128]{1,0:T(8,128)(2,1)S(1)}, s16[128,128]{1,0:T(8,128)(2,1)S(1)}, s16[128,128]{1,0:T(8,128)(2,1)S(1)}) custom-call(s16[32,2,16,128]{3,2,1,0:T(8,128)(2,1)S(1)} %all_to_all.5.in_ref), custom_call_target="tpu_custom_call" | custom-call | flops 4000000 | bytes 1048576 | tf_op jit(solution)/shard_map/pallas_call | solution.py:296
  38.8 1.1 %collective-permute-start.1 = (s16[128,128]{1,0:T(8,128)(2,1)S(1)}, s16[128,128]{1,0:T(8,128)(2,1)S(1)}, u32[]{:S(2)}, u32[]{:S(2)}) collective-permute-start(s16[128,128]{1,0:T(8,128)(2,1)S(1)} %get-tuple-element.16), channel_id=1, source_target_pairs={{0,1},{1,0},{2,3},{3,2},{4,5},{5,4},{6,7},{7,6},{8,9},{9,8},{10,11... | collective-permute-start | bytes 98312 | tf_op jit(solution)/shard_map/ppermute | solution.py:348
  39.9 2.9 %collective-permute-start.2 = (s16[128,128]{1,0:T(8,128)(2,1)S(1)}, s16[128,128]{1,0:T(8,128)(2,1)S(1)}, u32[]{:S(2)}, u32[]{:S(2)}) collective-permute-start(s16[128,128]{1,0:T(8,128)(2,1)S(1)} %get-tuple-element.17), channel_id=1, source_target_pairs={{0,2},{1,3},{2,0},{3,1},{4,6},{5,7},{6,4},{7,5},{8,10},{9,11},{10,... | collective-permute-start | bytes 98312 | tf_op jit(solution)/shard_map/ppermute | solution.py:348
  42.8 0.1 collective-permute-start.3
  42.9 1.6 %shard_map.42 = (f32[128,128]{1,0:T(8,128)S(1)}, s16[128,128]{1,0:T(8,128)(2,1)S(1)}, s16[128,128]{1,0:T(8,128)(2,1)S(1)}, s16[128,128]{1,0:T(8,128)(2,1)S(1)}) custom-call(s16[32,2,16,128]{3,2,1,0:T(8,128)(2,1)S(1)} %all_to_all.5.in_ref, f32[1024,128]{1,0:T(8,128)S(1)} %get-tuple-element.14.table_ref), custom_call_target="tpu_custom_call" | custom-call | flops 4000000 | bytes 1048576 | tf_op jit(solution)/shard_map/pallas_call | solution.py:296
  44.5 0.1 collective-permute-start.4
  44.6 2.1 %collective-permute-start.5 = (s16[128,128]{1,0:T(8,128)(2,1)S(1)}, s16[128,128]{1,0:T(8,128)(2,1)S(1)}, u32[]{:S(2)}, u32[]{:S(2)}) collective-permute-start(s16[128,128]{1,0:T(8,128)(2,1)S(1)} %get-tuple-element.21), channel_id=1, source_target_pairs={{0,2},{1,3},{2,0},{3,1},{4,6},{5,7},{6,4},{7,5},{8,10},{9,11},{10,... | collective-permute-start | bytes 98312 | tf_op jit(solution)/shard_map/ppermute | solution.py:348
  46.7 0.0 collective-permute-done.1.rest_0_
  46.7 0.3 collective-permute-start.6
  47.0 0.0 collective-permute-done.2.rest_1_
  47.1 0.0 collective-permute-done.3.rest_2_
  47.1 2.4 %shard_map.41.outside_ref = f32[512,128]{1,0:T(8,128)S(1)} custom-call(f32[1024,128]{1,0:T(8,128)S(1)} %get-tuple-element.14.table_ref, f32[128,128]{1,0:T(8,128)S(1)} %get-tuple-element.15.own_ref, s16[128,128]{1,0:T(8,128)(2,1)S(1)} %collective-permute-done.1.rest_0_, s16[128,128]{1,0:T(8,128)(2,1)S(1)} %collective-permute-done.2.rest_1_, ...), custom_call_target="tpu_custom_call" | custom-call | flops 4000000 | bytes 1048576 | tf_op jit(solution)/shard_map/pallas_call | solution.py:296
  49.5 0.0 collective-permute-done.5.rest_1_
  49.5 1.2 %collective-permute-done.6.rest_2_ = s16[128,128]{1,0:T(8,128)(2,1)S(1)} collective-permute-done((s16[128,128]{1,0:T(8,128)(2,1)S(1)}, s16[128,128]{1,0:T(8,128)(2,1)S(1)}, u32[]{:S(2)}, u32[]{:S(2)}) %collective-permute-start.6) | collective-permute-done | bytes 32800 | tf_op jit(solution)/shard_map/ppermute | solution.py:348
  50.7 2.0 %shard_map.43 = f32[128,512]{1,0:T(8,128)} custom-call(f32[1024,128]{1,0:T(8,128)S(1)} %get-tuple-element.14.table_ref, f32[512,128]{1,0:T(8,128)S(1)} %shard_map.41.outside_ref, f32[128,128]{1,0:T(8,128)S(1)} %get-tuple-element.19.own_ref, s16[128,128]{1,0:T(8,128)(2,1)S(1)} %collective-permute-done.4.rest_0_, ...), custom_call_target="tpu_custom_call" | custom-call | flops 4000000 | bytes 1048576 | tf_op jit(solution)/shard_map/pallas_call | solution.py:296
  (4 shorter events, 0.0 us)
Async XLA Ops:
  1.8 9.0 %copy-start = (bf16[64,16,128]{2,1,0:T(8,128)(2,1)S(1)}, bf16[64,16,128]{2,1,0:T(8,128)(2,1)}, u32[]{:S(2)}) copy-start(bf16[64,16,128]{2,1,0:T(8,128)(2,1)} %shard_map.37.mine_ref) | copy-start | bytes 786436
  1.8 9.0 %collective-permute-start = (bf16[64,16,128]{2,1,0:T(8,128)(2,1)}, bf16[64,16,128]{2,1,0:T(8,128)(2,1)S(1)}, u32[]{:S(2)}, u32[]{:S(2)}) collective-permute-start(bf16[64,16,128]{2,1,0:T(8,128)(2,1)} %shard_map.37.mine_ref), channel_id=1, source_target_pairs={{0,128},{128,0},{1,129},{129,1},{2,130},{130,2},{3,131},{131,3},{4... | collective-permute-start | bytes 786440 | tf_op jit(solution)/shard_map/ppermute | solution.py:320
  5.5 1.0 %copy-start.1 = (s32[64,16,128]{2,1,0:T(8,128)S(1)}, s32[64,16,128]{2,1,0:T(8,128)}, u32[]{:S(2)}) copy-start(s32[64,16,128]{2,1,0:T(8,128)} %occupied_ref.1) | copy-start | bytes 1572868
  6.5 1.0 %copy-start.2 = (s32[64,16,128]{2,1,0:T(8,128)S(1)}, s32[64,16,128]{2,1,0:T(8,128)}, u32[]{:S(2)}) copy-start(s32[64,16,128]{2,1,0:T(8,128)} %unknown_ref.1) | copy-start | bytes 1572868
  38.8 7.9 %collective-permute-start.1 = (s16[128,128]{1,0:T(8,128)(2,1)S(1)}, s16[128,128]{1,0:T(8,128)(2,1)S(1)}, u32[]{:S(2)}, u32[]{:S(2)}) collective-permute-start(s16[128,128]{1,0:T(8,128)(2,1)S(1)} %get-tuple-element.16), channel_id=1, source_target_pairs={{0,1},{1,0},{2,3},{3,2},{4,5},{5,4},{6,7},{7,6},{8,9},{9,8},{10,11... | collective-permute-start | bytes 98312 | tf_op jit(solution)/shard_map/ppermute | solution.py:348
  39.9 7.1 %collective-permute-start.2 = (s16[128,128]{1,0:T(8,128)(2,1)S(1)}, s16[128,128]{1,0:T(8,128)(2,1)S(1)}, u32[]{:S(2)}, u32[]{:S(2)}) collective-permute-start(s16[128,128]{1,0:T(8,128)(2,1)S(1)} %get-tuple-element.17), channel_id=1, source_target_pairs={{0,2},{1,3},{2,0},{3,1},{4,6},{5,7},{6,4},{7,5},{8,10},{9,11},{10,... | collective-permute-start | bytes 98312 | tf_op jit(solution)/shard_map/ppermute | solution.py:348
  42.8 4.2 %collective-permute-start.3 = (s16[128,128]{1,0:T(8,128)(2,1)S(1)}, s16[128,128]{1,0:T(8,128)(2,1)S(1)}, u32[]{:S(2)}, u32[]{:S(2)}) collective-permute-start(s16[128,128]{1,0:T(8,128)(2,1)S(1)} %get-tuple-element.18), channel_id=1, source_target_pairs={{0,3},{1,2},{2,1},{3,0},{4,7},{5,6},{6,5},{7,4},{8,11},{9,10},{10,... | collective-permute-start | bytes 98312 | tf_op jit(solution)/shard_map/ppermute | solution.py:348
  44.5 5.0 %collective-permute-start.4 = (s16[128,128]{1,0:T(8,128)(2,1)S(1)}, s16[128,128]{1,0:T(8,128)(2,1)S(1)}, u32[]{:S(2)}, u32[]{:S(2)}) collective-permute-start(s16[128,128]{1,0:T(8,128)(2,1)S(1)} %get-tuple-element.20), channel_id=1, source_target_pairs={{0,1},{1,0},{2,3},{3,2},{4,5},{5,4},{6,7},{7,6},{8,9},{9,8},{10,11... | collective-permute-start | bytes 98312 | tf_op jit(solution)/shard_map/ppermute | solution.py:348
  44.6 4.9 %collective-permute-start.5 = (s16[128,128]{1,0:T(8,128)(2,1)S(1)}, s16[128,128]{1,0:T(8,128)(2,1)S(1)}, u32[]{:S(2)}, u32[]{:S(2)}) collective-permute-start(s16[128,128]{1,0:T(8,128)(2,1)S(1)} %get-tuple-element.21), channel_id=1, source_target_pairs={{0,2},{1,3},{2,0},{3,1},{4,6},{5,7},{6,4},{7,5},{8,10},{9,11},{10,... | collective-permute-start | bytes 98312 | tf_op jit(solution)/shard_map/ppermute | solution.py:348
  46.7 4.0 %collective-permute-start.6 = (s16[128,128]{1,0:T(8,128)(2,1)S(1)}, s16[128,128]{1,0:T(8,128)(2,1)S(1)}, u32[]{:S(2)}, u32[]{:S(2)}) collective-permute-start(s16[128,128]{1,0:T(8,128)(2,1)S(1)} %get-tuple-element.22), channel_id=1, source_target_pairs={{0,3},{1,2},{2,1},{3,0},{4,7},{5,6},{6,5},{7,4},{8,11},{9,10},{10,... | collective-permute-start | bytes 98312 | tf_op jit(solution)/shard_map/ppermute | solution.py:348

commit v8 on v6

--- a/solution.py
+++ b/solution.py
@@ -56,7 +56,7 @@
             field_ref[field, place] = merged + raise_ref[field, source]
         return 0
 
-    lax.fori_loop(0, depth, seed, 0, unroll=4)
+    lax.fori_loop(0, depth, seed, 0, unroll=8)
     groups = field_ref.shape[2] // ROWS
 
     def sweep(piece, _):
@@ -80,7 +80,7 @@
             out_ref[place, field] = encode(best_ref[field, target])
         return 0
 
-    lax.fori_loop(0, own, send, 0, unroll=4)
+    lax.fori_loop(0, own, send, 0, unroll=8)
 
 
 def bit(place):
@@ -155,7 +155,6 @@
 
 def sparse_pass(line_ref, far_ref, table_ref, kept_ref, _):
     size = BLOCK // 2
-    fill_table(table_ref)
     find_blocks(line_ref, kept_ref, size)
 
     def target(block, _):
@@ -168,7 +167,6 @@
 
 
 def dense_pass(line_ref, far_ref, table_ref, kept_ref, reached_ref):
-    fill_table(table_ref)
     margin = jnp.full((PAD, LANES), 3e38, jnp.float32)
     line_ref[:PAD, :] = margin
     line_ref[PAD + LINE :, :] = margin
@@ -209,12 +207,14 @@
 PASSES = (sparse_pass, dense_pass)
 
 
-def row_kernel(field, in_ref, own_ref, *rest):
-    send_refs, (line_ref, far_ref, *scratch) = rest[:-5], rest[-5:]
+def row_kernel(field, in_ref, table_ref, own_ref, *rest):
+    send_refs, (line_ref, far_ref, *scratch) = rest[:-4], rest[-4:]
     chunk = in_ref.shape[2]
+    if field == 0:
+        fill_table(table_ref)
     for piece in range(in_ref.shape[0]):
         line_ref[PAD + piece * chunk : PAD + (piece + 1) * chunk, :] = decode(in_ref[piece, field])
-    PASSES[field](line_ref, far_ref, *scratch)
+    PASSES[field](line_ref, far_ref, table_ref, *scratch)
     for step in range(len(send_refs) + 1):
         part = pl.ds(pl.multiple_of((lax.axis_index("yz") ^ step) * LANES, LANES), LANES)
         value = far_ref[part, :].T
@@ -230,16 +230,16 @@
         line_ref[part, :] = decode(got_refs[step - 1][...]) if step else own_ref[...]
 
 
-def column_kernel(own_ref, *rest):
-    got_refs, (far_ref, line_ref, *scratch) = rest[:-5], rest[-5:]
+def column_kernel(table_ref, own_ref, *rest):
+    got_refs, (far_ref, line_ref, *scratch) = rest[:-4], rest[-4:]
     gather_lines(own_ref, got_refs, line_ref)
-    PASSES[0](line_ref, far_ref, *scratch)
-
-
-def last_kernel(outside_ref, own_ref, *rest):
-    got_refs, (out_ref, line_ref, far_ref, *scratch) = rest[:-6], rest[-6:]
+    sparse_pass(line_ref, far_ref, table_ref, *scratch)
+
+
+def last_kernel(table_ref, outside_ref, own_ref, *rest):
+    got_refs, (out_ref, line_ref, far_ref, *scratch) = rest[:-5], rest[-5:]
     gather_lines(own_ref, got_refs, line_ref)
-    PASSES[1](line_ref, far_ref, *scratch)
+    dense_pass(line_ref, far_ref, table_ref, *scratch)
     for piece in range(LINE // LANES):
         part = pl.ds(piece * LANES, LANES)
         signed = voxel_size * (jnp.sqrt(outside_ref[part, :]) - jnp.sqrt(far_ref[part, :]))
@@ -252,7 +252,7 @@
     vmem = pl.BlockSpec(memory_space=pltpu.VMEM)
     f32 = jnp.float32
 
-    def call(kernel, out_shape, scratch, *args, work=4e6):
+    def call(kernel, out_shape, scratch, *args):
         return pl.pallas_call(
             kernel,
             out_shape=out_shape,
@@ -260,7 +260,7 @@
             out_specs=jax.tree.map(lambda _: vmem, out_shape),
             scratch_shapes=scratch,
             compiler_params=pltpu.CompilerParams(vmem_limit_bytes=16 * 2**20),
-            cost_estimate=pl.CostEstimate(flops=int(work), bytes_accessed=2**20, transcendentals=0),
+            cost_estimate=pl.CostEstimate(flops=4 * 10**6, bytes_accessed=2**20, transcendentals=0),
         )(*args)
 
     lowest = jnp.min(seed_cost, axis=0)
@@ -281,29 +281,29 @@
     parts = lax.axis_size("yz")
     share = LINE // parts
     line = pltpu.VMEM((LINE + 2 * PAD, LANES), f32)
-    scratch = [
-        pltpu.VMEM((2 * LINE, LANES), f32),
-        pltpu.SMEM((BLOCKS,), jnp.int32),
-        pltpu.VMEM((BLOCKS, LANES), f32),
-    ]
+    scratch = [pltpu.SMEM((BLOCKS,), jnp.int32), pltpu.VMEM((BLOCKS, LANES), f32)]
     lines = [line, pltpu.VMEM((LINE, LANES), f32), *scratch]
+    squares = jax.ShapeDtypeStruct((2 * LINE, LANES), f32)
     shapes = (jax.ShapeDtypeStruct((columns, share), f32),)
     shapes += (jax.ShapeDtypeStruct((columns, share), jnp.int16),) * (parts - 1)
+    row_calls = [functools.partial(row_kernel, field) for field in range(FIELDS)]
+    table, *first = call(row_calls[0], (squares, *shapes), lines, crossed)
+    second = call(row_calls[1], shapes, lines, crossed, table)
     settled = []
-    for field in range(FIELDS):
-        own_part, *others = call(
-            functools.partial(row_kernel, field), shapes, lines, crossed
-        )
+    for own_part, *others in (first, second):
         got = [
             lax.ppermute(part, "yz", [(i, i ^ step) for i in range(parts)])
             for step, part in enumerate(others, 1)
         ]
         settled.append((own_part, *got))
-    outside = call(
-        column_kernel, jax.ShapeDtypeStruct((LINE, share), f32), [line, *scratch], *settled[0]
-    )
+    outside = call(column_kernel, jax.ShapeDtypeStruct((LINE, share), f32), [line, *scratch], table, *settled[0])
     signed = call(
-        last_kernel, jax.ShapeDtypeStruct((share, LINE), f32), lines, outside, *settled[1]
+        last_kernel,
+        jax.ShapeDtypeStruct((share, LINE), f32),
+        lines,
+        table,
+        outside,
+        *settled[1],
     )
     return signed[None]
 

time: 51.4 us -> 51.1 us (level); the launches traced: 52.4 us -> 51.2 us
  starting transfers between devices: 12.3 us -> 8.39 us
  waiting for transfers between devices: 3.81 us -> 5.23 us
  Pallas kernels: 12.3 us -> 13.7 us
    ppermute x6, starting transfers between devices: 8.69 us -> 4.74 us  [body(): lax.ppermute(part, 'yz', [(i, i ^ step) for i in range(parts)])]
    ppermute x6, waiting for transfers between devices: 0.02 us -> 1.44 us  [body(): lax.ppermute(part, 'yz', [(i, i ^ step) for i in range(parts)])]
    pallas_call x6, Pallas kernels: 12.3 us -> 13.7 us  [call(): pl.pallas_call(kernel, out_shape=out_shape, in_specs=[vmem] * len(args),...]
  transfers between devices with their start and end apart: 7 -> 7, of which waited for: 1 -> 2; matrix products, arithmetic and copies ran while one was open for 0% -> 0% of each run, Pallas kernels for 8% -> 7%
where the time goes in v8:
time: 51.1 us; the launch traced here: 51.2 us
  blocking collectives  21.6 us (42%)
  Pallas kernels  13.7 us (27%)
  starting transfers between devices  8.39 us (16%)
  waiting for transfers between devices  5.23 us (10%)
  other arithmetic  1.19 us (2%)
  local copies, waits for them, and re-layouts  1.05 us (2%)
    all_to_all x1, blocking collectives, body(): lax.all_to_all(planes, 'xy', split_axis=0, concat_axis=0, tiled=True)  21.6 us
    pallas_call x6, Pallas kernels, call(): pl.pallas_call(kernel, out_shape=out_shape, in_specs=[vmem] * len(args),...  13.7 us
    ppermute x6, starting transfers between devices, body(): lax.ppermute(part, 'yz', [(i, i ^ step) for i in range(parts)])  4.74 us
    ppermute x1, waiting for transfers between devices, body(): other = lax.ppermute(lowest, 'robot', [(0, 1), (1, 0)])  3.79 us
    ppermute x1, starting transfers between devices, body(): other = lax.ppermute(lowest, 'robot', [(0, 1), (1, 0)])  3.65 us
    ppermute x6, waiting for transfers between devices, body(): lax.ppermute(part, 'yz', [(i, i ^ step) for i in range(parts)])  1.44 us
    reduce_min x1, other arithmetic, body(): lowest = jnp.min(seed_cost, axis=0)  1.19 us
    unnamed x4, local copies, waits for them, and re-layouts  1.05 us
  transfers between devices with their start and end apart: 7, of which 2 were waited for; matrix products, arithmetic and copies ran while one was open for 0% of the time, Pallas kernels for 7%

profile of v8, /device:TPU:1, one launch (start us, length us, event | category | flops | bytes accessed | tf_op | source)
XLA Modules:
  0.0 51.2 jit_solution(5617318687776747352)
XLA Ops:
  0.0 1.2 %reduce_min.9.mine_ref = bf16[64,16,128]{2,1,0:T(8,128)(2,1)S(1)} reduce(bf16[2,64,16,128]{3,2,1,0:T(8,128)(2,1)} %param.3, bf16[]{:T(256)} %constant.0.clone.1), dimensions={0}, to_apply=%region_0.0 | reduce | flops 131072 | bytes 786434 | tf_op jit(solution)/shard_map/reduce_min | solution.py:266
  1.2 3.6 %collective-permute-start = (bf16[64,16,128]{2,1,0:T(8,128)(2,1)S(1)}, bf16[64,16,128]{2,1,0:T(8,128)(2,1)S(1)}, u32[]{:S(2)}, u32[]{:S(2)}) collective-permute-start(bf16[64,16,128]{2,1,0:T(8,128)(2,1)S(1)} %reduce_min.9.mine_ref), channel_id=1, source_target_pairs={{0,128},{128,0},{1,129},{129,1},{2,130},{130,2},{3,131},{131,3},{4... | collective-permute-start | bytes 786440 | tf_op jit(solution)/shard_map/ppermute | solution.py:267
  4.8 0.0 copy-done
  4.8 1.0 %copy-done.1 = s32[64,16,128]{2,1,0:T(8,128)S(1)} copy-done((s32[64,16,128]{2,1,0:T(8,128)S(1)}, s32[64,16,128]{2,1,0:T(8,128)}, u32[]{:S(2)}) %copy-start.1) | copy-done | bytes 524312
  5.9 0.1 shard_map.37.raise_ref
  6.0 3.8 %collective-permute-done.other_ref = bf16[64,16,128]{2,1,0:T(8,128)(2,1)S(1)} collective-permute-done((bf16[64,16,128]{2,1,0:T(8,128)(2,1)S(1)}, bf16[64,16,128]{2,1,0:T(8,128)(2,1)S(1)}, u32[]{:S(2)}, u32[]{:S(2)}) %collective-permute-start) | collective-permute-done | bytes 262176 | tf_op jit(solution)/shard_map/ppermute | solution.py:267
  9.8 2.7 %shard_map.38 = s16[32,2,16,128]{3,2,1,0:T(8,128)(2,1)S(1)} custom-call(bf16[64,16,128]{2,1,0:T(8,128)(2,1)S(1)} %reduce_min.9.mine_ref, bf16[64,16,128]{2,1,0:T(8,128)(2,1)S(1)} %collective-permute-done.other_ref, f32[2,64,16,128]{3,2,1,0:T(8,128)S(1)} %shard_map.37.raise_ref), custom_call_target="tpu_custom_call" | custom-call | flops 4000000 | bytes 1048576 | tf_op jit(solution)/shard_map/pallas_call | solution.py:256
  12.6 21.6 %all_to_all.5.in_ref = s16[32,2,16,128]{3,2,1,0:T(8,128)(2,1)S(1)} all-to-all(s16[32,2,16,128]{3,2,1,0:T(8,128)(2,1)S(1)} %shard_map.38), channel_id=1, replica_groups=mesh['robot'=2,'xy'=32,'yz'=4] {'xy'}, dimensions={0} | all-to-all | bytes 524288 | tf_op jit(solution)/shard_map/all_to_all | solution.py:279
  34.2 5.3 %shard_map.39 = (f32[1024,128]{1,0:T(8,128)S(1)}, f32[128,128]{1,0:T(8,128)S(1)}, s16[128,128]{1,0:T(8,128)(2,1)S(1)}, s16[128,128]{1,0:T(8,128)(2,1)S(1)}, s16[128,128]{1,0:T(8,128)(2,1)S(1)}) custom-call(s16[32,2,16,128]{3,2,1,0:T(8,128)(2,1)S(1)} %all_to_all.5.in_ref), custom_call_target="tpu_custom_call" | custom-call | flops 4000000 | bytes 1048576 | tf_op jit(solution)/shard_map/pallas_call | solution.py:256
  39.5 0.1 collective-permute-start.1
  39.6 2.3 %collective-permute-start.2 = (s16[128,128]{1,0:T(8,128)(2,1)S(1)}, s16[128,128]{1,0:T(8,128)(2,1)S(1)}, u32[]{:S(2)}, u32[]{:S(2)}) collective-permute-start(s16[128,128]{1,0:T(8,128)(2,1)S(1)} %get-tuple-element.17), channel_id=1, source_target_pairs={{0,2},{1,3},{2,0},{3,1},{4,6},{5,7},{6,4},{7,5},{8,10},{9,11},{10,... | collective-permute-start | bytes 98312 | tf_op jit(solution)/shard_map/ppermute | solution.py:295
  42.0 0.1 collective-permute-start.3
  42.0 2.2 %shard_map.41 = (f32[128,128]{1,0:T(8,128)S(1)}, s16[128,128]{1,0:T(8,128)(2,1)S(1)}, s16[128,128]{1,0:T(8,128)(2,1)S(1)}, s16[128,128]{1,0:T(8,128)(2,1)S(1)}) custom-call(s16[32,2,16,128]{3,2,1,0:T(8,128)(2,1)S(1)} %all_to_all.5.in_ref, f32[1024,128]{1,0:T(8,128)S(1)} %get-tuple-element.14.table_ref), custom_call_target="tpu_custom_call" | custom-call | flops 4000000 | bytes 1048576 | tf_op jit(solution)/shard_map/pallas_call | solution.py:256
  44.2 0.1 collective-permute-start.4
  44.3 1.5 %collective-permute-start.5 = (s16[128,128]{1,0:T(8,128)(2,1)S(1)}, s16[128,128]{1,0:T(8,128)(2,1)S(1)}, u32[]{:S(2)}, u32[]{:S(2)}) collective-permute-start(s16[128,128]{1,0:T(8,128)(2,1)S(1)} %get-tuple-element.21), channel_id=1, source_target_pairs={{0,2},{1,3},{2,0},{3,1},{4,6},{5,7},{6,4},{7,5},{8,10},{9,11},{10,... | collective-permute-start | bytes 98312 | tf_op jit(solution)/shard_map/ppermute | solution.py:295
  45.9 0.0 collective-permute-done.1.rest_0_
  45.9 0.6 %collective-permute-start.6 = (s16[128,128]{1,0:T(8,128)(2,1)S(1)}, s16[128,128]{1,0:T(8,128)(2,1)S(1)}, u32[]{:S(2)}, u32[]{:S(2)}) collective-permute-start(s16[128,128]{1,0:T(8,128)(2,1)S(1)} %get-tuple-element.22), channel_id=1, source_target_pairs={{0,3},{1,2},{2,1},{3,0},{4,7},{5,6},{6,5},{7,4},{8,11},{9,10},{10,... | collective-permute-start | bytes 98312 | tf_op jit(solution)/shard_map/ppermute | solution.py:295
  46.5 0.0 collective-permute-done.2.rest_1_
  46.5 0.0 collective-permute-done.3.rest_2_
  46.5 1.3 %shard_map.40.outside_ref = f32[512,128]{1,0:T(8,128)S(1)} custom-call(f32[1024,128]{1,0:T(8,128)S(1)} %get-tuple-element.14.table_ref, f32[128,128]{1,0:T(8,128)S(1)} %get-tuple-element.15.own_ref, s16[128,128]{1,0:T(8,128)(2,1)S(1)} %collective-permute-done.1.rest_0_, s16[128,128]{1,0:T(8,128)(2,1)S(1)} %collective-permute-done.2.rest_1_, ...), custom_call_target="tpu_custom_call" | custom-call | flops 4000000 | bytes 1048576 | tf_op jit(solution)/shard_map/pallas_call | solution.py:256
  47.8 0.0 collective-permute-done.4.rest_0_
  47.8 0.0 collective-permute-done.5.rest_1_
  47.8 1.4 %collective-permute-done.6.rest_2_ = s16[128,128]{1,0:T(8,128)(2,1)S(1)} collective-permute-done((s16[128,128]{1,0:T(8,128)(2,1)S(1)}, s16[128,128]{1,0:T(8,128)(2,1)S(1)}, u32[]{:S(2)}, u32[]{:S(2)}) %collective-permute-start.6) | collective-permute-done | bytes 32800 | tf_op jit(solution)/shard_map/ppermute | solution.py:295
  49.2 2.0 %shard_map.42 = f32[128,512]{1,0:T(8,128)} custom-call(f32[1024,128]{1,0:T(8,128)S(1)} %get-tuple-element.14.table_ref, f32[512,128]{1,0:T(8,128)S(1)} %shard_map.40.outside_ref, f32[128,128]{1,0:T(8,128)S(1)} %get-tuple-element.19.own_ref, s16[128,128]{1,0:T(8,128)(2,1)S(1)} %collective-permute-done.4.rest_0_, ...), custom_call_target="tpu_custom_call" | custom-call | flops 4000000 | bytes 1048576 | tf_op jit(solution)/shard_map/pallas_call | solution.py:256
  (2 shorter events, 0.0 us)
Async XLA Ops:
  0.0 4.8 %copy-start = (s32[64,16,128]{2,1,0:T(8,128)S(1)}, s32[64,16,128]{2,1,0:T(8,128)}, u32[]{:S(2)}) copy-start(s32[64,16,128]{2,1,0:T(8,128)} %occupied_ref.1) | copy-start | bytes 1572868
  1.2 8.6 %collective-permute-start = (bf16[64,16,128]{2,1,0:T(8,128)(2,1)S(1)}, bf16[64,16,128]{2,1,0:T(8,128)(2,1)S(1)}, u32[]{:S(2)}, u32[]{:S(2)}) collective-permute-start(bf16[64,16,128]{2,1,0:T(8,128)(2,1)S(1)} %reduce_min.9.mine_ref), channel_id=1, source_target_pairs={{0,128},{128,0},{1,129},{129,1},{2,130},{130,2},{3,131},{131,3},{4... | collective-permute-start | bytes 786440 | tf_op jit(solution)/shard_map/ppermute | solution.py:267
  4.8 1.0 %copy-start.1 = (s32[64,16,128]{2,1,0:T(8,128)S(1)}, s32[64,16,128]{2,1,0:T(8,128)}, u32[]{:S(2)}) copy-start(s32[64,16,128]{2,1,0:T(8,128)} %unknown_ref.1) | copy-start | bytes 1572868
  39.5 6.3 %collective-permute-start.1 = (s16[128,128]{1,0:T(8,128)(2,1)S(1)}, s16[128,128]{1,0:T(8,128)(2,1)S(1)}, u32[]{:S(2)}, u32[]{:S(2)}) collective-permute-start(s16[128,128]{1,0:T(8,128)(2,1)S(1)} %get-tuple-element.16), channel_id=1, source_target_pairs={{0,1},{1,0},{2,3},{3,2},{4,5},{5,4},{6,7},{7,6},{8,9},{9,8},{10,11... | collective-permute-start | bytes 98312 | tf_op jit(solution)/shard_map/ppermute | solution.py:295
  39.6 6.9 %collective-permute-start.2 = (s16[128,128]{1,0:T(8,128)(2,1)S(1)}, s16[128,128]{1,0:T(8,128)(2,1)S(1)}, u32[]{:S(2)}, u32[]{:S(2)}) collective-permute-start(s16[128,128]{1,0:T(8,128)(2,1)S(1)} %get-tuple-element.17), channel_id=1, source_target_pairs={{0,2},{1,3},{2,0},{3,1},{4,6},{5,7},{6,4},{7,5},{8,10},{9,11},{10,... | collective-permute-start | bytes 98312 | tf_op jit(solution)/shard_map/ppermute | solution.py:295
  42.0 4.5 %collective-permute-start.3 = (s16[128,128]{1,0:T(8,128)(2,1)S(1)}, s16[128,128]{1,0:T(8,128)(2,1)S(1)}, u32[]{:S(2)}, u32[]{:S(2)}) collective-permute-start(s16[128,128]{1,0:T(8,128)(2,1)S(1)} %get-tuple-element.18), channel_id=1, source_target_pairs={{0,3},{1,2},{2,1},{3,0},{4,7},{5,6},{6,5},{7,4},{8,11},{9,10},{10,... | collective-permute-start | bytes 98312 | tf_op jit(solution)/shard_map/ppermute | solution.py:295
  44.2 3.6 %collective-permute-start.4 = (s16[128,128]{1,0:T(8,128)(2,1)S(1)}, s16[128,128]{1,0:T(8,128)(2,1)S(1)}, u32[]{:S(2)}, u32[]{:S(2)}) collective-permute-start(s16[128,128]{1,0:T(8,128)(2,1)S(1)} %get-tuple-element.20), channel_id=1, source_target_pairs={{0,1},{1,0},{2,3},{3,2},{4,5},{5,4},{6,7},{7,6},{8,9},{9,8},{10,11... | collective-permute-start | bytes 98312 | tf_op jit(solution)/shard_map/ppermute | solution.py:295
  44.3 3.5 %collective-permute-start.5 = (s16[128,128]{1,0:T(8,128)(2,1)S(1)}, s16[128,128]{1,0:T(8,128)(2,1)S(1)}, u32[]{:S(2)}, u32[]{:S(2)}) collective-permute-start(s16[128,128]{1,0:T(8,128)(2,1)S(1)} %get-tuple-element.21), channel_id=1, source_target_pairs={{0,2},{1,3},{2,0},{3,1},{4,6},{5,7},{6,4},{7,5},{8,10},{9,11},{10,... | collective-permute-start | bytes 98312 | tf_op jit(solution)/shard_map/ppermute | solution.py:295
  45.9 3.4 %collective-permute-start.6 = (s16[128,128]{1,0:T(8,128)(2,1)S(1)}, s16[128,128]{1,0:T(8,128)(2,1)S(1)}, u32[]{:S(2)}, u32[]{:S(2)}) collective-permute-start(s16[128,128]{1,0:T(8,128)(2,1)S(1)} %get-tuple-element.22), channel_id=1, source_target_pairs={{0,3},{1,2},{2,1},{3,0},{4,7},{5,6},{6,5},{7,4},{8,11},{9,10},{10,... | collective-permute-start | bytes 98312 | tf_op jit(solution)/shard_map/ppermute | solution.py:295

commit v9 on v8

--- a/solution.py
+++ b/solution.py
@@ -169,7 +169,7 @@
 def dense_pass(line_ref, far_ref, table_ref, kept_ref, reached_ref):
     margin = jnp.full((PAD, LANES), 3e38, jnp.float32)
     line_ref[:PAD, :] = margin
-    line_ref[PAD + LINE :, :] = margin
+    line_ref[PAD + LINE : 2 * PAD + LINE, :] = margin
 
     def band(block, _):
         at = pl.multiple_of(block * BLOCK, BLOCK)
@@ -280,8 +280,8 @@
 
     parts = lax.axis_size("yz")
     share = LINE // parts
-    line = pltpu.VMEM((LINE + 2 * PAD, LANES), f32)
-    scratch = [pltpu.SMEM((BLOCKS,), jnp.int32), pltpu.VMEM((BLOCKS, LANES), f32)]
+    line = pltpu.VMEM((LINE + 2 * PAD + ROWS, LANES), f32)
+    scratch = [pltpu.SMEM((BLOCKS,), jnp.int32), pltpu.VMEM((BLOCKS + ROWS, LANES), f32)]
     lines = [line, pltpu.VMEM((LINE, LANES), f32), *scratch]
     squares = jax.ShapeDtypeStruct((2 * LINE, LANES), f32)
     shapes = (jax.ShapeDtypeStruct((columns, share), f32),)

time: 51.1 us -> 51 us (level); the launches traced: 51.2 us -> 50.5 us
  starting transfers between devices: 8.39 us -> 11.3 us
  Pallas kernels: 13.7 us -> 11.4 us
  waiting for transfers between devices: 5.23 us -> 3.81 us
    ppermute x6, starting transfers between devices: 4.74 us -> 7.69 us  [body(): lax.ppermute(part, 'yz', [(i, i ^ step) for i in range(parts)])]
    pallas_call x6, Pallas kernels: 13.7 us -> 11.4 us  [call(): pl.pallas_call(kernel, out_shape=out_shape, in_specs=[vmem] * len(args),...]
    ppermute x6, waiting for transfers between devices: 1.44 us -> 0.02 us  [body(): lax.ppermute(part, 'yz', [(i, i ^ step) for i in range(parts)])]
  transfers between devices with their start and end apart: 7 -> 7, of which waited for: 2 -> 1; matrix products, arithmetic and copies ran while one was open for 0% -> 0% of each run, Pallas kernels for 7% -> 9%
where the time goes in v9:
time: 51 us; the launch traced here: 50.5 us
  blocking collectives  21.6 us (42%)
  Pallas kernels  11.4 us (22%)
  starting transfers between devices  11.3 us (22%)
  waiting for transfers between devices  3.81 us (7%)
  other arithmetic  1.19 us (2%)
  local copies, waits for them, and re-layouts  1.05 us (2%)
    all_to_all x1, blocking collectives, body(): lax.all_to_all(planes, 'xy', split_axis=0, concat_axis=0, tiled=True)  21.6 us
    pallas_call x6, Pallas kernels, call(): pl.pallas_call(kernel, out_shape=out_shape, in_specs=[vmem] * len(args),...  11.4 us
    ppermute x6, starting transfers between devices, body(): lax.ppermute(part, 'yz', [(i, i ^ step) for i in range(parts)])  7.69 us
    ppermute x1, waiting for transfers between devices, body(): other = lax.ppermute(lowest, 'robot', [(0, 1), (1, 0)])  3.79 us
    ppermute x1, starting transfers between devices, body(): other = lax.ppermute(lowest, 'robot', [(0, 1), (1, 0)])  3.65 us
    reduce_min x1, other arithmetic, body(): lowest = jnp.min(seed_cost, axis=0)  1.19 us
    unnamed x4, local copies, waits for them, and re-layouts  1.05 us
  transfers between devices with their start and end apart: 7, of which 1 were waited for; matrix products, arithmetic and copies ran while one was open for 0% of the time, Pallas kernels for 9%

profile of v9, /device:TPU:1, one launch (start us, length us, event | category | flops | bytes accessed | tf_op | source)
XLA Modules:
  0.0 50.5 jit_solution(14305586185049826478)
XLA Ops:
  0.0 1.2 %reduce_min.9.mine_ref = bf16[64,16,128]{2,1,0:T(8,128)(2,1)S(1)} reduce(bf16[2,64,16,128]{3,2,1,0:T(8,128)(2,1)} %param.3, bf16[]{:T(256)} %constant.0.clone.1), dimensions={0}, to_apply=%region_0.0 | reduce | flops 131072 | bytes 786434 | tf_op jit(solution)/shard_map/reduce_min | solution.py:266
  1.2 3.6 %collective-permute-start = (bf16[64,16,128]{2,1,0:T(8,128)(2,1)S(1)}, bf16[64,16,128]{2,1,0:T(8,128)(2,1)S(1)}, u32[]{:S(2)}, u32[]{:S(2)}) collective-permute-start(bf16[64,16,128]{2,1,0:T(8,128)(2,1)S(1)} %reduce_min.9.mine_ref), channel_id=1, source_target_pairs={{0,128},{128,0},{1,129},{129,1},{2,130},{130,2},{3,131},{131,3},{4... | collective-permute-start | bytes 786440 | tf_op jit(solution)/shard_map/ppermute | solution.py:267
  4.8 0.0 copy-done
  4.8 1.0 %copy-done.1 = s32[64,16,128]{2,1,0:T(8,128)S(1)} copy-done((s32[64,16,128]{2,1,0:T(8,128)S(1)}, s32[64,16,128]{2,1,0:T(8,128)}, u32[]{:S(2)}) %copy-start.1) | copy-done | bytes 524312
  5.9 0.1 shard_map.37.raise_ref
  6.0 3.8 %collective-permute-done.other_ref = bf16[64,16,128]{2,1,0:T(8,128)(2,1)S(1)} collective-permute-done((bf16[64,16,128]{2,1,0:T(8,128)(2,1)S(1)}, bf16[64,16,128]{2,1,0:T(8,128)(2,1)S(1)}, u32[]{:S(2)}, u32[]{:S(2)}) %collective-permute-start) | collective-permute-done | bytes 262176 | tf_op jit(solution)/shard_map/ppermute | solution.py:267
  9.8 2.7 %shard_map.38 = s16[32,2,16,128]{3,2,1,0:T(8,128)(2,1)S(1)} custom-call(bf16[64,16,128]{2,1,0:T(8,128)(2,1)S(1)} %reduce_min.9.mine_ref, bf16[64,16,128]{2,1,0:T(8,128)(2,1)S(1)} %collective-permute-done.other_ref, f32[2,64,16,128]{3,2,1,0:T(8,128)S(1)} %shard_map.37.raise_ref), custom_call_target="tpu_custom_call" | custom-call | flops 4000000 | bytes 1048576 | tf_op jit(solution)/shard_map/pallas_call | solution.py:256
  12.6 21.6 %all_to_all.5.in_ref = s16[32,2,16,128]{3,2,1,0:T(8,128)(2,1)S(1)} all-to-all(s16[32,2,16,128]{3,2,1,0:T(8,128)(2,1)S(1)} %shard_map.38), channel_id=1, replica_groups=mesh['robot'=2,'xy'=32,'yz'=4] {'xy'}, dimensions={0} | all-to-all | bytes 524288 | tf_op jit(solution)/shard_map/all_to_all | solution.py:279
  34.2 2.4 %shard_map.39 = (f32[1024,128]{1,0:T(8,128)S(1)}, f32[128,128]{1,0:T(8,128)S(1)}, s16[128,128]{1,0:T(8,128)(2,1)S(1)}, s16[128,128]{1,0:T(8,128)(2,1)S(1)}, s16[128,128]{1,0:T(8,128)(2,1)S(1)}) custom-call(s16[32,2,16,128]{3,2,1,0:T(8,128)(2,1)S(1)} %all_to_all.5.in_ref), custom_call_target="tpu_custom_call" | custom-call | flops 4000000 | bytes 1048576 | tf_op jit(solution)/shard_map/pallas_call | solution.py:256
  36.6 3.8 %collective-permute-start.1 = (s16[128,128]{1,0:T(8,128)(2,1)S(1)}, s16[128,128]{1,0:T(8,128)(2,1)S(1)}, u32[]{:S(2)}, u32[]{:S(2)}) collective-permute-start(s16[128,128]{1,0:T(8,128)(2,1)S(1)} %get-tuple-element.16), channel_id=1, source_target_pairs={{0,1},{1,0},{2,3},{3,2},{4,5},{5,4},{6,7},{7,6},{8,9},{9,8},{10,11... | collective-permute-start | bytes 98312 | tf_op jit(solution)/shard_map/ppermute | solution.py:295
  40.3 0.2 collective-permute-start.2
  40.5 1.6 %collective-permute-start.3 = (s16[128,128]{1,0:T(8,128)(2,1)S(1)}, s16[128,128]{1,0:T(8,128)(2,1)S(1)}, u32[]{:S(2)}, u32[]{:S(2)}) collective-permute-start(s16[128,128]{1,0:T(8,128)(2,1)S(1)} %get-tuple-element.18), channel_id=1, source_target_pairs={{0,3},{1,2},{2,1},{3,0},{4,7},{5,6},{6,5},{7,4},{8,11},{9,10},{10,... | collective-permute-start | bytes 98312 | tf_op jit(solution)/shard_map/ppermute | solution.py:295
  42.1 1.7 %shard_map.41 = (f32[128,128]{1,0:T(8,128)S(1)}, s16[128,128]{1,0:T(8,128)(2,1)S(1)}, s16[128,128]{1,0:T(8,128)(2,1)S(1)}, s16[128,128]{1,0:T(8,128)(2,1)S(1)}) custom-call(s16[32,2,16,128]{3,2,1,0:T(8,128)(2,1)S(1)} %all_to_all.5.in_ref, f32[1024,128]{1,0:T(8,128)S(1)} %get-tuple-element.14.table_ref), custom_call_target="tpu_custom_call" | custom-call | flops 4000000 | bytes 1048576 | tf_op jit(solution)/shard_map/pallas_call | solution.py:256
  43.7 0.1 collective-permute-start.4
  43.8 0.1 collective-permute-start.5
  43.9 0.0 collective-permute-done.1.rest_0_
  44.0 2.0 %collective-permute-start.6 = (s16[128,128]{1,0:T(8,128)(2,1)S(1)}, s16[128,128]{1,0:T(8,128)(2,1)S(1)}, u32[]{:S(2)}, u32[]{:S(2)}) collective-permute-start(s16[128,128]{1,0:T(8,128)(2,1)S(1)} %get-tuple-element.22), channel_id=1, source_target_pairs={{0,3},{1,2},{2,1},{3,0},{4,7},{5,6},{6,5},{7,4},{8,11},{9,10},{10,... | collective-permute-start | bytes 98312 | tf_op jit(solution)/shard_map/ppermute | solution.py:295
  46.0 0.0 collective-permute-done.2.rest_1_
  46.0 0.0 collective-permute-done.3.rest_2_
  46.0 2.6 %shard_map.40.outside_ref = f32[512,128]{1,0:T(8,128)S(1)} custom-call(f32[1024,128]{1,0:T(8,128)S(1)} %get-tuple-element.14.table_ref, f32[128,128]{1,0:T(8,128)S(1)} %get-tuple-element.15.own_ref, s16[128,128]{1,0:T(8,128)(2,1)S(1)} %collective-permute-done.1.rest_0_, s16[128,128]{1,0:T(8,128)(2,1)S(1)} %collective-permute-done.2.rest_1_, ...), custom_call_target="tpu_custom_call" | custom-call | flops 4000000 | bytes 1048576 | tf_op jit(solution)/shard_map/pallas_call | solution.py:256
  48.6 0.0 collective-permute-done.4.rest_0_
  48.6 0.0 collective-permute-done.5.rest_1_
  48.7 0.0 collective-permute-done.6.rest_2_
  48.7 1.8 %shard_map.42 = f32[128,512]{1,0:T(8,128)} custom-call(f32[1024,128]{1,0:T(8,128)S(1)} %get-tuple-element.14.table_ref, f32[512,128]{1,0:T(8,128)S(1)} %shard_map.40.outside_ref, f32[128,128]{1,0:T(8,128)S(1)} %get-tuple-element.19.own_ref, s16[128,128]{1,0:T(8,128)(2,1)S(1)} %collective-permute-done.4.rest_0_, ...), custom_call_target="tpu_custom_call" | custom-call | flops 4000000 | bytes 1048576 | tf_op jit(solution)/shard_map/pallas_call | solution.py:256
  (2 shorter events, 0.0 us)
Async XLA Ops:
  0.0 4.8 %copy-start = (s32[64,16,128]{2,1,0:T(8,128)S(1)}, s32[64,16,128]{2,1,0:T(8,128)}, u32[]{:S(2)}) copy-start(s32[64,16,128]{2,1,0:T(8,128)} %occupied_ref.1) | copy-start | bytes 1572868
  1.2 8.6 %collective-permute-start = (bf16[64,16,128]{2,1,0:T(8,128)(2,1)S(1)}, bf16[64,16,128]{2,1,0:T(8,128)(2,1)S(1)}, u32[]{:S(2)}, u32[]{:S(2)}) collective-permute-start(bf16[64,16,128]{2,1,0:T(8,128)(2,1)S(1)} %reduce_min.9.mine_ref), channel_id=1, source_target_pairs={{0,128},{128,0},{1,129},{129,1},{2,130},{130,2},{3,131},{131,3},{4... | collective-permute-start | bytes 786440 | tf_op jit(solution)/shard_map/ppermute | solution.py:267
  4.8 1.0 %copy-start.1 = (s32[64,16,128]{2,1,0:T(8,128)S(1)}, s32[64,16,128]{2,1,0:T(8,128)}, u32[]{:S(2)}) copy-start(s32[64,16,128]{2,1,0:T(8,128)} %unknown_ref.1) | copy-start | bytes 1572868
  36.6 7.4 %collective-permute-start.1 = (s16[128,128]{1,0:T(8,128)(2,1)S(1)}, s16[128,128]{1,0:T(8,128)(2,1)S(1)}, u32[]{:S(2)}, u32[]{:S(2)}) collective-permute-start(s16[128,128]{1,0:T(8,128)(2,1)S(1)} %get-tuple-element.16), channel_id=1, source_target_pairs={{0,1},{1,0},{2,3},{3,2},{4,5},{5,4},{6,7},{7,6},{8,9},{9,8},{10,11... | collective-permute-start | bytes 98312 | tf_op jit(solution)/shard_map/ppermute | solution.py:295
  40.3 5.7 %collective-permute-start.2 = (s16[128,128]{1,0:T(8,128)(2,1)S(1)}, s16[128,128]{1,0:T(8,128)(2,1)S(1)}, u32[]{:S(2)}, u32[]{:S(2)}) collective-permute-start(s16[128,128]{1,0:T(8,128)(2,1)S(1)} %get-tuple-element.17), channel_id=1, source_target_pairs={{0,2},{1,3},{2,0},{3,1},{4,6},{5,7},{6,4},{7,5},{8,10},{9,11},{10,... | collective-permute-start | bytes 98312 | tf_op jit(solution)/shard_map/ppermute | solution.py:295
  40.5 5.5 %collective-permute-start.3 = (s16[128,128]{1,0:T(8,128)(2,1)S(1)}, s16[128,128]{1,0:T(8,128)(2,1)S(1)}, u32[]{:S(2)}, u32[]{:S(2)}) collective-permute-start(s16[128,128]{1,0:T(8,128)(2,1)S(1)} %get-tuple-element.18), channel_id=1, source_target_pairs={{0,3},{1,2},{2,1},{3,0},{4,7},{5,6},{6,5},{7,4},{8,11},{9,10},{10,... | collective-permute-start | bytes 98312 | tf_op jit(solution)/shard_map/ppermute | solution.py:295
  43.7 4.9 %collective-permute-start.4 = (s16[128,128]{1,0:T(8,128)(2,1)S(1)}, s16[128,128]{1,0:T(8,128)(2,1)S(1)}, u32[]{:S(2)}, u32[]{:S(2)}) collective-permute-start(s16[128,128]{1,0:T(8,128)(2,1)S(1)} %get-tuple-element.20), channel_id=1, source_target_pairs={{0,1},{1,0},{2,3},{3,2},{4,5},{5,4},{6,7},{7,6},{8,9},{9,8},{10,11... | collective-permute-start | bytes 98312 | tf_op jit(solution)/shard_map/ppermute | solution.py:295
  43.8 4.8 %collective-permute-start.5 = (s16[128,128]{1,0:T(8,128)(2,1)S(1)}, s16[128,128]{1,0:T(8,128)(2,1)S(1)}, u32[]{:S(2)}, u32[]{:S(2)}) collective-permute-start(s16[128,128]{1,0:T(8,128)(2,1)S(1)} %get-tuple-element.21), channel_id=1, source_target_pairs={{0,2},{1,3},{2,0},{3,1},{4,6},{5,7},{6,4},{7,5},{8,10},{9,11},{10,... | collective-permute-start | bytes 98312 | tf_op jit(solution)/shard_map/ppermute | solution.py:295
  44.0 4.7 %collective-permute-start.6 = (s16[128,128]{1,0:T(8,128)(2,1)S(1)}, s16[128,128]{1,0:T(8,128)(2,1)S(1)}, u32[]{:S(2)}, u32[]{:S(2)}) collective-permute-start(s16[128,128]{1,0:T(8,128)(2,1)S(1)} %get-tuple-element.22), channel_id=1, source_target_pairs={{0,3},{1,2},{2,1},{3,0},{4,7},{5,6},{6,5},{7,4},{8,11},{9,10},{10,... | collective-permute-start | bytes 98312 | tf_op jit(solution)/shard_map/ppermute | solution.py:295

commit v10 on v9

--- a/solution.py
+++ b/solution.py
@@ -16,6 +16,7 @@
 BLOCK = 32
 BLOCKS = LINE // BLOCK
 GROUPS = BLOCK // ROWS
+FINE = BLOCK // 2
 PAD = ROWS
 FIELDS = 2
 
@@ -33,7 +34,7 @@
     return jnp.maximum(jnp.exp(scaled) - 1.0, 0.0)
 
 
-def prepare_kernel(occupied_ref, unknown_ref, raise_ref):
+def prepare_kernel(occupied_ref, unknown_ref, raise_ref, table_ref, spans_ref):
     def masks(place, _):
         taken = occupied_ref[place] == 1
         hidden = taken | (unknown_ref[place] == 1)
@@ -42,6 +43,11 @@
         return 0
 
     lax.fori_loop(0, occupied_ref.shape[0], masks, 0, unroll=4)
+    fill_table(table_ref)
+    for half in range(BLOCKS // ROWS):
+        for place in range(LINE // FINE):
+            for kind, squares in enumerate(spans(half * ROWS, place * FINE, FINE, 0.0)):
+                spans_ref[kind, half, place] = squares
 
 
 def depth_kernel(mine_ref, other_ref, raise_ref, out_ref, field_ref, best_ref):
@@ -87,8 +93,15 @@
     return jnp.int32((1 << place) - (1 << 32 if place == 31 else 0))
 
 
-def find_blocks(line_ref, kept_ref, size, least_gap=0.0, reached_ref=None):
+def spans(first, source, size, least_gap):
     sublane = lax.broadcasted_iota(jnp.int32, (ROWS, LANES), 0).astype(jnp.float32)
+    after = sublane * float(BLOCK) + float(first * BLOCK - source)
+    far = jnp.maximum(after + float(BLOCK - 1), float(size - 1) - after)
+    near = jnp.maximum(jnp.maximum(after - float(size - 1), -after - float(BLOCK - 1)), least_gap)
+    return far * far, near * near
+
+
+def find_blocks(line_ref, kept_ref, size, least_gap=0.0, reached_ref=None, spans_ref=None):
     sources = range(0, LINE, size)
     low = []
     for source in sources:
@@ -102,12 +115,13 @@
         if reached_ref is not None:
             bound = jnp.minimum(bound, reached_ref[first : first + ROWS, :])
         floor = []
-        for source, least in zip(sources, low):
-            after = sublane * float(BLOCK) + float(first * BLOCK - source)
-            far = jnp.maximum(after + float(BLOCK - 1), float(size - 1) - after)
-            near = jnp.maximum(jnp.maximum(after - float(size - 1), -after - float(BLOCK - 1)), least_gap)
-            bound = jnp.minimum(bound, least + far * far)
-            floor.append(least + near * near)
+        for place, (source, least) in enumerate(zip(sources, low)):
+            if spans_ref is None:
+                far, near = spans(first, source, size, least_gap)
+            else:
+                far, near = (spans_ref[kind, first // ROWS, place] for kind in range(2))
+            bound = jnp.minimum(bound, least + far)
+            floor.append(least + near)
         kept = jnp.zeros((ROWS, 1), jnp.int32)
         for place in range(len(sources)):
             keep = jnp.min(floor[place] - bound, axis=1, keepdims=True) < 0.0
@@ -153,9 +167,9 @@
         table_ref[at : at + ROWS, :] = apart * apart
 
 
-def sparse_pass(line_ref, far_ref, table_ref, kept_ref, _):
-    size = BLOCK // 2
-    find_blocks(line_ref, kept_ref, size)
+def sparse_pass(line_ref, far_ref, table_ref, spans_ref, kept_ref, _):
+    size = FINE
+    find_blocks(line_ref, kept_ref, size, spans_ref=spans_ref)
 
     def target(block, _):
         at = pl.multiple_of(block * BLOCK, BLOCK) + PAD
@@ -166,7 +180,7 @@
     lax.fori_loop(0, BLOCKS, target, 0)
 
 
-def dense_pass(line_ref, far_ref, table_ref, kept_ref, reached_ref):
+def dense_pass(line_ref, far_ref, table_ref, _, kept_ref, reached_ref):
     margin = jnp.full((PAD, LANES), 3e38, jnp.float32)
     line_ref[:PAD, :] = margin
     line_ref[PAD + LINE : 2 * PAD + LINE, :] = margin
@@ -207,14 +221,12 @@
 PASSES = (sparse_pass, dense_pass)
 
 
-def row_kernel(field, in_ref, table_ref, own_ref, *rest):
+def row_kernel(field, in_ref, table_ref, spans_ref, own_ref, *rest):
     send_refs, (line_ref, far_ref, *scratch) = rest[:-4], rest[-4:]
     chunk = in_ref.shape[2]
-    if field == 0:
-        fill_table(table_ref)
     for piece in range(in_ref.shape[0]):
         line_ref[PAD + piece * chunk : PAD + (piece + 1) * chunk, :] = decode(in_ref[piece, field])
-    PASSES[field](line_ref, far_ref, table_ref, *scratch)
+    PASSES[field](line_ref, far_ref, table_ref, spans_ref, *scratch)
     for step in range(len(send_refs) + 1):
         part = pl.ds(pl.multiple_of((lax.axis_index("yz") ^ step) * LANES, LANES), LANES)
         value = far_ref[part, :].T
@@ -230,16 +242,16 @@
         line_ref[part, :] = decode(got_refs[step - 1][...]) if step else own_ref[...]
 
 
-def column_kernel(table_ref, own_ref, *rest):
+def column_kernel(table_ref, spans_ref, own_ref, *rest):
     got_refs, (far_ref, line_ref, *scratch) = rest[:-4], rest[-4:]
     gather_lines(own_ref, got_refs, line_ref)
-    sparse_pass(line_ref, far_ref, table_ref, *scratch)
+    sparse_pass(line_ref, far_ref, table_ref, spans_ref, *scratch)
 
 
 def last_kernel(table_ref, outside_ref, own_ref, *rest):
     got_refs, (out_ref, line_ref, far_ref, *scratch) = rest[:-5], rest[-5:]
     gather_lines(own_ref, got_refs, line_ref)
-    dense_pass(line_ref, far_ref, table_ref, *scratch)
+    dense_pass(line_ref, far_ref, table_ref, None, *scratch)
     for piece in range(LINE // LANES):
         part = pl.ds(piece * LANES, LANES)
         signed = voxel_size * (jnp.sqrt(outside_ref[part, :]) - jnp.sqrt(far_ref[part, :]))
@@ -265,8 +277,16 @@
 
     lowest = jnp.min(seed_cost, axis=0)
     other = lax.ppermute(lowest, "robot", [(0, 1), (1, 0)])
-    raised = call(
-        prepare_kernel, jax.ShapeDtypeStruct((FIELDS, depth, rows, columns), f32), [], occupied, unknown
+    raised, table, squares = call(
+        prepare_kernel,
+        (
+            jax.ShapeDtypeStruct((FIELDS, depth, rows, columns), f32),
+            jax.ShapeDtypeStruct((2 * LINE, LANES), f32),
+            jax.ShapeDtypeStruct((2, BLOCKS // ROWS, LINE // FINE, ROWS, LANES), f32),
+        ),
+        [],
+        occupied,
+        unknown,
     )
     planes = call(
         depth_kernel,
@@ -283,20 +303,17 @@
     line = pltpu.VMEM((LINE + 2 * PAD + ROWS, LANES), f32)
     scratch = [pltpu.SMEM((BLOCKS,), jnp.int32), pltpu.VMEM((BLOCKS + ROWS, LANES), f32)]
     lines = [line, pltpu.VMEM((LINE, LANES), f32), *scratch]
-    squares = jax.ShapeDtypeStruct((2 * LINE, LANES), f32)
     shapes = (jax.ShapeDtypeStruct((columns, share), f32),)
     shapes += (jax.ShapeDtypeStruct((columns, share), jnp.int16),) * (parts - 1)
-    row_calls = [functools.partial(row_kernel, field) for field in range(FIELDS)]
-    table, *first = call(row_calls[0], (squares, *shapes), lines, crossed)
-    second = call(row_calls[1], shapes, lines, crossed, table)
     settled = []
-    for own_part, *others in (first, second):
+    for field in range(FIELDS):
+        own_part, *others = call(functools.partial(row_kernel, field), shapes, lines, crossed, table, squares)
         got = [
             lax.ppermute(part, "yz", [(i, i ^ step) for i in range(parts)])
             for step, part in enumerate(others, 1)
         ]
         settled.append((own_part, *got))
-    outside = call(column_kernel, jax.ShapeDtypeStruct((LINE, share), f32), [line, *scratch], table, *settled[0])
+    outside = call(column_kernel, jax.ShapeDtypeStruct((LINE, share), f32), [line, *scratch], table, squares, *settled[0])
     signed = call(
         last_kernel,
         jax.ShapeDtypeStruct((share, LINE), f32),

time: 51 us -> 51.7 us (1.014)
  starting transfers between devices: 11.3 us -> 12.2 us
    ppermute x6, starting transfers between devices: 7.69 us -> 8.56 us  [body(): lax.ppermute(part, 'yz', [(i, i ^ step) for i in range(parts)])]
where the time goes in v10:
time: 51.7 us; the launch traced here: 51 us
  blocking collectives  21.6 us (42%)
  starting transfers between devices  12.2 us (24%)
  Pallas kernels  11.2 us (22%)
  waiting for transfers between devices  3.7 us (7%)
  other arithmetic  1.19 us (2%)
  local copies, waits for them, and re-layouts  1.05 us (2%)
    all_to_all x1, blocking collectives, body(): lax.all_to_all(planes, 'xy', split_axis=0, concat_axis=0, tiled=True)  21.6 us
    pallas_call x6, Pallas kernels, call(): pl.pallas_call(kernel, out_shape=out_shape, in_specs=[vmem] * len(args),...  11.2 us
    ppermute x6, starting transfers between devices, body(): lax.ppermute(part, 'yz', [(i, i ^ step) for i in range(parts)])  8.56 us
    ppermute x1, waiting for transfers between devices, body(): other = lax.ppermute(lowest, 'robot', [(0, 1), (1, 0)])  3.69 us
    ppermute x1, starting transfers between devices, body(): other = lax.ppermute(lowest, 'robot', [(0, 1), (1, 0)])  3.65 us
    reduce_min x1, other arithmetic, body(): lowest = jnp.min(seed_cost, axis=0)  1.19 us
    unnamed x4, local copies, waits for them, and re-layouts  1.05 us
  transfers between devices with their start and end apart: 7, of which 1 were waited for; matrix products, arithmetic and copies ran while one was open for 0% of the time, Pallas kernels for 9%

profile of v10, /device:TPU:1, one launch (start us, length us, event | category | flops | bytes accessed | tf_op | source)
XLA Modules:
  0.0 51.0 jit_solution(10769687125060057438)
XLA Ops:
  0.0 1.2 %reduce_min.9.mine_ref = bf16[64,16,128]{2,1,0:T(8,128)(2,1)S(1)} reduce(bf16[2,64,16,128]{3,2,1,0:T(8,128)(2,1)} %param.3, bf16[]{:T(256)} %constant.0.clone.1), dimensions={0}, to_apply=%region_0.0 | reduce | flops 131072 | bytes 786434 | tf_op jit(solution)/shard_map/reduce_min | solution.py:278
  1.2 3.6 %collective-permute-start = (bf16[64,16,128]{2,1,0:T(8,128)(2,1)S(1)}, bf16[64,16,128]{2,1,0:T(8,128)(2,1)S(1)}, u32[]{:S(2)}, u32[]{:S(2)}) collective-permute-start(bf16[64,16,128]{2,1,0:T(8,128)(2,1)S(1)} %reduce_min.9.mine_ref), channel_id=1, source_target_pairs={{0,128},{128,0},{1,129},{129,1},{2,130},{130,2},{3,131},{131,3},{4... | collective-permute-start | bytes 786440 | tf_op jit(solution)/shard_map/ppermute | solution.py:279
  4.8 0.0 copy-done
  4.8 1.0 %copy-done.1 = s32[64,16,128]{2,1,0:T(8,128)S(1)} copy-done((s32[64,16,128]{2,1,0:T(8,128)S(1)}, s32[64,16,128]{2,1,0:T(8,128)}, u32[]{:S(2)}) %copy-start.1) | copy-done | bytes 524312
  5.9 0.3 shard_map.37
  6.1 3.7 %collective-permute-done.other_ref = bf16[64,16,128]{2,1,0:T(8,128)(2,1)S(1)} collective-permute-done((bf16[64,16,128]{2,1,0:T(8,128)(2,1)S(1)}, bf16[64,16,128]{2,1,0:T(8,128)(2,1)S(1)}, u32[]{:S(2)}, u32[]{:S(2)}) %collective-permute-start) | collective-permute-done | bytes 262176 | tf_op jit(solution)/shard_map/ppermute | solution.py:279
  9.8 2.7 %shard_map.38 = s16[32,2,16,128]{3,2,1,0:T(8,128)(2,1)S(1)} custom-call(bf16[64,16,128]{2,1,0:T(8,128)(2,1)S(1)} %reduce_min.9.mine_ref, bf16[64,16,128]{2,1,0:T(8,128)(2,1)S(1)} %collective-permute-done.other_ref, f32[2,64,16,128]{3,2,1,0:T(8,128)S(1)} %get-tuple-element.18.raise_ref), custom_call_target="tpu_custom_call" | custom-call | flops 4000000 | bytes 1048576 | tf_op jit(solution)/shard_map/pallas_call | solution.py:268
  12.6 21.6 %all_to_all.5.in_ref = s16[32,2,16,128]{3,2,1,0:T(8,128)(2,1)S(1)} all-to-all(s16[32,2,16,128]{3,2,1,0:T(8,128)(2,1)S(1)} %shard_map.38), channel_id=1, replica_groups=mesh['robot'=2,'xy'=32,'yz'=4] {'xy'}, dimensions={0} | all-to-all | bytes 524288 | tf_op jit(solution)/shard_map/all_to_all | solution.py:299
  34.2 2.0 %shard_map.39 = (f32[128,128]{1,0:T(8,128)S(1)}, s16[128,128]{1,0:T(8,128)(2,1)S(1)}, s16[128,128]{1,0:T(8,128)(2,1)S(1)}, s16[128,128]{1,0:T(8,128)(2,1)S(1)}) custom-call(s16[32,2,16,128]{3,2,1,0:T(8,128)(2,1)S(1)} %all_to_all.5.in_ref, f32[1024,128]{1,0:T(8,128)S(1)} %get-tuple-element.16.table_ref, f32[2,2,32,8,128]{4,3,2,1,0:T(8,128)S(1)} %get-tuple-element.17.spans_ref), custom_call_target="tpu_custom_call" | custom-call | flops 4000000 | bytes 1048576 | tf_op jit(solution)/shard_map/pallas_call | solution.py:268
  36.2 4.6 %collective-permute-start.1 = (s16[128,128]{1,0:T(8,128)(2,1)S(1)}, s16[128,128]{1,0:T(8,128)(2,1)S(1)}, u32[]{:S(2)}, u32[]{:S(2)}) collective-permute-start(s16[128,128]{1,0:T(8,128)(2,1)S(1)} %get-tuple-element.20), channel_id=1, source_target_pairs={{0,1},{1,0},{2,3},{3,2},{4,5},{5,4},{6,7},{7,6},{8,9},{9,8},{10,11... | collective-permute-start | bytes 98312 | tf_op jit(solution)/shard_map/ppermute | solution.py:312
  40.8 0.2 collective-permute-start.2
  40.9 1.6 %collective-permute-start.3 = (s16[128,128]{1,0:T(8,128)(2,1)S(1)}, s16[128,128]{1,0:T(8,128)(2,1)S(1)}, u32[]{:S(2)}, u32[]{:S(2)}) collective-permute-start(s16[128,128]{1,0:T(8,128)(2,1)S(1)} %get-tuple-element.22), channel_id=1, source_target_pairs={{0,3},{1,2},{2,1},{3,0},{4,7},{5,6},{6,5},{7,4},{8,11},{9,10},{10,... | collective-permute-start | bytes 98312 | tf_op jit(solution)/shard_map/ppermute | solution.py:312
  42.5 1.7 %shard_map.41 = (f32[128,128]{1,0:T(8,128)S(1)}, s16[128,128]{1,0:T(8,128)(2,1)S(1)}, s16[128,128]{1,0:T(8,128)(2,1)S(1)}, s16[128,128]{1,0:T(8,128)(2,1)S(1)}) custom-call(s16[32,2,16,128]{3,2,1,0:T(8,128)(2,1)S(1)} %all_to_all.5.in_ref, f32[1024,128]{1,0:T(8,128)S(1)} %get-tuple-element.16.table_ref, f32[2,2,32,8,128]{4,3,2,1,0:T(8,128)S(1)} %get-tuple-element.17.spans_ref), custom_call_target="tpu_custom_call" | custom-call | flops 4000000 | bytes 1048576 | tf_op jit(solution)/shard_map/pallas_call | solution.py:268
  44.2 0.3 collective-permute-start.4
  44.5 0.0 collective-permute-start.5
  44.5 0.0 collective-permute-done.1.rest_0_
  44.5 1.9 %collective-permute-start.6 = (s16[128,128]{1,0:T(8,128)(2,1)S(1)}, s16[128,128]{1,0:T(8,128)(2,1)S(1)}, u32[]{:S(2)}, u32[]{:S(2)}) collective-permute-start(s16[128,128]{1,0:T(8,128)(2,1)S(1)} %get-tuple-element.26), channel_id=1, source_target_pairs={{0,3},{1,2},{2,1},{3,0},{4,7},{5,6},{6,5},{7,4},{8,11},{9,10},{10,... | collective-permute-start | bytes 98312 | tf_op jit(solution)/shard_map/ppermute | solution.py:312
  46.4 0.0 collective-permute-done.2.rest_1_
  46.4 0.0 collective-permute-done.3.rest_2_
  46.4 2.8 %shard_map.40.outside_ref = f32[512,128]{1,0:T(8,128)S(1)} custom-call(f32[1024,128]{1,0:T(8,128)S(1)} %get-tuple-element.16.table_ref, f32[2,2,32,8,128]{4,3,2,1,0:T(8,128)S(1)} %get-tuple-element.17.spans_ref, f32[128,128]{1,0:T(8,128)S(1)} %get-tuple-element.19.own_ref, s16[128,128]{1,0:T(8,128)(2,1)S(1)} %collective-permute-done.1.rest_0_, ...), custom_call_target="tpu_custom_call" | custom-call | flops 4000000 | bytes 1048576 | tf_op jit(solution)/shard_map/pallas_call | solution.py:268
  49.2 0.0 collective-permute-done.4.rest_0_
  49.2 0.0 collective-permute-done.5.rest_1_
  49.2 0.0 collective-permute-done.6.rest_2_
  49.2 1.8 %shard_map.42 = f32[128,512]{1,0:T(8,128)} custom-call(f32[1024,128]{1,0:T(8,128)S(1)} %get-tuple-element.16.table_ref, f32[512,128]{1,0:T(8,128)S(1)} %shard_map.40.outside_ref, f32[128,128]{1,0:T(8,128)S(1)} %get-tuple-element.23.own_ref, s16[128,128]{1,0:T(8,128)(2,1)S(1)} %collective-permute-done.4.rest_0_, ...), custom_call_target="tpu_custom_call" | custom-call | flops 4000000 | bytes 1048576 | tf_op jit(solution)/shard_map/pallas_call | solution.py:268
  (2 shorter events, 0.0 us)
Async XLA Ops:
  0.0 4.8 %copy-start = (s32[64,16,128]{2,1,0:T(8,128)S(1)}, s32[64,16,128]{2,1,0:T(8,128)}, u32[]{:S(2)}) copy-start(s32[64,16,128]{2,1,0:T(8,128)} %occupied_ref.1) | copy-start | bytes 1572868
  1.2 8.6 %collective-permute-start = (bf16[64,16,128]{2,1,0:T(8,128)(2,1)S(1)}, bf16[64,16,128]{2,1,0:T(8,128)(2,1)S(1)}, u32[]{:S(2)}, u32[]{:S(2)}) collective-permute-start(bf16[64,16,128]{2,1,0:T(8,128)(2,1)S(1)} %reduce_min.9.mine_ref), channel_id=1, source_target_pairs={{0,128},{128,0},{1,129},{129,1},{2,130},{130,2},{3,131},{131,3},{4... | collective-permute-start | bytes 786440 | tf_op jit(solution)/shard_map/ppermute | solution.py:279
  4.8 1.0 %copy-start.1 = (s32[64,16,128]{2,1,0:T(8,128)S(1)}, s32[64,16,128]{2,1,0:T(8,128)}, u32[]{:S(2)}) copy-start(s32[64,16,128]{2,1,0:T(8,128)} %unknown_ref.1) | copy-start | bytes 1572868
  36.2 8.3 %collective-permute-start.1 = (s16[128,128]{1,0:T(8,128)(2,1)S(1)}, s16[128,128]{1,0:T(8,128)(2,1)S(1)}, u32[]{:S(2)}, u32[]{:S(2)}) collective-permute-start(s16[128,128]{1,0:T(8,128)(2,1)S(1)} %get-tuple-element.20), channel_id=1, source_target_pairs={{0,1},{1,0},{2,3},{3,2},{4,5},{5,4},{6,7},{7,6},{8,9},{9,8},{10,11... | collective-permute-start | bytes 98312 | tf_op jit(solution)/shard_map/ppermute | solution.py:312
  40.8 5.6 %collective-permute-start.2 = (s16[128,128]{1,0:T(8,128)(2,1)S(1)}, s16[128,128]{1,0:T(8,128)(2,1)S(1)}, u32[]{:S(2)}, u32[]{:S(2)}) collective-permute-start(s16[128,128]{1,0:T(8,128)(2,1)S(1)} %get-tuple-element.21), channel_id=1, source_target_pairs={{0,2},{1,3},{2,0},{3,1},{4,6},{5,7},{6,4},{7,5},{8,10},{9,11},{10,... | collective-permute-start | bytes 98312 | tf_op jit(solution)/shard_map/ppermute | solution.py:312
  40.9 5.5 %collective-permute-start.3 = (s16[128,128]{1,0:T(8,128)(2,1)S(1)}, s16[128,128]{1,0:T(8,128)(2,1)S(1)}, u32[]{:S(2)}, u32[]{:S(2)}) collective-permute-start(s16[128,128]{1,0:T(8,128)(2,1)S(1)} %get-tuple-element.22), channel_id=1, source_target_pairs={{0,3},{1,2},{2,1},{3,0},{4,7},{5,6},{6,5},{7,4},{8,11},{9,10},{10,... | collective-permute-start | bytes 98312 | tf_op jit(solution)/shard_map/ppermute | solution.py:312
  44.2 5.0 %collective-permute-start.4 = (s16[128,128]{1,0:T(8,128)(2,1)S(1)}, s16[128,128]{1,0:T(8,128)(2,1)S(1)}, u32[]{:S(2)}, u32[]{:S(2)}) collective-permute-start(s16[128,128]{1,0:T(8,128)(2,1)S(1)} %get-tuple-element.24), channel_id=1, source_target_pairs={{0,1},{1,0},{2,3},{3,2},{4,5},{5,4},{6,7},{7,6},{8,9},{9,8},{10,11... | collective-permute-start | bytes 98312 | tf_op jit(solution)/shard_map/ppermute | solution.py:312
  44.5 4.7 %collective-permute-start.5 = (s16[128,128]{1,0:T(8,128)(2,1)S(1)}, s16[128,128]{1,0:T(8,128)(2,1)S(1)}, u32[]{:S(2)}, u32[]{:S(2)}) collective-permute-start(s16[128,128]{1,0:T(8,128)(2,1)S(1)} %get-tuple-element.25), channel_id=1, source_target_pairs={{0,2},{1,3},{2,0},{3,1},{4,6},{5,7},{6,4},{7,5},{8,10},{9,11},{10,... | collective-permute-start | bytes 98312 | tf_op jit(solution)/shard_map/ppermute | solution.py:312
  44.5 4.7 %collective-permute-start.6 = (s16[128,128]{1,0:T(8,128)(2,1)S(1)}, s16[128,128]{1,0:T(8,128)(2,1)S(1)}, u32[]{:S(2)}, u32[]{:S(2)}) collective-permute-start(s16[128,128]{1,0:T(8,128)(2,1)S(1)} %get-tuple-element.26), channel_id=1, source_target_pairs={{0,3},{1,2},{2,1},{3,0},{4,7},{5,6},{6,5},{7,4},{8,11},{9,10},{10,... | collective-permute-start | bytes 98312 | tf_op jit(solution)/shard_map/ppermute | solution.py:312
